TPU v7x, 256 devices: a whole 4x4x8 slice. The times are simulated.
256 devices in a mesh: word: 16 (over z_lo, x, core), ctx: 16 (over y, z_hi).
Axes of the slice: x: 4, y: 4, z: 8 (z_hi: 4, z_lo: 2; z = z_hi * 2 + z_lo), core: 2. Of those that a mesh axis runs over, the one named last changes fastest.
Arguments:
- counts: int32 [24576, 24576], P('word', 'ctx'), may hold values from 0 to 1800, as said below
- word_vecs: float32 [24576, 300], P(('word', 'ctx')), may hold values from -0.35 to 0.35
- word_bias: float32 [24576], P(('word', 'ctx')), may hold values from 0.5 to 3
- word_accum: float32 [24576, 300], P(('word', 'ctx')), may hold values from 1.6276042e-06 to 8.138021e-05
- word_bias_accum: float32 [24576], P(('word', 'ctx')), may hold values from 1 to 30
- ctx_vecs: float32 [24576, 300], P(('ctx', 'word')), may hold values from -0.35 to 0.35
- ctx_bias: float32 [24576], P(('ctx', 'word')), may hold values from 0.5 to 3
- ctx_accum: float32 [24576, 300], P(('ctx', 'word')), may hold values from 1.6276042e-06 to 8.138021e-05
- ctx_bias_accum: float32 [24576], P(('ctx', 'word')), may hold values from 1 to 30
Outputs:
- new_word_vecs: float32 [24576, 300], P(('word', 'ctx'))
- new_word_bias: float32 [24576], P(('word', 'ctx'))
- new_word_accum: float32 [24576, 300], P(('word', 'ctx'))
- new_word_bias_accum: float32 [24576], P(('word', 'ctx'))
- new_ctx_vecs: float32 [24576, 300], P(('ctx', 'word'))
- new_ctx_bias: float32 [24576], P(('ctx', 'word'))
- new_ctx_accum: float32 [24576, 300], P(('ctx', 'word'))
- new_ctx_bias_accum: float32 [24576], P(('ctx', 'word'))
Inputs may be any that keep to these rules, and one draw needn't show every extreme that they name: counts are non-negative integers, and a count is zero exactly where the word and the context never co-occur.
All inputs are finite; a program needn't handle non-finite values.
Results may differ from a plain program's by a relative error of at most 0.0045.
Values may be sent and summed in bfloat16 or wider, within the bound.
No kernel may reach another device: no remote copies, remote signals or barrier semaphores. Data moves between devices by JAX's collectives and lax.ppermute only.
A program may use at most 64 MiB of HBM per device.

v0:
```python
import functools

import jax
import jax.numpy as jnp
from jax import lax
from jax.experimental import pallas as pl
from jax.experimental.pallas import tpu as pltpu
from jax.sharding import PartitionSpec as P


count_cap = 100.0
power_law = 0.75
step_rate = 0.2

ROWS = 96
BLOCK = 120
HALF = 64
D = 300
LO = 256
MIB = 1 << 20


def pack_rows(main, tail):
    lane = lax.broadcasted_iota(jnp.int32, (24, 128), 1)
    low = lane < 64
    t = [tail[24 * g : 24 * g + 24, :] for g in range(4)]
    left = jnp.where(low, t[0], pltpu.roll(t[1], 64, 1))
    right = jnp.where(low, t[2], pltpu.roll(t[3], 64, 1))
    return jnp.concatenate([main, jnp.concatenate([left, right], axis=1)], axis=0)


def unpack_tail(packed):
    left, right = packed[ROWS:BLOCK, :128], packed[ROWS:BLOCK, 128:]
    return jnp.concatenate([left, pltpu.roll(left, 64, 1), right, pltpu.roll(right, 64, 1)], axis=0)


def to_column(row):
    eye = lax.broadcasted_iota(jnp.int32, (ROWS, ROWS), 0) == lax.broadcasted_iota(jnp.int32, (ROWS, ROWS), 1)
    return jnp.sum(jnp.where(eye, jnp.broadcast_to(row, (ROWS, ROWS)), 0.0), axis=1, keepdims=True)


def to_row(column):
    eye = lax.broadcasted_iota(jnp.int32, (ROWS, ROWS), 0) == lax.broadcasted_iota(jnp.int32, (ROWS, ROWS), 1)
    return jnp.sum(jnp.where(eye, jnp.broadcast_to(column, (ROWS, ROWS)), 0.0), axis=0, keepdims=True)


def pack_one(bias_lane, vec_ref, bias_ref, out_ref, tail_ref):
    tail_ref[...] = jnp.zeros_like(tail_ref)
    tail_ref[:, : D - LO] = vec_ref[:, LO:]
    lane = lax.broadcasted_iota(jnp.int32, (ROWS, 128), 1)
    tail = jnp.where(lane == bias_lane, jnp.broadcast_to(to_column(bias_ref[...]), (ROWS, 128)), tail_ref[...])
    out_ref[...] = pack_rows(vec_ref[:, :LO], tail).astype(jnp.bfloat16)


def pack_kernel(wv, wb, cv, cb, word_out, ctx_out, row_index, column_index, tail_ref):
    p, q = lax.axis_index("ctx"), lax.axis_index("word")
    y, z = lax.div(p, 4), lax.rem(p, 4)
    zl, x, c = lax.div(q, 8), lax.rem(lax.div(q, 2), 4), lax.rem(q, 2)
    for k in range(4):
        for j in range(4):
            row_index[4 * k + j] = lax.rem(y + k, 4) * 4 + lax.rem(z + j, 4)
    for i, (d, b, a) in enumerate((d, b, a) for d in (0, 1) for b in (0, 1, 3, 2) for a in (0, 1)):
        column_index[i] = lax.rem(zl + a, 2) * 8 + lax.rem(x + b, 4) * 2 + lax.rem(c + d, 2)
    pack_one(D - LO, wv, wb, word_out, tail_ref)
    pack_one(D - LO + 1, cv, cb, ctx_out, tail_ref)


def pack(word_vecs, word_bias, ctx_vecs, ctx_bias):
    return pl.pallas_call(
        pack_kernel,
        out_specs=[pl.BlockSpec(memory_space=pltpu.VMEM)] * 2 + [pl.BlockSpec(memory_space=pltpu.SMEM)] * 2,
        out_shape=[jax.ShapeDtypeStruct((BLOCK, LO), jnp.bfloat16)] * 2 + [jax.ShapeDtypeStruct((16,), jnp.int32)] * 2,
        scratch_shapes=[pltpu.VMEM((ROWS, 128), jnp.float32)],
        compiler_params=pltpu.CompilerParams(vmem_limit_bytes=4 * MIB),
        cost_estimate=pl.CostEstimate(flops=100000, bytes_accessed=400000, transcendentals=0),
        name="pack",
    )(*(pltpu.with_memory_space_constraint(v, pltpu.HBM) for v in (word_vecs, word_bias.reshape(1, ROWS), ctx_vecs, ctx_bias.reshape(1, ROWS))))


def weight_kernel(index_ref, counts_ref, weight_ref, log_ref):
    counts = counts_ref[...]
    values = counts.astype(jnp.float32)
    log_count = jnp.log(jnp.maximum(values, 1.0))
    power = jnp.exp(jnp.minimum(power_law * (log_count - jnp.log(jnp.float32(count_cap))), 0.0))
    weight_ref[...] = jnp.where(counts > 0, power, 0.0)
    log_ref[...] = log_count


def weights(k, index, counts):
    rows, columns = 4 * ROWS, counts.shape[1]
    spec = pl.BlockSpec((ROWS, columns), lambda j, index: (j, 0))
    return pl.pallas_call(
        weight_kernel,
        grid_spec=pltpu.PrefetchScalarGridSpec(
            num_scalar_prefetch=1,
            grid=(4,),
            in_specs=[pl.BlockSpec((ROWS, columns), lambda j, index: (index[4 * k + j], 0))],
            out_specs=[spec, spec],
        ),
        out_shape=[pltpu.VMEM((rows, columns), jnp.float32)] * 2,
        compiler_params=pltpu.CompilerParams(vmem_limit_bytes=6 * MIB),
        cost_estimate=pl.CostEstimate(
            flops=20 * rows * columns, bytes_accessed=12 * rows * columns, transcendentals=2 * rows * columns
        ),
    )(index, pltpu.with_memory_space_constraint(counts, pltpu.HBM))


def rows_of(index_ref, i):
    return pl.ds(pl.multiple_of(index_ref[i] * ROWS, ROWS), ROWS)


def word_chunk(blocks, weight, log_count, ctx_full, ctx_t, words, words_t, scaled_ref):
    lane = lax.broadcasted_iota(jnp.int32, (ROWS, 128), 1)
    bc = D - LO + 1
    for j in range(4):
        packed = blocks[j].astype(jnp.float32)
        tail = unpack_tail(packed)
        tail = jnp.where(lane < bc, tail, jnp.where(lane == bc, 1.0, 0.0))
        words[ROWS * j : ROWS * j + ROWS, :LO] = packed[:ROWS].astype(jnp.bfloat16)
        words[ROWS * j : ROWS * j + ROWS, LO:] = tail.astype(jnp.bfloat16)
    word_rows = words[...]
    words_t[...] = word_rows.T
    inner = jnp.dot(word_rows, ctx_t[...], preferred_element_type=jnp.float32)
    scaled_ref[...] = (weight[...] * (inner - log_count[...])).astype(jnp.bfloat16)
    term = jnp.dot(scaled_ref[...], ctx_full[...], preferred_element_type=jnp.float32)
    parts = [term[ROWS * j : ROWS * j + ROWS] for j in range(4)]
    return [pack_rows(part[:, :LO], part[:, LO:]) for part in parts]


def own_kernel(index_ref, w0, c0, c1, weight, log_count, grad, scaled, words_t, ctx_full, ctx_t, words):
    lane = lax.broadcasted_iota(jnp.int32, (ROWS, 128), 1)
    bw, bc = D - LO, D - LO + 1
    for i in range(16):
        packed = (c0 if i < 8 else c1)[i % 8].astype(jnp.float32)
        tail = unpack_tail(packed)
        tail = jnp.where(lane == bw, 1.0, jnp.where(lane <= bc, tail, 0.0))
        ctx_full[rows_of(index_ref, i), :LO] = packed[:ROWS].astype(jnp.bfloat16)
        ctx_full[rows_of(index_ref, i), LO:] = tail.astype(jnp.bfloat16)
    ctx_t[...] = ctx_full[...].T
    blocks = [w0[j] for j in range(4)]
    for j, packed in enumerate(word_chunk(blocks, weight, log_count, ctx_full, ctx_t, words, words_t, scaled)):
        grad[j] = packed


def near_kernel(w1, w3, k1, l1, k3, l3, ctx_full, ctx_t, g1, g3, scaled1, scaled3, words_t1, words_t3, words):
    for w, weight, log_count, grad, scaled, words_t in (
        (w1, k1, l1, g1, scaled1, words_t1), (w3, k3, l3, g3, scaled3, words_t3)
    ):
        blocks = [w[j] for j in range(4)]
        for j, packed in enumerate(word_chunk(blocks, weight, log_count, ctx_full, ctx_t, words, words_t, scaled)):
            grad[j] = packed.astype(jnp.bfloat16)


def far_kernel(w2a, w2b, weight, log_count, ctx_full, ctx_t, ga, gb, scaled, words_t, words):
    blocks = [(w2a, w2b)[j // 2][j % 2] for j in range(4)]
    for j, packed in enumerate(word_chunk(blocks, weight, log_count, ctx_full, ctx_t, words, words_t, scaled)):
        (ga, gb)[j // 2][j % 2] = packed.astype(jnp.bfloat16)


def ctx_kernel(index_ref, s0, s1, s2, s3, t0, t1, t2, t3, h_own, h_other, ctx_grad, back):
    for k, (t, s) in enumerate(((t0, s0), (t1, s1), (t2, s2), (t3, s3))):
        term = jnp.dot(t[...], s[...], preferred_element_type=jnp.float32)
        ctx_grad[...] = term if k == 0 else ctx_grad[...] + term
    back[...] = ctx_grad[...].T
    for i in range(16):
        term = back[rows_of(index_ref, i), :]
        packed = pack_rows(term[:, :LO], term[:, LO:])
        if i < 8:
            h_own[i] = packed
        else:
            h_other[i - 8] = packed.astype(jnp.bfloat16)


def sum_kernel(g0, rm, rp, ya, yb, own, nxt, last, far_a, far_b):
    f32 = jnp.float32
    for j, out in ((0, own), (1, nxt), (3, last), (2, None)):
        far = ya[j] if j < 2 else yb[j - 2]
        total = g0[j] + rm[j].astype(f32) + rp[j].astype(f32) + far.astype(f32)
        if out is None:
            far_a[...] = total[:HALF].astype(jnp.bfloat16)
            far_b[...] = total[HALF:].astype(jnp.bfloat16)
        else:
            out[...] = total


CHUNK, COLUMNS = 4 * ROWS, 16 * ROWS
SMEM_SPEC = pl.BlockSpec(memory_space=pltpu.SMEM)
VMEM_SPEC = pl.BlockSpec(memory_space=pltpu.VMEM)


def blocks_shape(n, dtype):
    return jax.ShapeDtypeStruct((n, BLOCK, LO), dtype)


def low_shape(*dims):
    return jax.ShapeDtypeStruct(dims, jnp.bfloat16)


def call(kernel, scalars, operands, out_shape, scratch, flops, limit):
    return pl.pallas_call(
        kernel,
        in_specs=[SMEM_SPEC] * len(scalars) + [VMEM_SPEC] * len(operands),
        out_specs=[VMEM_SPEC] * len(out_shape),
        out_shape=out_shape,
        scratch_shapes=scratch,
        compiler_params=pltpu.CompilerParams(vmem_limit_bytes=limit * MIB),
        cost_estimate=pl.CostEstimate(flops=flops, bytes_accessed=4 * MIB, transcendentals=0),
    )(*scalars, *operands)


CHUNK_FLOPS = 4 * CHUNK * COLUMNS * 384
WORDS_SCRATCH = [pltpu.VMEM((CHUNK, 384), jnp.bfloat16)]


def update_kernel(bias_lane, scale, total_ref, add_a, add_b, vec_ref, bias_ref, acc_ref, bacc_ref, nv, nb, na, nba):
    packed = total_ref[...] + add_a[...].astype(jnp.float32)
    if add_b is not None:
        packed = packed + add_b[...].astype(jnp.float32)
    packed = packed * scale
    tail = unpack_tail(packed)
    for columns, grad in ((slice(0, LO), packed[:ROWS]), (slice(LO, D), tail[:, : D - LO])):
        accum = acc_ref[:, columns] + grad * grad
        na[:, columns] = accum
        nv[:, columns] = vec_ref[:, columns] - step_rate * grad / jnp.sqrt(accum)
    grad = to_row(tail[:, bias_lane : bias_lane + 1])
    accum = bacc_ref[...] + grad * grad
    nba[...] = accum
    nb[...] = bias_ref[...] - step_rate * grad / jnp.sqrt(accum)


def update(total, add_a, add_b, vecs, bias, accum, bias_accum, bias_lane, scale):
    row = lambda a: a.reshape(1, ROWS)
    if add_b is None:
        kernel = lambda t, a, *rest: update_kernel(bias_lane, scale, t, a, None, *rest)
        sums = (total, add_a)
    else:
        kernel = functools.partial(update_kernel, bias_lane, scale)
        sums = (total, add_a, add_b)
    f32 = jnp.float32
    nv, nb, na, nba = pl.pallas_call(
        kernel,
        out_shape=[
            jax.ShapeDtypeStruct((ROWS, D), f32),
            jax.ShapeDtypeStruct((1, ROWS), f32),
            jax.ShapeDtypeStruct((ROWS, D), f32),
            jax.ShapeDtypeStruct((1, ROWS), f32),
        ],
        compiler_params=pltpu.CompilerParams(vmem_limit_bytes=6 * MIB),
        cost_estimate=pl.CostEstimate(flops=400000, bytes_accessed=800000, transcendentals=30000),
    )(*sums, vecs, row(bias), accum, row(bias_accum))
    return nv, nb.reshape(ROWS), na, nba.reshape(ROWS)


def ctx_shift(value, dy, dz):
    perm = [(i, ((i // 4 + dy) % 4) * 4 + (i % 4 + dz) % 4) for i in range(16)]
    return lax.ppermute(value, "ctx", perm)


def word_shift(value, dl, dx, dc):
    perm = [(i, ((i // 8 + dl) % 2) * 8 + ((i // 2 % 4 + dx) % 4) * 2 + (i % 2 + dc) % 2) for i in range(16)]
    return lax.ppermute(value, "word", perm)


def per_device(
    counts,
    word_vecs,
    word_bias,
    word_accum,
    word_bias_accum,
    ctx_vecs,
    ctx_bias,
    ctx_accum,
    ctx_bias_accum,
):
    f32, low = jnp.float32, jnp.bfloat16
    far_ctx = lambda v, dy, dz: ctx_shift(v, dy, dz)
    far_word = lambda v, dl, dx, dc: word_shift(v, dl, dx, dc)

    word_block, ctx_block, row_index, index = pack(word_vecs, word_bias, ctx_vecs, ctx_bias)

    zm, zp = far_ctx(word_block, 0, 1), far_ctx(word_block, 0, -1)
    pair = jnp.stack([ctx_block, far_word(ctx_block, 1, 0, 0)])
    xm, xp = far_word(pair, 0, 1, 0), far_word(pair, 0, -1, 0)
    zoa, zob = far_ctx(zm[:HALF], 0, 1), far_ctx(zp[HALF:], 0, -1)
    xoa, xob = far_word(xm[:1], 0, 1, 0), far_word(xp[1:], 0, -1, 0)
    w0 = jnp.stack([word_block, zp, jnp.concatenate([zoa, zob]), zm])
    w3, w1 = far_ctx(w0, 1, 0), far_ctx(w0, -1, 0)
    c0 = jnp.concatenate([pair, xp, xm, xoa, xob])
    c1 = far_word(c0, 0, 0, 1)
    w2a, w2b = far_ctx(w3[:2], 1, 0), far_ctx(w1[2:], -1, 0)

    weighted = []
    for k in range(4):
        pair_k = weights(k, row_index, counts)
        weighted.append([pltpu.with_memory_space_constraint(v, pltpu.VMEM) for v in pair_k])
    (k0, l0), (k1, l1), (k2, l2), (k3, l3) = weighted

    scaled_shape, words_t_shape = low_shape(CHUNK, COLUMNS), low_shape(384, CHUNK)
    g0, s0, t0, ctx_full, ctx_t = call(
        own_kernel, (index,), (w0, c0, c1, k0, l0),
        [blocks_shape(4, f32), scaled_shape, words_t_shape, low_shape(COLUMNS, 384), low_shape(384, COLUMNS)],
        WORDS_SCRATCH, CHUNK_FLOPS, 16,
    )
    g1, g3, s1, s3, t1, t3 = call(
        near_kernel, (), (w1, w3, k1, l1, k3, l3, ctx_full, ctx_t),
        [blocks_shape(4, low)] * 2 + [scaled_shape] * 2 + [words_t_shape] * 2,
        WORDS_SCRATCH, 2 * CHUNK_FLOPS, 16,
    )
    g2a, g2b, s2, t2 = call(
        far_kernel, (), (w2a, w2b, k2, l2, ctx_full, ctx_t),
        [blocks_shape(2, low)] * 2 + [scaled_shape, words_t_shape],
        WORDS_SCRATCH, CHUNK_FLOPS, 16,
    )
    h_own, h_other = call(
        ctx_kernel, (index,), (s0, s1, s2, s3, t0, t1, t2, t3),
        [blocks_shape(8, f32), blocks_shape(8, low)],
        [pltpu.VMEM((384, COLUMNS), f32), pltpu.VMEM((COLUMNS, 384), f32)], 2 * CHUNK_FLOPS, 16,
    )

    rm, rp = far_ctx(g1, 1, 0), far_ctx(g3, -1, 0)
    ya, yb = far_ctx(g2a, 1, 0), far_ctx(g2b, -1, 0)
    ya2, yb2 = far_ctx(ya, 1, 0), far_ctx(yb, -1, 0)
    hc = far_word(h_other, 0, 0, 1)
    s = h_own + hc.astype(f32)
    xa, xb = far_word(s[6:7].astype(low), 0, 1, 0), far_word(s[7:8].astype(low), 0, -1, 0)
    send_xp = jnp.concatenate([s[2:3] + xa.astype(f32), s[3:4]]).astype(low)
    send_xm = jnp.concatenate([s[4:5], s[5:6] + xb.astype(f32)]).astype(low)
    rxm, rxp = far_word(send_xp, 0, 1, 0), far_word(send_xm, 0, -1, 0)
    z_own, z_next, z_last, far_a, far_b = call(
        sum_kernel, (), (g0, rm, rp, ya2, yb2),
        [jax.ShapeDtypeStruct((BLOCK, LO), f32)] * 3 + [low_shape(HALF, LO), low_shape(BLOCK - HALF, LO)],
        [], 4 * BLOCK * LO * 4, 8,
    )
    za, zb = far_ctx(far_a, 0, 1), far_ctx(far_b, 0, -1)
    t = s[:2] + rxm.astype(f32) + rxp.astype(f32)
    rl = far_word(t[1].astype(low), 1, 0, 0)
    send_zp = jnp.concatenate([z_next[:HALF] + za.astype(f32), z_next[HALF:]]).astype(low)
    send_zm = jnp.concatenate([z_last[:HALF], z_last[HALF:] + zb.astype(f32)]).astype(low)
    rzm, rzp = far_ctx(send_zp, 0, 1), far_ctx(send_zm, 0, -1)

    word_scale = 2.0 / (counts.shape[1] * lax.axis_size("ctx"))
    ctx_scale = 2.0 / (counts.shape[0] * lax.axis_size("word"))
    new_ctx_vecs, new_ctx_bias, new_ctx_accum, new_ctx_bias_accum = update(
        t[0], rl, None, ctx_vecs, ctx_bias, ctx_accum, ctx_bias_accum, D - LO + 1, ctx_scale
    )
    new_word_vecs, new_word_bias, new_word_accum, new_word_bias_accum = update(
        z_own, rzm, rzp, word_vecs, word_bias, word_accum, word_bias_accum, D - LO, word_scale
    )
    return (
        new_word_vecs,
        new_word_bias,
        new_word_accum,
        new_word_bias_accum,
        new_ctx_vecs,
        new_ctx_bias,
        new_ctx_accum,
        new_ctx_bias_accum,
    )


def solution(mesh):
    words, contexts = P(("word", "ctx")), P(("ctx", "word"))
    return jax.shard_map(
        per_device,
        mesh=mesh,
        in_specs=(P("word", "ctx"), words, words, words, words, contexts, contexts, contexts, contexts),
        out_specs=(words, words, words, words, contexts, contexts, contexts, contexts),
        check_vma=False,
    )
```

profile of v0, /device:TPU:6, one launch (start us, length us, event | category | flops | bytes accessed | tf_op | source)
XLA Modules:
  0.0 108.4 jit_solution(1480752423228384154)
XLA Ops:
  0.6 1.7 %pack.1 = (bf16[120,256]{1,0:T(8,128)(2,1)S(1)}, bf16[120,256]{1,0:T(8,128)(2,1)S(1)}, s32[16]{0:T(128)S(1)}, s32[16]{0:T(128)S(1)}) custom-call(f32[96,300]{1,0:T(8,128)} %vec_ref.1, f32[1,96]{1,0:T(1,128)} %bitcast.23, f32[96,300]{1,0:T(8,128)} %rest_0_.1, f32[1,96]{1,0:T(1,128)} %bitcast.25), custom_call_target="tpu_custom_call" | custom-call | flops 100000 | bytes 400000 | tf_op jit(solution)/shard_map/pack/pallas_call | solution.py:69
  2.4 3.3 %collective-permute-start.1 = (bf16[120,256]{1,0:T(8,128)(2,1)S(1)}, bf16[120,256]{1,0:T(8,128)(2,1)S(1)}, u32[]{:S(2)}, u32[]{:S(2)}) collective-permute-start(bf16[120,256]{1,0:T(8,128)(2,1)S(1)} %get-tuple-element.51), channel_id=1, source_target_pairs={{0,1},{1,2},{2,3},{3,0},{4,5},{5,6},{6,7},{7,4},{8,9},{9,10},{10,1... | collective-permute-start | bytes 184328 | tf_op jit(solution)/shard_map/ppermute | solution.py:256
  5.7 3.1 %collective-permute-start = (bf16[120,256]{1,0:T(8,128)(2,1)S(1)}, bf16[120,256]{1,0:T(8,128)(2,1)S(1)}, u32[]{:S(2)}, u32[]{:S(2)}) collective-permute-start(bf16[120,256]{1,0:T(8,128)(2,1)S(1)} %get-tuple-element.51), channel_id=1, source_target_pairs={{0,3},{1,0},{2,1},{3,2},{4,7},{5,4},{6,5},{7,6},{8,11},{9,8},{10,9... | collective-permute-start | bytes 184328 | tf_op jit(solution)/shard_map/ppermute | solution.py:256
  8.8 1.0 collective-permute-start.4
  9.9 4.3 %collective-permute-done.4 = bf16[120,256]{1,0:T(8,128)(2,1)S(1)} collective-permute-done((bf16[120,256]{1,0:T(8,128)(2,1)S(1)}, bf16[120,256]{1,0:T(8,128)(2,1)S(1)}, u32[]{:S(2)}, u32[]{:S(2)}) %collective-permute-start.4) | collective-permute-done | bytes 61472 | tf_op jit(solution)/shard_map/ppermute | solution.py:261
  14.2 0.9 collective-permute-start.5
  15.1 2.4 %collective-permute-start.6 = (bf16[2,120,256]{2,1,0:T(8,128)(2,1)S(1)}, bf16[2,120,256]{2,1,0:T(8,128)(2,1)S(1)}, u32[]{:S(2)}, u32[]{:S(2)}) collective-permute-start(bf16[2,120,256]{2,1,0:T(8,128)(2,1)S(1)} %pad_maximum_fusion.1), channel_id=1, source_target_pairs={{0,32},{16,48},{32,64},{48,80},{64,96},{80,112},{96,0},{112,16},{1... | collective-permute-start | bytes 368648 | tf_op jit(solution)/shard_map/ppermute | solution.py:261
  17.5 2.6 %collective-permute-start.3 = (bf16[56,256]{1,0:T(8,128)(2,1)S(1)}, bf16[56,256]{1,0:T(8,128)(2,1)S(1)}, u32[]{:S(2)}, u32[]{:S(2)}) collective-permute-start(bf16[56,256]{1,0:T(8,128)(2,1)S(1)} %slice.84), channel_id=1, source_target_pairs={{0,3},{1,0},{2,1},{3,2},{4,7},{5,4},{6,5},{7,6},{8,11},{9,8},{10,9... | collective-permute-start | bytes 86024 | tf_op jit(solution)/shard_map/ppermute | solution.py:256
  20.1 0.4 collective-permute-start.2
  20.5 3.1 %collective-permute-start.7 = (bf16[1,120,256]{2,1,0:T(8,128)(2,1)S(1)}, bf16[1,120,256]{2,1,0:T(8,128)(2,1)S(1)}, u32[]{:S(2)}, u32[]{:S(2)}) collective-permute-start(bf16[1,120,256]{2,1,0:T(8,128)(2,1)S(1)} %slice.85), channel_id=1, source_target_pairs={{0,32},{16,48},{32,64},{48,80},{64,96},{80,112},{96,0},{112,16},{1... | collective-permute-start | bytes 184328 | tf_op jit(solution)/shard_map/ppermute | solution.py:261
  23.8 1.7 %collective-permute-done.7 = bf16[1,120,256]{2,1,0:T(8,128)(2,1)S(1)} collective-permute-done((bf16[1,120,256]{2,1,0:T(8,128)(2,1)S(1)}, bf16[1,120,256]{2,1,0:T(8,128)(2,1)S(1)}, u32[]{:S(2)}, u32[]{:S(2)}) %collective-permute-start.7) | collective-permute-done | bytes 61472 | tf_op jit(solution)/shard_map/ppermute | solution.py:261
  25.5 3.6 %collective-permute-done.8 = bf16[1,120,256]{2,1,0:T(8,128)(2,1)S(1)} collective-permute-done((bf16[1,120,256]{2,1,0:T(8,128)(2,1)S(1)}, bf16[1,120,256]{2,1,0:T(8,128)(2,1)S(1)}, u32[]{:S(2)}, u32[]{:S(2)}) %collective-permute-start.8) | collective-permute-done | bytes 61472 | tf_op jit(solution)/shard_map/ppermute | solution.py:261
  29.2 1.7 %collective-permute-start.11 = (bf16[4,120,256]{2,1,0:T(8,128)(2,1)S(1)}, bf16[4,120,256]{2,1,0:T(8,128)(2,1)S(1)}, u32[]{:S(2)}, u32[]{:S(2)}) collective-permute-start(bf16[4,120,256]{2,1,0:T(8,128)(2,1)S(1)} %pad_maximum_fusion.w0), channel_id=1, source_target_pairs={{0,4},{1,5},{2,6},{3,7},{4,8},{5,9},{6,10},{7,11},{8,12},{9,13},{1... | collective-permute-start | bytes 737288 | tf_op jit(solution)/shard_map/ppermute | solution.py:256
  30.9 1.7 %collective-permute-start.10 = (bf16[4,120,256]{2,1,0:T(8,128)(2,1)S(1)}, bf16[4,120,256]{2,1,0:T(8,128)(2,1)S(1)}, u32[]{:S(2)}, u32[]{:S(2)}) collective-permute-start(bf16[4,120,256]{2,1,0:T(8,128)(2,1)S(1)} %pad_maximum_fusion.w0), channel_id=1, source_target_pairs={{0,12},{1,13},{2,14},{3,15},{4,0},{5,1},{6,2},{7,3},{8,4},{9,5},{1... | collective-permute-start | bytes 737288 | tf_op jit(solution)/shard_map/ppermute | solution.py:256
  32.6 6.4 %collective-permute-done.11.w3 = bf16[4,120,256]{2,1,0:T(8,128)(2,1)S(1)} collective-permute-done((bf16[4,120,256]{2,1,0:T(8,128)(2,1)S(1)}, bf16[4,120,256]{2,1,0:T(8,128)(2,1)S(1)}, u32[]{:S(2)}, u32[]{:S(2)}) %collective-permute-start.11) | collective-permute-done | bytes 245792 | tf_op jit(solution)/shard_map/ppermute | solution.py:256
  39.0 0.4 collective-permute-start.14
  39.4 3.2 %collective-permute-start.15 = (bf16[2,120,256]{2,1,0:T(8,128)(2,1)S(1)}, bf16[2,120,256]{2,1,0:T(8,128)(2,1)S(1)}, u32[]{:S(2)}, u32[]{:S(2)}) collective-permute-start(bf16[2,120,256]{2,1,0:T(8,128)(2,1)S(1)} %slice.88), channel_id=1, source_target_pairs={{0,12},{1,13},{2,14},{3,15},{4,0},{5,1},{6,2},{7,3},{8,4},{9,5},{1... | collective-permute-start | bytes 368648 | tf_op jit(solution)/shard_map/ppermute | solution.py:256
  42.5 3.5 %shard_map.152 = (f32[384,1536]{1,0:T(8,128)S(1)}, f32[384,1536]{1,0:T(8,128)S(1)}) custom-call(s32[16]{0:T(128)S(1)} %get-tuple-element.53.index_ref, s32[1536,1536]{1,0:T(8,128)} %counts_ref.7), custom_call_target="tpu_custom_call" | custom-call | flops 11796480 | bytes 7077888 | tf_op jit(solution)/shard_map/pallas_call | solution.py:92
  46.1 3.5 %shard_map.154 = (f32[384,1536]{1,0:T(8,128)S(1)}, f32[384,1536]{1,0:T(8,128)S(1)}) custom-call(s32[16]{0:T(128)S(1)} %get-tuple-element.53.index_ref, s32[1536,1536]{1,0:T(8,128)} %counts_ref.7), custom_call_target="tpu_custom_call" | custom-call | flops 11796480 | bytes 7077888 | tf_op jit(solution)/shard_map/pallas_call | solution.py:92
  49.6 3.5 %shard_map.155 = (f32[384,1536]{1,0:T(8,128)S(1)}, f32[384,1536]{1,0:T(8,128)S(1)}) custom-call(s32[16]{0:T(128)S(1)} %get-tuple-element.53.index_ref, s32[1536,1536]{1,0:T(8,128)} %counts_ref.7), custom_call_target="tpu_custom_call" | custom-call | flops 11796480 | bytes 7077888 | tf_op jit(solution)/shard_map/pallas_call | solution.py:92
  53.1 3.5 %shard_map.157 = (f32[384,1536]{1,0:T(8,128)S(1)}, f32[384,1536]{1,0:T(8,128)S(1)}) custom-call(s32[16]{0:T(128)S(1)} %get-tuple-element.53.index_ref, s32[1536,1536]{1,0:T(8,128)} %counts_ref.7), custom_call_target="tpu_custom_call" | custom-call | flops 11796480 | bytes 7077888 | tf_op jit(solution)/shard_map/pallas_call | solution.py:92
  56.7 2.3 %shard_map.153 = (f32[4,120,256]{2,1,0:T(8,128)S(1)}, bf16[384,1536]{1,0:T(8,128)(2,1)S(1)}, bf16[384,384]{1,0:T(8,128)(2,1)S(1)}, bf16[1536,384]{1,0:T(8,128)(2,1)S(1)}, bf16[384,1536]{1,0:T(8,128)(2,1)S(1)}) custom-call(s32[16]{0:T(128)S(1)} %get-tuple-element.50.index_ref, bf16[4,120,256]{2,1,0:T(8,128)(2,1)S(1)} %pad_maximum_fusion.w0, ...), custom_call_target="tpu_custom_call" | custom-call | flops 905969664 | bytes 4194304 | tf_op jit(solution)/shard_map/pallas_call | solution.py:200
  59.0 1.5 %shard_map.158 = (bf16[2,120,256]{2,1,0:T(8,128)(2,1)S(1)}, bf16[2,120,256]{2,1,0:T(8,128)(2,1)S(1)}, bf16[384,1536]{1,0:T(8,128)(2,1)S(1)}, bf16[384,384]{1,0:T(8,128)(2,1)S(1)}) custom-call(bf16[2,120,256]{2,1,0:T(8,128)(2,1)S(1)} %collective-permute-done.14.w2a, bf16[2,120,256]{2,1,0:T(8,128)(2,1)S(1)} %collective-permute-done.15.w2b, ...), custom_call_target="tpu_custom_call" | custom-call | flops 905969664 | bytes 4194304 | tf_op jit(solution)/shard_map/pallas_call | solution.py:200
  60.5 0.1 collective-permute-start.16
  60.6 3.2 %collective-permute-start.18 = (bf16[2,120,256]{2,1,0:T(8,128)(2,1)S(1)}, bf16[2,120,256]{2,1,0:T(8,128)(2,1)S(1)}, u32[]{:S(2)}, u32[]{:S(2)}) collective-permute-start(bf16[2,120,256]{2,1,0:T(8,128)(2,1)S(1)} %get-tuple-element.68), channel_id=1, source_target_pairs={{0,12},{1,13},{2,14},{3,15},{4,0},{5,1},{6,2},{7,3},{8,4},{9,5},{1... | collective-permute-start | bytes 368648 | tf_op jit(solution)/shard_map/ppermute | solution.py:256
  63.8 2.8 %shard_map.156 = (bf16[4,120,256]{2,1,0:T(8,128)(2,1)S(1)}, bf16[4,120,256]{2,1,0:T(8,128)(2,1)S(1)}, bf16[384,1536]{1,0:T(8,128)(2,1)S(1)}, bf16[384,1536]{1,0:...) custom-call(bf16[4,120,256]{2,1,0:T(8,128)(2,1)S(1)} %collective-permute-done.10.w1, ...), custom_call_target="tpu_custom_call" | custom-call | flops 1811939328 | bytes 4194304 | tf_op jit(solution)/shard_map/pallas_call | solution.py:200
  66.6 0.1 collective-permute-start.12
  66.7 3.2 %collective-permute-start.13 = (bf16[4,120,256]{2,1,0:T(8,128)(2,1)S(1)}, bf16[4,120,256]{2,1,0:T(8,128)(2,1)S(1)}, u32[]{:S(2)}, u32[]{:S(2)}) collective-permute-start(bf16[4,120,256]{2,1,0:T(8,128)(2,1)S(1)} %get-tuple-element.64), channel_id=1, source_target_pairs={{0,12},{1,13},{2,14},{3,15},{4,0},{5,1},{6,2},{7,3},{8,4},{9,5},{1... | collective-permute-start | bytes 737288 | tf_op jit(solution)/shard_map/ppermute | solution.py:256
  70.0 3.2 %collective-permute-start.19 = (bf16[2,120,256]{2,1,0:T(8,128)(2,1)S(1)}, bf16[2,120,256]{2,1,0:T(8,128)(2,1)S(1)}, u32[]{:S(2)}, u32[]{:S(2)}) collective-permute-start(bf16[2,120,256]{2,1,0:T(8,128)(2,1)S(1)} %collective-permute-done.18), channel_id=1, source_target_pairs={{0,12},{1,13},{2,14},{3,15},{4,0},{5,1},{6,2},{7,3},{8,4},{9,5},{1... | collective-permute-start | bytes 368648 | tf_op jit(solution)/shard_map/ppermute | solution.py:256
  73.2 3.5 %shard_map.161 = (f32[8,120,256]{2,1,0:T(8,128)S(1)}, bf16[8,120,256]{2,1,0:T(8,128)(2,1)S(1)}) custom-call(s32[16]{0:T(128)S(1)} %get-tuple-element.50.index_ref, bf16[384,1536]{1,0:T(8,128)(2,1)S(1)} %get-tuple-element.78.s0, bf16[384,1536]{1,0:T(8,128)(2,1)S(1)} %get-tuple-element.79.s1, bf16[384,1536]{1,0:T(8,128)(2,1)S(1)} %get-tuple-element.80.s2, ...), custom_call_target="tpu_custom_call" | custom-call | flops 1811939328 | bytes 4194304 | tf_op jit(solution)/shard_map/pallas_call | solution.py:200
  76.7 0.3 collective-permute-start.24
  77.1 0.1 shard_map.159
  77.2 2.6 %collective-permute-start.22 = (bf16[56,256]{1,0:T(8,128)(2,1)S(1)}, bf16[56,256]{1,0:T(8,128)(2,1)S(1)}, u32[]{:S(2)}, u32[]{:S(2)}) collective-permute-start(bf16[56,256]{1,0:T(8,128)(2,1)S(1)} %get-tuple-element.73), channel_id=1, source_target_pairs={{0,3},{1,0},{2,1},{3,2},{4,7},{5,4},{6,5},{7,6},{8,11},{9,8},{10,9... | collective-permute-start | bytes 86024 | tf_op jit(solution)/shard_map/ppermute | solution.py:256
  79.8 0.4 collective-permute-start.20
  80.2 1.8 %collective-permute-done.22 = bf16[56,256]{1,0:T(8,128)(2,1)S(1)} collective-permute-done((bf16[56,256]{1,0:T(8,128)(2,1)S(1)}, bf16[56,256]{1,0:T(8,128)(2,1)S(1)}, u32[]{:S(2)}, u32[]{:S(2)}) %collective-permute-start.22) | collective-permute-done | bytes 28704 | tf_op jit(solution)/shard_map/ppermute | solution.py:256
  82.1 4.0 %collective-permute-start.23 = (bf16[120,256]{1,0:T(8,128)(2,1)S(1)}, bf16[120,256]{1,0:T(8,128)(2,1)S(1)}, u32[]{:S(2)}, u32[]{:S(2)}) collective-permute-start(bf16[120,256]{1,0:T(8,128)(2,1)S(1)} %pad_maximum_fusion.5), channel_id=1, source_target_pairs={{0,3},{1,0},{2,1},{3,2},{4,7},{5,4},{6,5},{7,6},{8,11},{9,8},{10,9... | collective-permute-start | bytes 184328 | tf_op jit(solution)/shard_map/ppermute | solution.py:256
  86.2 0.1 fusion.4
  86.4 0.1 collective-permute-start.25
  86.5 2.0 %collective-permute-start.27 = (bf16[1,120,256]{2,1,0:T(8,128)(2,1)S(1)}, bf16[1,120,256]{2,1,0:T(8,128)(2,1)S(1)}, u32[]{:S(2)}, u32[]{:S(2)}) collective-permute-start(bf16[1,120,256]{2,1,0:T(8,128)(2,1)S(1)} %get-tuple-element.97), channel_id=1, source_target_pairs={{0,96},{16,112},{32,0},{48,16},{64,32},{80,48},{96,64},{112,80},{1... | collective-permute-start | bytes 184328 | tf_op jit(solution)/shard_map/ppermute | solution.py:261
  88.5 2.2 %collective-permute-done.25 = bf16[1,120,256]{2,1,0:T(8,128)(2,1)S(1)} collective-permute-done((bf16[1,120,256]{2,1,0:T(8,128)(2,1)S(1)}, bf16[1,120,256]{2,1,0:T(8,128)(2,1)S(1)}, u32[]{:S(2)}, u32[]{:S(2)}) %collective-permute-start.25) | collective-permute-done | bytes 61472 | tf_op jit(solution)/shard_map/ppermute | solution.py:261
  90.7 1.3 %collective-permute-done.27 = bf16[1,120,256]{2,1,0:T(8,128)(2,1)S(1)} collective-permute-done((bf16[1,120,256]{2,1,0:T(8,128)(2,1)S(1)}, bf16[1,120,256]{2,1,0:T(8,128)(2,1)S(1)}, u32[]{:S(2)}, u32[]{:S(2)}) %collective-permute-start.27) | collective-permute-done | bytes 61472 | tf_op jit(solution)/shard_map/ppermute | solution.py:261
  92.0 0.8 collective-permute-start.28
  92.8 2.6 %collective-permute-start.26 = (bf16[2,120,256]{2,1,0:T(8,128)(2,1)S(1)}, bf16[2,120,256]{2,1,0:T(8,128)(2,1)S(1)}, u32[]{:S(2)}, u32[]{:S(2)}) collective-permute-start(bf16[2,120,256]{2,1,0:T(8,128)(2,1)S(1)} %pad_maximum_fusion.2), channel_id=1, source_target_pairs={{0,32},{16,48},{32,64},{48,80},{64,96},{80,112},{96,0},{112,16},{1... | collective-permute-start | bytes 368648 | tf_op jit(solution)/shard_map/ppermute | solution.py:261
  95.4 6.8 %collective-permute-done.21.add_a = bf16[120,256]{1,0:T(8,128)(2,1)S(1)} collective-permute-done((bf16[120,256]{1,0:T(8,128)(2,1)S(1)}, bf16[120,256]{1,0:T(8,128)(2,1)S(1)}, u32[]{:S(2)}, u32[]{:S(2)}) %collective-permute-start.21) | collective-permute-done | bytes 61472 | tf_op jit(solution)/shard_map/ppermute | solution.py:256
  102.2 0.9 shard_map.160
  103.2 0.1 collective-permute-start.29
  103.3 4.2 %collective-permute-done.29.a = bf16[120,256]{1,0:T(8,128)(2,1)S(1)} collective-permute-done((bf16[120,256]{1,0:T(8,128)(2,1)S(1)}, bf16[120,256]{1,0:T(8,128)(2,1)S(1)}, u32[]{:S(2)}, u32[]{:S(2)}) %collective-permute-start.29) | collective-permute-done | bytes 61472 | tf_op jit(solution)/shard_map/ppermute | solution.py:261
  107.5 0.9 shard_map.162
  (69 shorter events, 0.5 us)
Async XLA Ops:
  2.4 17.7 %collective-permute-start.1 = (bf16[120,256]{1,0:T(8,128)(2,1)S(1)}, bf16[120,256]{1,0:T(8,128)(2,1)S(1)}, u32[]{:S(2)}, u32[]{:S(2)}) collective-permute-start(bf16[120,256]{1,0:T(8,128)(2,1)S(1)} %get-tuple-element.51), channel_id=1, source_target_pairs={{0,1},{1,2},{2,3},{3,0},{4,5},{5,6},{6,7},{7,4},{8,9},{9,10},{10,1... | collective-permute-start | bytes 184328 | tf_op jit(solution)/shard_map/ppermute | solution.py:256
  5.7 11.8 %collective-permute-start = (bf16[120,256]{1,0:T(8,128)(2,1)S(1)}, bf16[120,256]{1,0:T(8,128)(2,1)S(1)}, u32[]{:S(2)}, u32[]{:S(2)}) collective-permute-start(bf16[120,256]{1,0:T(8,128)(2,1)S(1)} %get-tuple-element.51), channel_id=1, source_target_pairs={{0,3},{1,0},{2,1},{3,2},{4,7},{5,4},{6,5},{7,6},{8,11},{9,8},{10,9... | collective-permute-start | bytes 184328 | tf_op jit(solution)/shard_map/ppermute | solution.py:256
  8.8 5.4 %collective-permute-start.4 = (bf16[120,256]{1,0:T(8,128)(2,1)S(1)}, bf16[120,256]{1,0:T(8,128)(2,1)S(1)}, u32[]{:S(2)}, u32[]{:S(2)}) collective-permute-start(bf16[120,256]{1,0:T(8,128)(2,1)S(1)} %get-tuple-element.52), channel_id=1, source_target_pairs={{0,128},{16,144},{32,160},{48,176},{64,192},{80,208},{96,224},{112... | collective-permute-start | bytes 184328 | tf_op jit(solution)/shard_map/ppermute | solution.py:261
  14.2 9.4 %collective-permute-start.5 = (bf16[2,120,256]{2,1,0:T(8,128)(2,1)S(1)}, bf16[2,120,256]{2,1,0:T(8,128)(2,1)S(1)}, u32[]{:S(2)}, u32[]{:S(2)}) collective-permute-start(bf16[2,120,256]{2,1,0:T(8,128)(2,1)S(1)} %pad_maximum_fusion.1), channel_id=1, source_target_pairs={{0,96},{16,112},{32,0},{48,16},{64,32},{80,48},{96,64},{112,80},{1... | collective-permute-start | bytes 368648 | tf_op jit(solution)/shard_map/ppermute | solution.py:261
  15.1 5.4 %collective-permute-start.6 = (bf16[2,120,256]{2,1,0:T(8,128)(2,1)S(1)}, bf16[2,120,256]{2,1,0:T(8,128)(2,1)S(1)}, u32[]{:S(2)}, u32[]{:S(2)}) collective-permute-start(bf16[2,120,256]{2,1,0:T(8,128)(2,1)S(1)} %pad_maximum_fusion.1), channel_id=1, source_target_pairs={{0,32},{16,48},{32,64},{48,80},{64,96},{80,112},{96,0},{112,16},{1... | collective-permute-start | bytes 368648 | tf_op jit(solution)/shard_map/ppermute | solution.py:261
  17.5 11.6 %collective-permute-start.3 = (bf16[56,256]{1,0:T(8,128)(2,1)S(1)}, bf16[56,256]{1,0:T(8,128)(2,1)S(1)}, u32[]{:S(2)}, u32[]{:S(2)}) collective-permute-start(bf16[56,256]{1,0:T(8,128)(2,1)S(1)} %slice.84), channel_id=1, source_target_pairs={{0,3},{1,0},{2,1},{3,2},{4,7},{5,4},{6,5},{7,6},{8,11},{9,8},{10,9... | collective-permute-start | bytes 86024 | tf_op jit(solution)/shard_map/ppermute | solution.py:256
  20.1 9.1 %collective-permute-start.2 = (bf16[64,256]{1,0:T(8,128)(2,1)S(1)}, bf16[64,256]{1,0:T(8,128)(2,1)S(1)}, u32[]{:S(2)}, u32[]{:S(2)}) collective-permute-start(bf16[64,256]{1,0:T(8,128)(2,1)S(1)} %slice.83), channel_id=1, source_target_pairs={{0,1},{1,2},{2,3},{3,0},{4,5},{5,6},{6,7},{7,4},{8,9},{9,10},{10,1... | collective-permute-start | bytes 98312 | tf_op jit(solution)/shard_map/ppermute | solution.py:256
  20.5 5.0 %collective-permute-start.7 = (bf16[1,120,256]{2,1,0:T(8,128)(2,1)S(1)}, bf16[1,120,256]{2,1,0:T(8,128)(2,1)S(1)}, u32[]{:S(2)}, u32[]{:S(2)}) collective-permute-start(bf16[1,120,256]{2,1,0:T(8,128)(2,1)S(1)} %slice.85), channel_id=1, source_target_pairs={{0,32},{16,48},{32,64},{48,80},{64,96},{80,112},{96,0},{112,16},{1... | collective-permute-start | bytes 184328 | tf_op jit(solution)/shard_map/ppermute | solution.py:261
  23.6 5.5 %collective-permute-start.8 = (bf16[1,120,256]{2,1,0:T(8,128)(2,1)S(1)}, bf16[1,120,256]{2,1,0:T(8,128)(2,1)S(1)}, u32[]{:S(2)}, u32[]{:S(2)}) collective-permute-start(bf16[1,120,256]{2,1,0:T(8,128)(2,1)S(1)} %slice.86), channel_id=1, source_target_pairs={{0,96},{16,112},{32,0},{48,16},{64,32},{80,48},{96,64},{112,80},{1... | collective-permute-start | bytes 184328 | tf_op jit(solution)/shard_map/ppermute | solution.py:261
  29.2 27.5 %collective-permute-start.9 = (bf16[8,120,256]{2,1,0:T(8,128)(2,1)S(1)}, bf16[8,120,256]{2,1,0:T(8,128)(2,1)S(1)}, u32[]{:S(2)}, u32[]{:S(2)}) collective-permute-start(bf16[8,120,256]{2,1,0:T(8,128)(2,1)S(1)} %constant_dynamic-update-slice_fusion.c0), channel_id=1, source_target_pairs={{0,16},{16,0},{32,48},{48,32},{64,80},{80,64},{96,112},{112,96},{1... | collective-permute-start | bytes 1474568 | tf_op jit(solution)/shard_map/ppermute | solution.py:261
  29.2 9.7 %collective-permute-start.11 = (bf16[4,120,256]{2,1,0:T(8,128)(2,1)S(1)}, bf16[4,120,256]{2,1,0:T(8,128)(2,1)S(1)}, u32[]{:S(2)}, u32[]{:S(2)}) collective-permute-start(bf16[4,120,256]{2,1,0:T(8,128)(2,1)S(1)} %pad_maximum_fusion.w0), channel_id=1, source_target_pairs={{0,4},{1,5},{2,6},{3,7},{4,8},{5,9},{6,10},{7,11},{8,12},{9,13},{1... | collective-permute-start | bytes 737288 | tf_op jit(solution)/shard_map/ppermute | solution.py:256
  30.9 8.4 %collective-permute-start.10 = (bf16[4,120,256]{2,1,0:T(8,128)(2,1)S(1)}, bf16[4,120,256]{2,1,0:T(8,128)(2,1)S(1)}, u32[]{:S(2)}, u32[]{:S(2)}) collective-permute-start(bf16[4,120,256]{2,1,0:T(8,128)(2,1)S(1)} %pad_maximum_fusion.w0), channel_id=1, source_target_pairs={{0,12},{1,13},{2,14},{3,15},{4,0},{5,1},{6,2},{7,3},{8,4},{9,5},{1... | collective-permute-start | bytes 737288 | tf_op jit(solution)/shard_map/ppermute | solution.py:256
  39.0 20.1 %collective-permute-start.14 = (bf16[2,120,256]{2,1,0:T(8,128)(2,1)S(1)}, bf16[2,120,256]{2,1,0:T(8,128)(2,1)S(1)}, u32[]{:S(2)}, u32[]{:S(2)}) collective-permute-start(bf16[2,120,256]{2,1,0:T(8,128)(2,1)S(1)} %slice.87), channel_id=1, source_target_pairs={{0,4},{1,5},{2,6},{3,7},{4,8},{5,9},{6,10},{7,11},{8,12},{9,13},{1... | collective-permute-start | bytes 368648 | tf_op jit(solution)/shard_map/ppermute | solution.py:256
  39.4 19.7 %collective-permute-start.15 = (bf16[2,120,256]{2,1,0:T(8,128)(2,1)S(1)}, bf16[2,120,256]{2,1,0:T(8,128)(2,1)S(1)}, u32[]{:S(2)}, u32[]{:S(2)}) collective-permute-start(bf16[2,120,256]{2,1,0:T(8,128)(2,1)S(1)} %slice.88), channel_id=1, source_target_pairs={{0,12},{1,13},{2,14},{3,15},{4,0},{5,1},{6,2},{7,3},{8,4},{9,5},{1... | collective-permute-start | bytes 368648 | tf_op jit(solution)/shard_map/ppermute | solution.py:256
  60.5 9.4 %collective-permute-start.16 = (bf16[2,120,256]{2,1,0:T(8,128)(2,1)S(1)}, bf16[2,120,256]{2,1,0:T(8,128)(2,1)S(1)}, u32[]{:S(2)}, u32[]{:S(2)}) collective-permute-start(bf16[2,120,256]{2,1,0:T(8,128)(2,1)S(1)} %get-tuple-element.67), channel_id=1, source_target_pairs={{0,4},{1,5},{2,6},{3,7},{4,8},{5,9},{6,10},{7,11},{8,12},{9,13},{1... | collective-permute-start | bytes 368648 | tf_op jit(solution)/shard_map/ppermute | solution.py:256
  60.6 9.3 %collective-permute-start.18 = (bf16[2,120,256]{2,1,0:T(8,128)(2,1)S(1)}, bf16[2,120,256]{2,1,0:T(8,128)(2,1)S(1)}, u32[]{:S(2)}, u32[]{:S(2)}) collective-permute-start(bf16[2,120,256]{2,1,0:T(8,128)(2,1)S(1)} %get-tuple-element.68), channel_id=1, source_target_pairs={{0,12},{1,13},{2,14},{3,15},{4,0},{5,1},{6,2},{7,3},{8,4},{9,5},{1... | collective-permute-start | bytes 368648 | tf_op jit(solution)/shard_map/ppermute | solution.py:256
  66.6 10.4 %collective-permute-start.12 = (bf16[4,120,256]{2,1,0:T(8,128)(2,1)S(1)}, bf16[4,120,256]{2,1,0:T(8,128)(2,1)S(1)}, u32[]{:S(2)}, u32[]{:S(2)}) collective-permute-start(bf16[4,120,256]{2,1,0:T(8,128)(2,1)S(1)} %get-tuple-element.63), channel_id=1, source_target_pairs={{0,4},{1,5},{2,6},{3,7},{4,8},{5,9},{6,10},{7,11},{8,12},{9,13},{1... | collective-permute-start | bytes 737288 | tf_op jit(solution)/shard_map/ppermute | solution.py:256
  66.7 10.3 %collective-permute-start.13 = (bf16[4,120,256]{2,1,0:T(8,128)(2,1)S(1)}, bf16[4,120,256]{2,1,0:T(8,128)(2,1)S(1)}, u32[]{:S(2)}, u32[]{:S(2)}) collective-permute-start(bf16[4,120,256]{2,1,0:T(8,128)(2,1)S(1)} %get-tuple-element.64), channel_id=1, source_target_pairs={{0,12},{1,13},{2,14},{3,15},{4,0},{5,1},{6,2},{7,3},{8,4},{9,5},{1... | collective-permute-start | bytes 737288 | tf_op jit(solution)/shard_map/ppermute | solution.py:256
  70.0 7.1 %collective-permute-start.17 = (bf16[2,120,256]{2,1,0:T(8,128)(2,1)S(1)}, bf16[2,120,256]{2,1,0:T(8,128)(2,1)S(1)}, u32[]{:S(2)}, u32[]{:S(2)}) collective-permute-start(bf16[2,120,256]{2,1,0:T(8,128)(2,1)S(1)} %collective-permute-done.16), channel_id=1, source_target_pairs={{0,4},{1,5},{2,6},{3,7},{4,8},{5,9},{6,10},{7,11},{8,12},{9,13},{1... | collective-permute-start | bytes 368648 | tf_op jit(solution)/shard_map/ppermute | solution.py:256
  70.0 7.1 %collective-permute-start.19 = (bf16[2,120,256]{2,1,0:T(8,128)(2,1)S(1)}, bf16[2,120,256]{2,1,0:T(8,128)(2,1)S(1)}, u32[]{:S(2)}, u32[]{:S(2)}) collective-permute-start(bf16[2,120,256]{2,1,0:T(8,128)(2,1)S(1)} %collective-permute-done.18), channel_id=1, source_target_pairs={{0,12},{1,13},{2,14},{3,15},{4,0},{5,1},{6,2},{7,3},{8,4},{9,5},{1... | collective-permute-start | bytes 368648 | tf_op jit(solution)/shard_map/ppermute | solution.py:256
  76.7 9.4 %collective-permute-start.24 = (bf16[8,120,256]{2,1,0:T(8,128)(2,1)S(1)}, bf16[8,120,256]{2,1,0:T(8,128)(2,1)S(1)}, u32[]{:S(2)}, u32[]{:S(2)}) collective-permute-start(bf16[8,120,256]{2,1,0:T(8,128)(2,1)S(1)} %get-tuple-element.87), channel_id=1, source_target_pairs={{0,16},{16,0},{32,48},{48,32},{64,80},{80,64},{96,112},{112,96},{1... | collective-permute-start | bytes 1474568 | tf_op jit(solution)/shard_map/ppermute | solution.py:261
  77.2 4.9 %collective-permute-start.22 = (bf16[56,256]{1,0:T(8,128)(2,1)S(1)}, bf16[56,256]{1,0:T(8,128)(2,1)S(1)}, u32[]{:S(2)}, u32[]{:S(2)}) collective-permute-start(bf16[56,256]{1,0:T(8,128)(2,1)S(1)} %get-tuple-element.73), channel_id=1, source_target_pairs={{0,3},{1,0},{2,1},{3,2},{4,7},{5,4},{6,5},{7,6},{8,11},{9,8},{10,9... | collective-permute-start | bytes 86024 | tf_op jit(solution)/shard_map/ppermute | solution.py:256
  79.8 8.6 %collective-permute-start.20 = (bf16[64,256]{1,0:T(8,128)(2,1)S(1)}, bf16[64,256]{1,0:T(8,128)(2,1)S(1)}, u32[]{:S(2)}, u32[]{:S(2)}) collective-permute-start(bf16[64,256]{1,0:T(8,128)(2,1)S(1)} %get-tuple-element.71), channel_id=1, source_target_pairs={{0,1},{1,2},{2,3},{3,0},{4,5},{5,6},{6,7},{7,4},{8,9},{9,10},{10,1... | collective-permute-start | bytes 98312 | tf_op jit(solution)/shard_map/ppermute | solution.py:256
  82.1 20.1 %copy-start = (f32[96,300]{1,0:T(8,128)S(1)}, f32[96,300]{1,0:T(8,128)}, u32[]{:S(2)}) copy-start(f32[96,300]{1,0:T(8,128)} %vec_ref.1) | copy-start | bytes 345604
  82.1 20.1 %copy-start.2 = (f32[96,300]{1,0:T(8,128)S(1)}, f32[96,300]{1,0:T(8,128)}, u32[]{:S(2)}) copy-start(f32[96,300]{1,0:T(8,128)} %acc_ref.1) | copy-start | bytes 345604
  82.1 20.1 %copy-start.4 = (f32[96]{0:T(128)S(1)}, f32[96]{0:T(128)}, u32[]{:S(2)}) copy-start(f32[96]{0:T(128)} %param.11) | copy-start | bytes 1156
  82.1 20.1 %copy-start.6 = (f32[96]{0:T(128)S(1)}, f32[96]{0:T(128)}, u32[]{:S(2)}) copy-start(f32[96]{0:T(128)} %param.13) | copy-start | bytes 1156
  82.1 13.3 %collective-permute-start.23 = (bf16[120,256]{1,0:T(8,128)(2,1)S(1)}, bf16[120,256]{1,0:T(8,128)(2,1)S(1)}, u32[]{:S(2)}, u32[]{:S(2)}) collective-permute-start(bf16[120,256]{1,0:T(8,128)(2,1)S(1)} %pad_maximum_fusion.5), channel_id=1, source_target_pairs={{0,3},{1,0},{2,1},{3,2},{4,7},{5,4},{6,5},{7,6},{8,11},{9,8},{10,9... | collective-permute-start | bytes 184328 | tf_op jit(solution)/shard_map/ppermute | solution.py:256
  86.3 21.2 %copy-start.1 = (f32[96,300]{1,0:T(8,128)S(1)}, f32[96,300]{1,0:T(8,128)}, u32[]{:S(2)}) copy-start(f32[96,300]{1,0:T(8,128)} %rest_0_.1) | copy-start | bytes 345604
  86.3 21.2 %copy-start.3 = (f32[96,300]{1,0:T(8,128)S(1)}, f32[96,300]{1,0:T(8,128)}, u32[]{:S(2)}) copy-start(f32[96,300]{1,0:T(8,128)} %rest_2_.1) | copy-start | bytes 345604
  86.3 21.2 %copy-start.5 = (f32[96]{0:T(128)S(1)}, f32[96]{0:T(128)}, u32[]{:S(2)}) copy-start(f32[96]{0:T(128)} %param.15) | copy-start | bytes 1156
  86.3 21.2 %copy-start.7 = (f32[96]{0:T(128)S(1)}, f32[96]{0:T(128)}, u32[]{:S(2)}) copy-start(f32[96]{0:T(128)} %param.17) | copy-start | bytes 1156
  86.4 4.3 %collective-permute-start.25 = (bf16[1,120,256]{2,1,0:T(8,128)(2,1)S(1)}, bf16[1,120,256]{2,1,0:T(8,128)(2,1)S(1)}, u32[]{:S(2)}, u32[]{:S(2)}) collective-permute-start(bf16[1,120,256]{2,1,0:T(8,128)(2,1)S(1)} %get-tuple-element.96), channel_id=1, source_target_pairs={{0,32},{16,48},{32,64},{48,80},{64,96},{80,112},{96,0},{112,16},{1... | collective-permute-start | bytes 184328 | tf_op jit(solution)/shard_map/ppermute | solution.py:261
  86.5 5.5 %collective-permute-start.27 = (bf16[1,120,256]{2,1,0:T(8,128)(2,1)S(1)}, bf16[1,120,256]{2,1,0:T(8,128)(2,1)S(1)}, u32[]{:S(2)}, u32[]{:S(2)}) collective-permute-start(bf16[1,120,256]{2,1,0:T(8,128)(2,1)S(1)} %get-tuple-element.97), channel_id=1, source_target_pairs={{0,96},{16,112},{32,0},{48,16},{64,32},{80,48},{96,64},{112,80},{1... | collective-permute-start | bytes 184328 | tf_op jit(solution)/shard_map/ppermute | solution.py:261
  92.0 11.1 %collective-permute-start.28 = (bf16[2,120,256]{2,1,0:T(8,128)(2,1)S(1)}, bf16[2,120,256]{2,1,0:T(8,128)(2,1)S(1)}, u32[]{:S(2)}, u32[]{:S(2)}) collective-permute-start(bf16[2,120,256]{2,1,0:T(8,128)(2,1)S(1)} %pad_maximum_fusion.3), channel_id=1, source_target_pairs={{0,96},{16,112},{32,0},{48,16},{64,32},{80,48},{96,64},{112,80},{1... | collective-permute-start | bytes 368648 | tf_op jit(solution)/shard_map/ppermute | solution.py:261
  92.8 10.3 %collective-permute-start.26 = (bf16[2,120,256]{2,1,0:T(8,128)(2,1)S(1)}, bf16[2,120,256]{2,1,0:T(8,128)(2,1)S(1)}, u32[]{:S(2)}, u32[]{:S(2)}) collective-permute-start(bf16[2,120,256]{2,1,0:T(8,128)(2,1)S(1)} %pad_maximum_fusion.2), channel_id=1, source_target_pairs={{0,32},{16,48},{32,64},{48,80},{64,96},{80,112},{96,0},{112,16},{1... | collective-permute-start | bytes 368648 | tf_op jit(solution)/shard_map/ppermute | solution.py:261
  95.4 6.8 %collective-permute-start.21 = (bf16[120,256]{1,0:T(8,128)(2,1)S(1)}, bf16[120,256]{1,0:T(8,128)(2,1)S(1)}, u32[]{:S(2)}, u32[]{:S(2)}) collective-permute-start(bf16[120,256]{1,0:T(8,128)(2,1)S(1)} %pad_maximum_fusion.4), channel_id=1, source_target_pairs={{0,1},{1,2},{2,3},{3,0},{4,5},{5,6},{6,7},{7,4},{8,9},{9,10},{10,1... | collective-permute-start | bytes 184328 | tf_op jit(solution)/shard_map/ppermute | solution.py:256
  103.2 4.3 %collective-permute-start.29 = (bf16[120,256]{1,0:T(8,128)(2,1)S(1)}, bf16[120,256]{1,0:T(8,128)(2,1)S(1)}, u32[]{:S(2)}, u32[]{:S(2)}) collective-permute-start(bf16[120,256]{1,0:T(8,128)(2,1)S(1)} %fusion.3), channel_id=1, source_target_pairs={{0,128},{16,144},{32,160},{48,176},{64,192},{80,208},{96,224},{112... | collective-permute-start | bytes 184328 | tf_op jit(solution)/shard_map/ppermute | solution.py:261
where the time goes:
time: 109 us; the launch traced here: 108 us
  starting transfers between devices  46.6 us (43%)
  waiting for transfers between devices  32.4 us (30%)
  Pallas kernels  27.8 us (26%)
    ppermute x18, starting transfers between devices, ctx_shift(): return lax.ppermute(value, 'ctx', perm)  33.1 us
    ppermute x12, waiting for transfers between devices, word_shift(): return lax.ppermute(value, 'word', perm)  17.4 us
    ppermute x18, waiting for transfers between devices, ctx_shift(): return lax.ppermute(value, 'ctx', perm)  15 us
    pallas_call x4, Pallas kernels, weights(): pl.pallas_call(weight_kernel, grid_spec=pltpu.PrefetchScalarGridSpec(num_...  14.1 us
    ppermute x12, starting transfers between devices, word_shift(): return lax.ppermute(value, 'word', perm)  13.5 us
    pallas_call x5, Pallas kernels, call(): pl.pallas_call(kernel, in_specs=[SMEM_SPEC] * len(scalars) + [VMEM_SPEC]...  10.2 us
  transfers between devices with their start and end apart: 30, of which 9 were waited for; matrix products, arithmetic and copies ran while one was open for 0% of the time, Pallas kernels for 22%

commit v1 on v0

--- a/solution.py
+++ b/solution.py
@@ -1,4 +1,5 @@
 import functools
+import math
 
 import jax
 import jax.numpy as jnp
@@ -14,7 +15,6 @@
 
 ROWS = 96
 BLOCK = 120
-HALF = 64
 D = 300
 LO = 256
 MIB = 1 << 20
@@ -52,15 +52,24 @@
     out_ref[...] = pack_rows(vec_ref[:, :LO], tail).astype(jnp.bfloat16)
 
 
-def pack_kernel(wv, wb, cv, cb, word_out, ctx_out, row_index, column_index, tail_ref):
+PIECES = (
+    (0, 0, 0), (0, 0, 1), (1, 0, 0), (1, 0, 1), (0, -1, 0), (0, -1, 1), (1, -1, 0), (1, -1, 1), (0, 2, 0), (0, 2, 1),
+    (1, 1, 0), (1, 1, 1), (0, 1, 0), (0, 1, 1), (1, 2, 0), (1, 2, 1),
+)
+RESULTS = tuple((d, b if d == 0 else -b, a) for d in (0, 1) for b in range(4) for a in (0, 1))
+
+
+def pack_kernel(wv, wb, cv, cb, word_out, ctx_out, row_index, piece_index, result_index, tail_ref):
     p, q = lax.axis_index("ctx"), lax.axis_index("word")
     y, z = lax.div(p, 4), lax.rem(p, 4)
     zl, x, c = lax.div(q, 8), lax.rem(lax.div(q, 2), 4), lax.rem(q, 2)
+    s = 1 - 2 * c
     for k in range(4):
         for j in range(4):
-            row_index[4 * k + j] = lax.rem(y + k, 4) * 4 + lax.rem(z + j, 4)
-    for i, (d, b, a) in enumerate((d, b, a) for d in (0, 1) for b in (0, 1, 3, 2) for a in (0, 1)):
-        column_index[i] = lax.rem(zl + a, 2) * 8 + lax.rem(x + b, 4) * 2 + lax.rem(c + d, 2)
+            row_index[4 * k + j] = lax.rem(y + k * s + 4, 4) * 4 + lax.rem(z + j * s + 4, 4)
+    for out, table in ((piece_index, PIECES), (result_index, RESULTS)):
+        for i, (d, b, a) in enumerate(table):
+            out[i] = lax.rem(zl + a, 2) * 8 + lax.rem(x + b * s + 4, 4) * 2 + lax.rem(c + d, 2)
     pack_one(D - LO, wv, wb, word_out, tail_ref)
     pack_one(D - LO + 1, cv, cb, ctx_out, tail_ref)
 
@@ -68,8 +77,8 @@
 def pack(word_vecs, word_bias, ctx_vecs, ctx_bias):
     return pl.pallas_call(
         pack_kernel,
-        out_specs=[pl.BlockSpec(memory_space=pltpu.VMEM)] * 2 + [pl.BlockSpec(memory_space=pltpu.SMEM)] * 2,
-        out_shape=[jax.ShapeDtypeStruct((BLOCK, LO), jnp.bfloat16)] * 2 + [jax.ShapeDtypeStruct((16,), jnp.int32)] * 2,
+        out_specs=[pl.BlockSpec(memory_space=pltpu.VMEM)] * 2 + [pl.BlockSpec(memory_space=pltpu.SMEM)] * 3,
+        out_shape=[jax.ShapeDtypeStruct((BLOCK, LO), jnp.bfloat16)] * 2 + [jax.ShapeDtypeStruct((16,), jnp.int32)] * 3,
         scratch_shapes=[pltpu.VMEM((ROWS, 128), jnp.float32)],
         compiler_params=pltpu.CompilerParams(vmem_limit_bytes=4 * MIB),
         cost_estimate=pl.CostEstimate(flops=100000, bytes_accessed=400000, transcendentals=0),
@@ -77,30 +86,44 @@
     )(*(pltpu.with_memory_space_constraint(v, pltpu.HBM) for v in (word_vecs, word_bias.reshape(1, ROWS), ctx_vecs, ctx_bias.reshape(1, ROWS))))
 
 
-def weight_kernel(index_ref, counts_ref, weight_ref, log_ref):
-    counts = counts_ref[...]
-    values = counts.astype(jnp.float32)
-    log_count = jnp.log(jnp.maximum(values, 1.0))
-    power = jnp.exp(jnp.minimum(power_law * (log_count - jnp.log(jnp.float32(count_cap))), 0.0))
-    weight_ref[...] = jnp.where(counts > 0, power, 0.0)
-    log_ref[...] = log_count
-
-
-def weights(k, index, counts):
-    rows, columns = 4 * ROWS, counts.shape[1]
-    spec = pl.BlockSpec((ROWS, columns), lambda j, index: (j, 0))
+def weight_kernel(chunks, index_ref, counts, *refs):
+    outs, (held, sems) = refs[:-2], refs[-2:]
+
+    def fetch(n):
+        start = pl.multiple_of(index_ref[4 * chunks[n // 4] + n % 4] * ROWS, ROWS)
+        return pltpu.make_async_copy(counts.at[pl.ds(start, ROWS)], held.at[n], sems.at[n])
+
+    copies = [fetch(n) for n in range(4 * len(chunks))]
+    for copy in copies:
+        copy.start()
+    for n, copy in enumerate(copies):
+        weight_ref, log_ref = outs[n // 4 * 2], outs[n // 4 * 2 + 1]
+        copy.wait()
+
+        def step(i, _):
+            rows = pl.ds(pl.multiple_of(i * 8, 8), 8)
+            count = held[n, rows, :]
+            log_count = jnp.log(jnp.maximum(count, 1).astype(jnp.float32))
+            power = jnp.exp(jnp.minimum(power_law * (log_count - math.log(count_cap)), 0.0))
+            to = pl.ds(pl.multiple_of(n % 4 * ROWS + i * 8, 8), 8)
+            weight_ref[to, :] = jnp.where(count > 0, power, 0.0)
+            log_ref[to, :] = log_count
+            return 0
+
+        lax.fori_loop(0, ROWS // 8, step, 0, unroll=3)
+
+
+def weights(chunks, index, counts):
+    columns, n = counts.shape[1], len(chunks)
     return pl.pallas_call(
-        weight_kernel,
-        grid_spec=pltpu.PrefetchScalarGridSpec(
-            num_scalar_prefetch=1,
-            grid=(4,),
-            in_specs=[pl.BlockSpec((ROWS, columns), lambda j, index: (index[4 * k + j], 0))],
-            out_specs=[spec, spec],
-        ),
-        out_shape=[pltpu.VMEM((rows, columns), jnp.float32)] * 2,
-        compiler_params=pltpu.CompilerParams(vmem_limit_bytes=6 * MIB),
+        functools.partial(weight_kernel, chunks),
+        in_specs=[pl.BlockSpec(memory_space=pltpu.SMEM), pl.BlockSpec(memory_space=pltpu.HBM)],
+        out_specs=[pl.BlockSpec(memory_space=pltpu.VMEM)] * (2 * n),
+        out_shape=[pltpu.VMEM((4 * ROWS, columns), jnp.float32)] * (2 * n),
+        scratch_shapes=[pltpu.VMEM((4 * n, ROWS, columns), jnp.int32), pltpu.SemaphoreType.DMA((4 * n,))],
+        compiler_params=pltpu.CompilerParams(vmem_limit_bytes=8 * MIB),
         cost_estimate=pl.CostEstimate(
-            flops=20 * rows * columns, bytes_accessed=12 * rows * columns, transcendentals=2 * rows * columns
+            flops=80 * n * ROWS * columns, bytes_accessed=48 * n * ROWS * columns, transcendentals=8 * n * ROWS * columns
         ),
     )(index, pltpu.with_memory_space_constraint(counts, pltpu.HBM))
 
@@ -131,7 +154,7 @@
     lane = lax.broadcasted_iota(jnp.int32, (ROWS, 128), 1)
     bw, bc = D - LO, D - LO + 1
     for i in range(16):
-        packed = (c0 if i < 8 else c1)[i % 8].astype(jnp.float32)
+        packed = (c0[i] if i < 10 else c1[i - 10]).astype(jnp.float32)
         tail = unpack_tail(packed)
         tail = jnp.where(lane == bw, 1.0, jnp.where(lane <= bc, tail, 0.0))
         ctx_full[rows_of(index_ref, i), :LO] = packed[:ROWS].astype(jnp.bfloat16)
@@ -151,10 +174,10 @@
             grad[j] = packed.astype(jnp.bfloat16)
 
 
-def far_kernel(w2a, w2b, weight, log_count, ctx_full, ctx_t, ga, gb, scaled, words_t, words):
-    blocks = [(w2a, w2b)[j // 2][j % 2] for j in range(4)]
+def far_kernel(w2, weight, log_count, ctx_full, ctx_t, grad, scaled, words_t, words):
+    blocks = [w2[j] for j in range(4)]
     for j, packed in enumerate(word_chunk(blocks, weight, log_count, ctx_full, ctx_t, words, words_t, scaled)):
-        (ga, gb)[j // 2][j % 2] = packed.astype(jnp.bfloat16)
+        grad[j] = packed.astype(jnp.bfloat16)
 
 
 def ctx_kernel(index_ref, s0, s1, s2, s3, t0, t1, t2, t3, h_own, h_other, ctx_grad, back):
@@ -171,16 +194,11 @@
             h_other[i - 8] = packed.astype(jnp.bfloat16)
 
 
-def sum_kernel(g0, rm, rp, ya, yb, own, nxt, last, far_a, far_b):
+def sum_kernel(g0, rn, f2, ya, own, nxt, far, back):
     f32 = jnp.float32
-    for j, out in ((0, own), (1, nxt), (3, last), (2, None)):
-        far = ya[j] if j < 2 else yb[j - 2]
-        total = g0[j] + rm[j].astype(f32) + rp[j].astype(f32) + far.astype(f32)
-        if out is None:
-            far_a[...] = total[:HALF].astype(jnp.bfloat16)
-            far_b[...] = total[HALF:].astype(jnp.bfloat16)
-        else:
-            out[...] = total
+    for j, out in enumerate((own, nxt, far, back)):
+        total = g0[j] + rn[j].astype(f32) + f2[j].astype(f32) + ya[j].astype(f32)
+        out[...] = total.astype(out.dtype)
 
 
 CHUNK, COLUMNS = 4 * ROWS, 16 * ROWS
@@ -213,7 +231,7 @@
 
 
 def update_kernel(bias_lane, scale, total_ref, add_a, add_b, vec_ref, bias_ref, acc_ref, bacc_ref, nv, nb, na, nba):
-    packed = total_ref[...] + add_a[...].astype(jnp.float32)
+    packed = total_ref[...] + (add_a[0] if len(add_a.shape) == 3 else add_a[...]).astype(jnp.float32)
     if add_b is not None:
         packed = packed + add_b[...].astype(jnp.float32)
     packed = packed * scale
@@ -251,14 +269,33 @@
     return nv, nb.reshape(ROWS), na, nba.reshape(ROWS)
 
 
-def ctx_shift(value, dy, dz):
-    perm = [(i, ((i // 4 + dy) % 4) * 4 + (i % 4 + dz) % 4) for i in range(16)]
-    return lax.ppermute(value, "ctx", perm)
-
-
-def word_shift(value, dl, dx, dc):
-    perm = [(i, ((i // 8 + dl) % 2) * 8 + ((i // 2 % 4 + dx) % 4) * 2 + (i % 2 + dc) % 2) for i in range(16)]
-    return lax.ppermute(value, "word", perm)
+def spread(index):
+    q, p = index // 16, index % 16
+    return q // 8, q // 2 % 4, q % 2, p // 4, p % 4
+
+
+def place(zl, x, c, y, z):
+    return (zl % 2 * 8 + x % 4 * 2 + c % 2) * 16 + y % 4 * 4 + z % 4
+
+
+def move(value, axis):
+    perm = []
+    for i in range(256):
+        zl, x, c, y, z = spread(i)
+        s = 1 - 2 * c
+        to = {
+            "core": (zl, x, c + 1, y, z),
+            "zl": (zl + 1, x, c, y, z),
+            "x": (zl, x + s, c, y, z),
+            "y": (zl, x, c, y + s, z),
+            "z": (zl, x, c, y, z + s),
+        }[axis]
+        perm.append((i, place(*to)))
+    return lax.ppermute(value, ("word", "ctx"), perm)
+
+
+def keep(arrays):
+    return [pltpu.with_memory_space_constraint(v, pltpu.VMEM) for v in arrays]
 
 
 def per_device(
@@ -273,70 +310,68 @@
     ctx_bias_accum,
 ):
     f32, low = jnp.float32, jnp.bfloat16
-    far_ctx = lambda v, dy, dz: ctx_shift(v, dy, dz)
-    far_word = lambda v, dl, dx, dc: word_shift(v, dl, dx, dc)
-
-    word_block, ctx_block, row_index, index = pack(word_vecs, word_bias, ctx_vecs, ctx_bias)
-
-    zm, zp = far_ctx(word_block, 0, 1), far_ctx(word_block, 0, -1)
-    pair = jnp.stack([ctx_block, far_word(ctx_block, 1, 0, 0)])
-    xm, xp = far_word(pair, 0, 1, 0), far_word(pair, 0, -1, 0)
-    zoa, zob = far_ctx(zm[:HALF], 0, 1), far_ctx(zp[HALF:], 0, -1)
-    xoa, xob = far_word(xm[:1], 0, 1, 0), far_word(xp[1:], 0, -1, 0)
-    w0 = jnp.stack([word_block, zp, jnp.concatenate([zoa, zob]), zm])
-    w3, w1 = far_ctx(w0, 1, 0), far_ctx(w0, -1, 0)
-    c0 = jnp.concatenate([pair, xp, xm, xoa, xob])
-    c1 = far_word(c0, 0, 0, 1)
-    w2a, w2b = far_ctx(w3[:2], 1, 0), far_ctx(w1[2:], -1, 0)
-
-    weighted = []
-    for k in range(4):
-        pair_k = weights(k, row_index, counts)
-        weighted.append([pltpu.with_memory_space_constraint(v, pltpu.VMEM) for v in pair_k])
-    (k0, l0), (k1, l1), (k2, l2), (k3, l3) = weighted
-
+    go = lambda value, axis: move(value, axis)
+
+    word_block, ctx_block, row_index, piece_index, result_index = pack(word_vecs, word_bias, ctx_vecs, ctx_bias)
+
+    both = jnp.stack([word_block, go(word_block, "core")])
+    pair = jnp.stack([ctx_block, go(ctx_block, "zl")])
+    zr1 = go(both, "z")
+    four = jnp.concatenate([pair, go(pair, "core")])
+    zr2 = go(zr1[:1], "z")
+    xr1 = go(four, "x")
+    e1 = go(jnp.concatenate([zr1[1:], zr1[:1], zr2]), "core")
+    wy = jnp.concatenate([both[:1], e1[:1], zr2, zr1[:1], both[1:], zr1[1:], e1[2:], e1[1:2]])
+    yr1 = go(wy, "y")
+    xr2 = go(xr1[:2], "x")
+    c0 = jnp.concatenate([four, xr1, xr2])
+    c1 = go(c0[4:], "core")
+    w2 = go(yr1[:4], "y")
+    w1 = go(yr1[4:], "core")
+
+    k0, l0, k1, l1 = keep(weights((0, 1), row_index, counts))
+    k3, l3, k2, l2 = keep(weights((3, 2), row_index, counts))
     scaled_shape, words_t_shape = low_shape(CHUNK, COLUMNS), low_shape(384, CHUNK)
     g0, s0, t0, ctx_full, ctx_t = call(
-        own_kernel, (index,), (w0, c0, c1, k0, l0),
+        own_kernel, (piece_index,), (wy, c0, c1, k0, l0),
         [blocks_shape(4, f32), scaled_shape, words_t_shape, low_shape(COLUMNS, 384), low_shape(384, COLUMNS)],
         WORDS_SCRATCH, CHUNK_FLOPS, 16,
     )
     g1, g3, s1, s3, t1, t3 = call(
-        near_kernel, (), (w1, w3, k1, l1, k3, l3, ctx_full, ctx_t),
+        near_kernel, (), (w1, yr1, k1, l1, k3, l3, ctx_full, ctx_t),
         [blocks_shape(4, low)] * 2 + [scaled_shape] * 2 + [words_t_shape] * 2,
         WORDS_SCRATCH, 2 * CHUNK_FLOPS, 16,
     )
-    g2a, g2b, s2, t2 = call(
-        far_kernel, (), (w2a, w2b, k2, l2, ctx_full, ctx_t),
-        [blocks_shape(2, low)] * 2 + [scaled_shape, words_t_shape],
+    g2, s2, t2 = call(
+        far_kernel, (), (w2, k2, l2, ctx_full, ctx_t),
+        [blocks_shape(4, low), scaled_shape, words_t_shape],
         WORDS_SCRATCH, CHUNK_FLOPS, 16,
     )
     h_own, h_other = call(
-        ctx_kernel, (index,), (s0, s1, s2, s3, t0, t1, t2, t3),
+        ctx_kernel, (result_index,), (s0, s1, s2, s3, t0, t1, t2, t3),
         [blocks_shape(8, f32), blocks_shape(8, low)],
         [pltpu.VMEM((384, COLUMNS), f32), pltpu.VMEM((COLUMNS, 384), f32)], 2 * CHUNK_FLOPS, 16,
     )
 
-    rm, rp = far_ctx(g1, 1, 0), far_ctx(g3, -1, 0)
-    ya, yb = far_ctx(g2a, 1, 0), far_ctx(g2b, -1, 0)
-    ya2, yb2 = far_ctx(ya, 1, 0), far_ctx(yb, -1, 0)
-    hc = far_word(h_other, 0, 0, 1)
+    f1 = go(g3, "core")
+    ya = go(g2, "y")
+    rn = go(jnp.concatenate([g1, f1]), "y")
+    hc = go(h_other, "core")
+    ya2 = go(ya, "y")
     s = h_own + hc.astype(f32)
-    xa, xb = far_word(s[6:7].astype(low), 0, 1, 0), far_word(s[7:8].astype(low), 0, -1, 0)
-    send_xp = jnp.concatenate([s[2:3] + xa.astype(f32), s[3:4]]).astype(low)
-    send_xm = jnp.concatenate([s[4:5], s[5:6] + xb.astype(f32)]).astype(low)
-    rxm, rxp = far_word(send_xp, 0, 1, 0), far_word(send_xm, 0, -1, 0)
-    z_own, z_next, z_last, far_a, far_b = call(
-        sum_kernel, (), (g0, rm, rp, ya2, yb2),
-        [jax.ShapeDtypeStruct((BLOCK, LO), f32)] * 3 + [low_shape(HALF, LO), low_shape(BLOCK - HALF, LO)],
-        [], 4 * BLOCK * LO * 4, 8,
-    )
-    za, zb = far_ctx(far_a, 0, 1), far_ctx(far_b, 0, -1)
-    t = s[:2] + rxm.astype(f32) + rxp.astype(f32)
-    rl = far_word(t[1].astype(low), 1, 0, 0)
-    send_zp = jnp.concatenate([z_next[:HALF] + za.astype(f32), z_next[HALF:]]).astype(low)
-    send_zm = jnp.concatenate([z_last[:HALF], z_last[HALF:] + zb.astype(f32)]).astype(low)
-    rzm, rzp = far_ctx(send_zp, 0, 1), far_ctx(send_zm, 0, -1)
+    xa, x3 = go(s[4:6].astype(low), "x"), go(s[6:8].astype(low), "core")
+    f2 = go(rn[4:], "core")
+    z_own, z_next, z_far, z_back = call(
+        sum_kernel, (), (g0, rn, f2, ya2),
+        [jax.ShapeDtypeStruct((BLOCK, LO), f32)] * 2 + [low_shape(BLOCK, LO)] * 2, [], 4 * BLOCK * LO * 4, 8,
+    )
+    za, f3 = go(z_far, "z"), go(z_back, "core")
+    xr = go(jnp.concatenate([(s[2:4] + xa.astype(f32)).astype(low), x3]), "x")
+    x4 = go(xr[2:], "core")
+    rz = go(jnp.stack([(z_next + za.astype(f32)).astype(low), f3]), "z")
+    t = s[:2] + xr[:2].astype(f32) + x4.astype(f32)
+    rl = go(t[1].astype(low), "zl")
+    f4 = go(rz[1], "core")
 
     word_scale = 2.0 / (counts.shape[1] * lax.axis_size("ctx"))
     ctx_scale = 2.0 / (counts.shape[0] * lax.axis_size("word"))
@@ -344,7 +379,7 @@
         t[0], rl, None, ctx_vecs, ctx_bias, ctx_accum, ctx_bias_accum, D - LO + 1, ctx_scale
     )
     new_word_vecs, new_word_bias, new_word_accum, new_word_bias_accum = update(
-        z_own, rzm, rzp, word_vecs, word_bias, word_accum, word_bias_accum, D - LO, word_scale
+        z_own, rz, f4, word_vecs, word_bias, word_accum, word_bias_accum, D - LO, word_scale
     )
     return (
         new_word_vecs,

time: 109 us -> 93.5 us (0.86)
  the two profiles are of different devices: /device:TPU:6 before, /device:TPU:1 now
where the time goes in v1:
time: 93.5 us; the launch traced here: 92.7 us
  starting transfers between devices  45.6 us (49%)
  waiting for transfers between devices  23.6 us (25%)
  Pallas kernels  21.9 us (23%)
  between operations  1.02 us (1%)
    ppermute x27, starting transfers between devices, move(): return lax.ppermute(value, ('word', 'ctx'), perm)  45.6 us
    ppermute x27, waiting for transfers between devices, move(): return lax.ppermute(value, ('word', 'ctx'), perm)  23.6 us
    pallas_call x5, Pallas kernels, call(): pl.pallas_call(kernel, in_specs=[SMEM_SPEC] * len(scalars) + [VMEM_SPEC]...  10.2 us
    pallas_call x2, Pallas kernels, weights(): pl.pallas_call(functools.partial(weight_kernel, chunks), in_specs=[pl.Blo...  8.13 us
  transfers between devices with their start and end apart: 27, of which 11 were waited for; matrix products, arithmetic and copies ran while one was open for 1% of the time, Pallas kernels for 14%

profile of v1, /device:TPU:1, one launch (start us, length us, event | category | flops | bytes accessed | tf_op | source)
XLA Modules:
  0.0 92.7 jit_solution(15710588052602248860)
XLA Ops:
  0.6 1.8 %pack.1 = (bf16[120,256]{1,0:T(8,128)(2,1)S(1)}, bf16[120,256]{1,0:T(8,128)(2,1)S(1)}, s32[16]{0:T(128)S(1)}, s32[16]{0:T(128)S(1)}, s32[16]{0:T(128)S(1)}) custom-call(f32[96,300]{1,0:T(8,128)} %vec_ref.1, f32[1,96]{1,0:T(1,128)} %bitcast.28, f32[96,300]{1,0:T(8,128)} %rest_0_.1, f32[1,96]{1,0:T(1,128)} %bitcast.30), custom_call_target="tpu_custom_call" | custom-call | flops 100000 | bytes 400000 | tf_op jit(solution)/shard_map/pack/pallas_call | solution.py:78
  2.4 3.3 %collective-permute-start = (bf16[120,256]{1,0:T(8,128)(2,1)S(1)}, bf16[120,256]{1,0:T(8,128)(2,1)S(1)}, u32[]{:S(2)}, u32[]{:S(2)}) collective-permute-start(bf16[120,256]{1,0:T(8,128)(2,1)S(1)} %get-tuple-element.50), channel_id=1, source_target_pairs={{0,16},{1,17},{2,18},{3,19},{4,20},{5,21},{6,22},{7,23},{8,24},{9,... | collective-permute-start | bytes 184328 | tf_op jit(solution)/shard_map/ppermute | solution.py:294
  5.7 0.9 collective-permute-done
  6.6 4.4 %collective-permute-start.1 = (bf16[2,120,256]{2,1,0:T(8,128)(2,1)S(1)}, bf16[2,120,256]{2,1,0:T(8,128)(2,1)S(1)}, u32[]{:S(2)}, u32[]{:S(2)}) collective-permute-start(bf16[2,120,256]{2,1,0:T(8,128)(2,1)S(1)} %pad_maximum_fusion.5), channel_id=1, source_target_pairs={{0,1},{1,2},{2,3},{3,0},{4,5},{5,6},{6,7},{7,4},{8,9},{9,10},{10,1... | collective-permute-start | bytes 368648 | tf_op jit(solution)/shard_map/ppermute | solution.py:294
  11.0 0.7 collective-permute-start.4
  11.7 2.4 %collective-permute-done.1 = bf16[2,120,256]{2,1,0:T(8,128)(2,1)S(1)} collective-permute-done((bf16[2,120,256]{2,1,0:T(8,128)(2,1)S(1)}, bf16[2,120,256]{2,1,0:T(8,128)(2,1)S(1)}, u32[]{:S(2)}, u32[]{:S(2)}) %collective-permute-start.1) | collective-permute-done | bytes 122912 | tf_op jit(solution)/shard_map/ppermute | solution.py:294
  14.2 4.1 %collective-permute-start.2 = (bf16[1,120,256]{2,1,0:T(8,128)(2,1)S(1)}, bf16[1,120,256]{2,1,0:T(8,128)(2,1)S(1)}, u32[]{:S(2)}, u32[]{:S(2)}) collective-permute-start(bf16[1,120,256]{2,1,0:T(8,128)(2,1)S(1)} %get-tuple-element.97), channel_id=1, source_target_pairs={{0,1},{1,2},{2,3},{3,0},{4,5},{5,6},{6,7},{7,4},{8,9},{9,10},{10,1... | collective-permute-start | bytes 184328 | tf_op jit(solution)/shard_map/ppermute | solution.py:294
  18.3 0.1 collective-permute-start.5
  18.4 1.3 %collective-permute-done.2 = bf16[1,120,256]{2,1,0:T(8,128)(2,1)S(1)} collective-permute-done((bf16[1,120,256]{2,1,0:T(8,128)(2,1)S(1)}, bf16[1,120,256]{2,1,0:T(8,128)(2,1)S(1)}, u32[]{:S(2)}, u32[]{:S(2)}) %collective-permute-start.2) | collective-permute-done | bytes 61472 | tf_op jit(solution)/shard_map/ppermute | solution.py:294
  19.7 1.4 %collective-permute-start.3 = (bf16[3,120,256]{2,1,0:T(8,128)(2,1)S(1)}, bf16[3,120,256]{2,1,0:T(8,128)(2,1)S(1)}, u32[]{:S(2)}, u32[]{:S(2)}) collective-permute-start(bf16[3,120,256]{2,1,0:T(8,128)(2,1)S(1)} %pad_maximum_fusion.4), channel_id=1, source_target_pairs={{0,16},{1,17},{2,18},{3,19},{4,20},{5,21},{6,22},{7,23},{8,24},{9,... | collective-permute-start | bytes 552968 | tf_op jit(solution)/shard_map/ppermute | solution.py:294
  21.2 2.6 %collective-permute-start.6 = (bf16[4,120,256]{2,1,0:T(8,128)(2,1)S(1)}, bf16[4,120,256]{2,1,0:T(8,128)(2,1)S(1)}, u32[]{:S(2)}, u32[]{:S(2)}) collective-permute-start(bf16[4,120,256]{2,1,0:T(8,128)(2,1)S(1)} %pad_maximum_fusion.2), channel_id=1, source_target_pairs={{0,32},{1,33},{2,34},{3,35},{4,36},{5,37},{6,38},{7,39},{8,40},{9,... | collective-permute-start | bytes 737288 | tf_op jit(solution)/shard_map/ppermute | solution.py:294
  23.8 2.8 %collective-permute-start.9 = (bf16[8,120,256]{2,1,0:T(8,128)(2,1)S(1)}, bf16[8,120,256]{2,1,0:T(8,128)(2,1)S(1)}, u32[]{:S(2)}, u32[]{:S(2)}) collective-permute-start(bf16[8,120,256]{2,1,0:T(8,128)(2,1)S(1)} %slice_dynamic-update-slice_fusion.w0), channel_id=1, source_target_pairs={{0,4},{1,5},{2,6},{3,7},{4,8},{5,9},{6,10},{7,11},{8,12},{9,13},{1... | collective-permute-start | bytes 1474568 | tf_op jit(solution)/shard_map/ppermute | solution.py:294
  26.7 4.1 %shard_map.152 = (f32[384,1536]{1,0:T(8,128)S(1)}, f32[384,1536]{1,0:T(8,128)S(1)}, f32[384,1536]{1,0:T(8,128)S(1)}, f32[384,1536]{1,0:T(8,128)S(1)}) custom-call(s32[16]{0:T(128)S(1)} %get-tuple-element.52.index_ref, s32[1536,1536]{1,0:T(8,128)} %counts.3), custom_call_target="tpu_custom_call" | custom-call | flops 23592960 | bytes 14155776 | tf_op jit(solution)/shard_map/pallas_call | solution.py:118
  30.7 4.1 %shard_map.154 = (f32[384,1536]{1,0:T(8,128)S(1)}, f32[384,1536]{1,0:T(8,128)S(1)}, f32[384,1536]{1,0:T(8,128)S(1)}, f32[384,1536]{1,0:T(8,128)S(1)}) custom-call(s32[16]{0:T(128)S(1)} %get-tuple-element.52.index_ref, s32[1536,1536]{1,0:T(8,128)} %counts.3), custom_call_target="tpu_custom_call" | custom-call | flops 23592960 | bytes 14155776 | tf_op jit(solution)/shard_map/pallas_call | solution.py:118
  34.8 1.0 %collective-permute-start.7 = (bf16[2,120,256]{2,1,0:T(8,128)(2,1)S(1)}, bf16[2,120,256]{2,1,0:T(8,128)(2,1)S(1)}, u32[]{:S(2)}, u32[]{:S(2)}) collective-permute-start(bf16[2,120,256]{2,1,0:T(8,128)(2,1)S(1)} %slice.85), channel_id=1, source_target_pairs={{0,32},{1,33},{2,34},{3,35},{4,36},{5,37},{6,38},{7,39},{8,40},{9,... | collective-permute-start | bytes 368648 | tf_op jit(solution)/shard_map/ppermute | solution.py:294
  35.8 2.8 %collective-permute-done.7 = bf16[2,120,256]{2,1,0:T(8,128)(2,1)S(1)} collective-permute-done((bf16[2,120,256]{2,1,0:T(8,128)(2,1)S(1)}, bf16[2,120,256]{2,1,0:T(8,128)(2,1)S(1)}, u32[]{:S(2)}, u32[]{:S(2)}) %collective-permute-start.7) | collective-permute-done | bytes 122912 | tf_op jit(solution)/shard_map/ppermute | solution.py:294
  38.7 0.3 collective-permute-start.8
  39.0 1.5 %collective-permute-start.14 = (bf16[4,120,256]{2,1,0:T(8,128)(2,1)S(1)}, bf16[4,120,256]{2,1,0:T(8,128)(2,1)S(1)}, u32[]{:S(2)}, u32[]{:S(2)}) collective-permute-start(bf16[4,120,256]{2,1,0:T(8,128)(2,1)S(1)} %get-tuple-element.94), channel_id=1, source_target_pairs={{0,4},{1,5},{2,6},{3,7},{4,8},{5,9},{6,10},{7,11},{8,12},{9,13},{1... | collective-permute-start | bytes 737288 | tf_op jit(solution)/shard_map/ppermute | solution.py:294
  40.5 0.5 collective-permute-start.10
  41.0 2.3 %shard_map.153 = (f32[4,120,256]{2,1,0:T(8,128)S(1)}, bf16[384,1536]{1,0:T(8,128)(2,1)S(1)}, bf16[384,384]{1,0:T(8,128)(2,1)S(1)}, bf16[1536,384]{1,0:T(8,128)(2,1)S(1)}, bf16[384,1536]{1,0:T(8,128)(2,1)S(1)}) custom-call(s32[16]{0:T(128)S(1)} %get-tuple-element.49.index_ref, bf16[8,120,256]{2,1,0:T(8,128)(2,1)S(1)} %slice_dynamic-update-slice_fusion.w0, ...), custom_call_target="tpu_custom_call" | custom-call | flops 905969664 | bytes 4194304 | tf_op jit(solution)/shard_map/pallas_call | solution.py:218
  43.4 1.1 %collective-permute-done.14.w2 = bf16[4,120,256]{2,1,0:T(8,128)(2,1)S(1)} collective-permute-done((bf16[4,120,256]{2,1,0:T(8,128)(2,1)S(1)}, bf16[4,120,256]{2,1,0:T(8,128)(2,1)S(1)}, u32[]{:S(2)}, u32[]{:S(2)}) %collective-permute-start.14) | collective-permute-done | bytes 245792 | tf_op jit(solution)/shard_map/ppermute | solution.py:294
  44.5 1.5 %shard_map.156 = (bf16[4,120,256]{2,1,0:T(8,128)(2,1)S(1)}, bf16[384,1536]{1,0:T(8,128)(2,1)S(1)}, bf16[384,384]{1,0:T(8,128)(2,1)S(1)}) custom-call(bf16[4,120,256]{2,1,0:T(8,128)(2,1)S(1)} %collective-permute-done.14.w2, f32[384,1536]{1,0:T(8,128)S(1)} %get-tuple-element.64.weight, f32[384,1536]{1,0:T(8,128)S(1)} %get-tuple-element.65.log_count, ...), custom_call_target="tpu_custom_call" | custom-call | flops 905969664 | bytes 4194304 | tf_op jit(solution)/shard_map/pallas_call | solution.py:218
  46.0 2.8 %shard_map.155 = (bf16[4,120,256]{2,1,0:T(8,128)(2,1)S(1)}, bf16[4,120,256]{2,1,0:T(8,128)(2,1)S(1)}, bf16[384,1536]{1,0:T(8,128)(2,1)S(1)}, bf16[384,1536]{1,0:...) custom-call(bf16[4,120,256]{2,1,0:T(8,128)(2,1)S(1)} %collective-permute-done.10.w1, ...), custom_call_target="tpu_custom_call" | custom-call | flops 1811939328 | bytes 4194304 | tf_op jit(solution)/shard_map/pallas_call | solution.py:218
  48.7 3.5 %shard_map.159 = (f32[8,120,256]{2,1,0:T(8,128)S(1)}, bf16[8,120,256]{2,1,0:T(8,128)(2,1)S(1)}) custom-call(s32[16]{0:T(128)S(1)} %get-tuple-element.75.index_ref, bf16[384,1536]{1,0:T(8,128)(2,1)S(1)} %get-tuple-element.76.s0, bf16[384,1536]{1,0:T(8,128)(2,1)S(1)} %get-tuple-element.77.s1, bf16[384,1536]{1,0:T(8,128)(2,1)S(1)} %get-tuple-element.78.s2, ...), custom_call_target="tpu_custom_call" | custom-call | flops 1811939328 | bytes 4194304 | tf_op jit(solution)/shard_map/pallas_call | solution.py:218
  52.3 2.4 %collective-permute-start.21 = (bf16[8,120,256]{2,1,0:T(8,128)(2,1)S(1)}, bf16[8,120,256]{2,1,0:T(8,128)(2,1)S(1)}, u32[]{:S(2)}, u32[]{:S(2)}) collective-permute-start(bf16[8,120,256]{2,1,0:T(8,128)(2,1)S(1)} %get-tuple-element.85), channel_id=1, source_target_pairs={{0,16},{1,17},{2,18},{3,19},{4,20},{5,21},{6,22},{7,23},{8,24},{9,... | collective-permute-start | bytes 1474568 | tf_op jit(solution)/shard_map/ppermute | solution.py:294
  54.7 0.1 collective-permute-start.11
  54.8 1.4 %collective-permute-done.21 = bf16[8,120,256]{2,1,0:T(8,128)(2,1)S(1)} collective-permute-done((bf16[8,120,256]{2,1,0:T(8,128)(2,1)S(1)}, bf16[8,120,256]{2,1,0:T(8,128)(2,1)S(1)}, u32[]{:S(2)}, u32[]{:S(2)}) %collective-permute-start.21) | collective-permute-done | bytes 491552 | tf_op jit(solution)/shard_map/ppermute | solution.py:294
  56.2 0.2 fusion.4
  56.4 2.2 %collective-permute-start.22 = (bf16[2,120,256]{2,1,0:T(8,128)(2,1)S(1)}, bf16[2,120,256]{2,1,0:T(8,128)(2,1)S(1)}, u32[]{:S(2)}, u32[]{:S(2)}) collective-permute-start(bf16[2,120,256]{2,1,0:T(8,128)(2,1)S(1)} %get-tuple-element.92), channel_id=1, source_target_pairs={{0,32},{1,33},{2,34},{3,35},{4,36},{5,37},{6,38},{7,39},{8,40},{9,... | collective-permute-start | bytes 368648 | tf_op jit(solution)/shard_map/ppermute | solution.py:294
  58.6 0.1 collective-permute-start.12
  58.7 0.3 collective-permute-start.15
  59.1 1.4 %collective-permute-done.22 = bf16[2,120,256]{2,1,0:T(8,128)(2,1)S(1)} collective-permute-done((bf16[2,120,256]{2,1,0:T(8,128)(2,1)S(1)}, bf16[2,120,256]{2,1,0:T(8,128)(2,1)S(1)}, u32[]{:S(2)}, u32[]{:S(2)}) %collective-permute-start.22) | collective-permute-done | bytes 122912 | tf_op jit(solution)/shard_map/ppermute | solution.py:294
  60.6 3.2 %collective-permute-start.24 = (bf16[4,120,256]{2,1,0:T(8,128)(2,1)S(1)}, bf16[4,120,256]{2,1,0:T(8,128)(2,1)S(1)}, u32[]{:S(2)}, u32[]{:S(2)}) collective-permute-start(bf16[4,120,256]{2,1,0:T(8,128)(2,1)S(1)} %pad_maximum_fusion.3), channel_id=1, source_target_pairs={{0,32},{1,33},{2,34},{3,35},{4,36},{5,37},{6,38},{7,39},{8,40},{9,... | collective-permute-start | bytes 737288 | tf_op jit(solution)/shard_map/ppermute | solution.py:294
  63.7 5.6 %collective-permute-done.15 = bf16[4,120,256]{2,1,0:T(8,128)(2,1)S(1)} collective-permute-done((bf16[4,120,256]{2,1,0:T(8,128)(2,1)S(1)}, bf16[4,120,256]{2,1,0:T(8,128)(2,1)S(1)}, u32[]{:S(2)}, u32[]{:S(2)}) %collective-permute-start.15) | collective-permute-done | bytes 245792 | tf_op jit(solution)/shard_map/ppermute | solution.py:294
  69.3 0.9 collective-permute-start.16
  70.3 0.3 collective-permute-start.13
  70.6 0.6 collective-permute-start.25
  71.2 3.5 %collective-permute-done.16.ya = bf16[4,120,256]{2,1,0:T(8,128)(2,1)S(1)} collective-permute-done((bf16[4,120,256]{2,1,0:T(8,128)(2,1)S(1)}, bf16[4,120,256]{2,1,0:T(8,128)(2,1)S(1)}, u32[]{:S(2)}, u32[]{:S(2)}) %collective-permute-start.16) | collective-permute-done | bytes 245792 | tf_op jit(solution)/shard_map/ppermute | solution.py:294
  74.7 0.1 shard_map.157
  74.8 2.8 %collective-permute-start.17 = (bf16[120,256]{1,0:T(8,128)(2,1)S(1)}, bf16[120,256]{1,0:T(8,128)(2,1)S(1)}, u32[]{:S(2)}, u32[]{:S(2)}) collective-permute-start(bf16[120,256]{1,0:T(8,128)(2,1)S(1)} %get-tuple-element.69), channel_id=1, source_target_pairs={{0,1},{1,2},{2,3},{3,0},{4,5},{5,6},{6,7},{7,4},{8,9},{9,10},{10,1... | collective-permute-start | bytes 184328 | tf_op jit(solution)/shard_map/ppermute | solution.py:294
  77.7 1.5 %collective-permute-start.18 = (bf16[120,256]{1,0:T(8,128)(2,1)S(1)}, bf16[120,256]{1,0:T(8,128)(2,1)S(1)}, u32[]{:S(2)}, u32[]{:S(2)}) collective-permute-start(bf16[120,256]{1,0:T(8,128)(2,1)S(1)} %get-tuple-element.70), channel_id=1, source_target_pairs={{0,16},{1,17},{2,18},{3,19},{4,20},{5,21},{6,22},{7,23},{8,24},{9,... | collective-permute-start | bytes 184328 | tf_op jit(solution)/shard_map/ppermute | solution.py:294
  79.2 0.9 collective-permute-done.18
  80.0 3.7 %collective-permute-start.19 = (bf16[2,120,256]{2,1,0:T(8,128)(2,1)S(1)}, bf16[2,120,256]{2,1,0:T(8,128)(2,1)S(1)}, u32[]{:S(2)}, u32[]{:S(2)}) collective-permute-start(bf16[2,120,256]{2,1,0:T(8,128)(2,1)S(1)} %pad_maximum_fusion.7), channel_id=1, source_target_pairs={{0,1},{1,2},{2,3},{3,0},{4,5},{5,6},{6,7},{7,4},{8,9},{9,10},{10,1... | collective-permute-start | bytes 368648 | tf_op jit(solution)/shard_map/ppermute | solution.py:294
  83.7 0.7 collective-permute-start.26
  84.4 2.3 %collective-permute-done.19.add_a = bf16[2,120,256]{2,1,0:T(8,128)(2,1)S(1)} collective-permute-done((bf16[2,120,256]{2,1,0:T(8,128)(2,1)S(1)}, bf16[2,120,256]{2,1,0:T(8,128)(2,1)S(1)}, u32[]{:S(2)}, u32[]{:S(2)}) %collective-permute-start.19) | collective-permute-done | bytes 122912 | tf_op jit(solution)/shard_map/ppermute | solution.py:294
  86.7 4.2 %collective-permute-start.20 = (bf16[120,256]{1,0:T(8,128)(2,1)S(1)}, bf16[120,256]{1,0:T(8,128)(2,1)S(1)}, u32[]{:S(2)}, u32[]{:S(2)}) collective-permute-start(bf16[120,256]{1,0:T(8,128)(2,1)S(1)} %slice_bitcast_fusion.1), channel_id=1, source_target_pairs={{0,16},{1,17},{2,18},{3,19},{4,20},{5,21},{6,22},{7,23},{8,24},{9,... | collective-permute-start | bytes 184328 | tf_op jit(solution)/shard_map/ppermute | solution.py:294
  90.9 0.9 shard_map.160
  91.8 0.9 shard_map.158
  (66 shorter events, 0.6 us)
Async XLA Ops:
  2.4 4.2 %collective-permute-start = (bf16[120,256]{1,0:T(8,128)(2,1)S(1)}, bf16[120,256]{1,0:T(8,128)(2,1)S(1)}, u32[]{:S(2)}, u32[]{:S(2)}) collective-permute-start(bf16[120,256]{1,0:T(8,128)(2,1)S(1)} %get-tuple-element.50), channel_id=1, source_target_pairs={{0,16},{1,17},{2,18},{3,19},{4,20},{5,21},{6,22},{7,23},{8,24},{9,... | collective-permute-start | bytes 184328 | tf_op jit(solution)/shard_map/ppermute | solution.py:294
  6.6 7.5 %collective-permute-start.1 = (bf16[2,120,256]{2,1,0:T(8,128)(2,1)S(1)}, bf16[2,120,256]{2,1,0:T(8,128)(2,1)S(1)}, u32[]{:S(2)}, u32[]{:S(2)}) collective-permute-start(bf16[2,120,256]{2,1,0:T(8,128)(2,1)S(1)} %pad_maximum_fusion.5), channel_id=1, source_target_pairs={{0,1},{1,2},{2,3},{3,0},{4,5},{5,6},{6,7},{7,4},{8,9},{9,10},{10,1... | collective-permute-start | bytes 368648 | tf_op jit(solution)/shard_map/ppermute | solution.py:294
  11.0 7.2 %collective-permute-start.4 = (bf16[120,256]{1,0:T(8,128)(2,1)S(1)}, bf16[120,256]{1,0:T(8,128)(2,1)S(1)}, u32[]{:S(2)}, u32[]{:S(2)}) collective-permute-start(bf16[120,256]{1,0:T(8,128)(2,1)S(1)} %get-tuple-element.51), channel_id=1, source_target_pairs={{0,128},{1,129},{2,130},{3,131},{4,132},{5,133},{6,134},{7,135},{8... | collective-permute-start | bytes 184328 | tf_op jit(solution)/shard_map/ppermute | solution.py:294
  14.2 5.5 %collective-permute-start.2 = (bf16[1,120,256]{2,1,0:T(8,128)(2,1)S(1)}, bf16[1,120,256]{2,1,0:T(8,128)(2,1)S(1)}, u32[]{:S(2)}, u32[]{:S(2)}) collective-permute-start(bf16[1,120,256]{2,1,0:T(8,128)(2,1)S(1)} %get-tuple-element.97), channel_id=1, source_target_pairs={{0,1},{1,2},{2,3},{3,0},{4,5},{5,6},{6,7},{7,4},{8,9},{9,10},{10,1... | collective-permute-start | bytes 184328 | tf_op jit(solution)/shard_map/ppermute | solution.py:294
  18.3 2.9 %collective-permute-start.5 = (bf16[2,120,256]{2,1,0:T(8,128)(2,1)S(1)}, bf16[2,120,256]{2,1,0:T(8,128)(2,1)S(1)}, u32[]{:S(2)}, u32[]{:S(2)}) collective-permute-start(bf16[2,120,256]{2,1,0:T(8,128)(2,1)S(1)} %pad_maximum_fusion.6), channel_id=1, source_target_pairs={{0,16},{1,17},{2,18},{3,19},{4,20},{5,21},{6,22},{7,23},{8,24},{9,... | collective-permute-start | bytes 368648 | tf_op jit(solution)/shard_map/ppermute | solution.py:294
  19.7 4.0 %collective-permute-start.3 = (bf16[3,120,256]{2,1,0:T(8,128)(2,1)S(1)}, bf16[3,120,256]{2,1,0:T(8,128)(2,1)S(1)}, u32[]{:S(2)}, u32[]{:S(2)}) collective-permute-start(bf16[3,120,256]{2,1,0:T(8,128)(2,1)S(1)} %pad_maximum_fusion.4), channel_id=1, source_target_pairs={{0,16},{1,17},{2,18},{3,19},{4,20},{5,21},{6,22},{7,23},{8,24},{9,... | collective-permute-start | bytes 552968 | tf_op jit(solution)/shard_map/ppermute | solution.py:294
  21.2 13.6 %collective-permute-start.6 = (bf16[4,120,256]{2,1,0:T(8,128)(2,1)S(1)}, bf16[4,120,256]{2,1,0:T(8,128)(2,1)S(1)}, u32[]{:S(2)}, u32[]{:S(2)}) collective-permute-start(bf16[4,120,256]{2,1,0:T(8,128)(2,1)S(1)} %pad_maximum_fusion.2), channel_id=1, source_target_pairs={{0,32},{1,33},{2,34},{3,35},{4,36},{5,37},{6,38},{7,39},{8,40},{9,... | collective-permute-start | bytes 737288 | tf_op jit(solution)/shard_map/ppermute | solution.py:294
  23.8 15.2 %collective-permute-start.9 = (bf16[8,120,256]{2,1,0:T(8,128)(2,1)S(1)}, bf16[8,120,256]{2,1,0:T(8,128)(2,1)S(1)}, u32[]{:S(2)}, u32[]{:S(2)}) collective-permute-start(bf16[8,120,256]{2,1,0:T(8,128)(2,1)S(1)} %slice_dynamic-update-slice_fusion.w0), channel_id=1, source_target_pairs={{0,4},{1,5},{2,6},{3,7},{4,8},{5,9},{6,10},{7,11},{8,12},{9,13},{1... | collective-permute-start | bytes 1474568 | tf_op jit(solution)/shard_map/ppermute | solution.py:294
  34.8 3.8 %collective-permute-start.7 = (bf16[2,120,256]{2,1,0:T(8,128)(2,1)S(1)}, bf16[2,120,256]{2,1,0:T(8,128)(2,1)S(1)}, u32[]{:S(2)}, u32[]{:S(2)}) collective-permute-start(bf16[2,120,256]{2,1,0:T(8,128)(2,1)S(1)} %slice.85), channel_id=1, source_target_pairs={{0,32},{1,33},{2,34},{3,35},{4,36},{5,37},{6,38},{7,39},{8,40},{9,... | collective-permute-start | bytes 368648 | tf_op jit(solution)/shard_map/ppermute | solution.py:294
  38.7 2.4 %collective-permute-start.8 = (bf16[6,120,256]{2,1,0:T(8,128)(2,1)S(1)}, bf16[6,120,256]{2,1,0:T(8,128)(2,1)S(1)}, u32[]{:S(2)}, u32[]{:S(2)}) collective-permute-start(bf16[6,120,256]{2,1,0:T(8,128)(2,1)S(1)} %pad_maximum_fusion.1), channel_id=1, source_target_pairs={{0,16},{1,17},{2,18},{3,19},{4,20},{5,21},{6,22},{7,23},{8,24},{9,... | collective-permute-start | bytes 1105928 | tf_op jit(solution)/shard_map/ppermute | solution.py:294
  39.0 5.4 %collective-permute-start.14 = (bf16[4,120,256]{2,1,0:T(8,128)(2,1)S(1)}, bf16[4,120,256]{2,1,0:T(8,128)(2,1)S(1)}, u32[]{:S(2)}, u32[]{:S(2)}) collective-permute-start(bf16[4,120,256]{2,1,0:T(8,128)(2,1)S(1)} %get-tuple-element.94), channel_id=1, source_target_pairs={{0,4},{1,5},{2,6},{3,7},{4,8},{5,9},{6,10},{7,11},{8,12},{9,13},{1... | collective-permute-start | bytes 737288 | tf_op jit(solution)/shard_map/ppermute | solution.py:294
  40.5 5.5 %collective-permute-start.10 = (bf16[4,120,256]{2,1,0:T(8,128)(2,1)S(1)}, bf16[4,120,256]{2,1,0:T(8,128)(2,1)S(1)}, u32[]{:S(2)}, u32[]{:S(2)}) collective-permute-start(bf16[4,120,256]{2,1,0:T(8,128)(2,1)S(1)} %get-tuple-element.95), channel_id=1, source_target_pairs={{0,16},{1,17},{2,18},{3,19},{4,20},{5,21},{6,22},{7,23},{8,24},{9,... | collective-permute-start | bytes 737288 | tf_op jit(solution)/shard_map/ppermute | solution.py:294
  52.3 3.9 %collective-permute-start.21 = (bf16[8,120,256]{2,1,0:T(8,128)(2,1)S(1)}, bf16[8,120,256]{2,1,0:T(8,128)(2,1)S(1)}, u32[]{:S(2)}, u32[]{:S(2)}) collective-permute-start(bf16[8,120,256]{2,1,0:T(8,128)(2,1)S(1)} %get-tuple-element.85), channel_id=1, source_target_pairs={{0,16},{1,17},{2,18},{3,19},{4,20},{5,21},{6,22},{7,23},{8,24},{9,... | collective-permute-start | bytes 1474568 | tf_op jit(solution)/shard_map/ppermute | solution.py:294
  54.7 3.9 %collective-permute-start.11 = (bf16[4,120,256]{2,1,0:T(8,128)(2,1)S(1)}, bf16[4,120,256]{2,1,0:T(8,128)(2,1)S(1)}, u32[]{:S(2)}, u32[]{:S(2)}) collective-permute-start(bf16[4,120,256]{2,1,0:T(8,128)(2,1)S(1)} %get-tuple-element.63), channel_id=1, source_target_pairs={{0,16},{1,17},{2,18},{3,19},{4,20},{5,21},{6,22},{7,23},{8,24},{9,... | collective-permute-start | bytes 737288 | tf_op jit(solution)/shard_map/ppermute | solution.py:294
  56.4 4.1 %collective-permute-start.22 = (bf16[2,120,256]{2,1,0:T(8,128)(2,1)S(1)}, bf16[2,120,256]{2,1,0:T(8,128)(2,1)S(1)}, u32[]{:S(2)}, u32[]{:S(2)}) collective-permute-start(bf16[2,120,256]{2,1,0:T(8,128)(2,1)S(1)} %get-tuple-element.92), channel_id=1, source_target_pairs={{0,32},{1,33},{2,34},{3,35},{4,36},{5,37},{6,38},{7,39},{8,40},{9,... | collective-permute-start | bytes 368648 | tf_op jit(solution)/shard_map/ppermute | solution.py:294
  58.6 11.6 %collective-permute-start.12 = (bf16[8,120,256]{2,1,0:T(8,128)(2,1)S(1)}, bf16[8,120,256]{2,1,0:T(8,128)(2,1)S(1)}, u32[]{:S(2)}, u32[]{:S(2)}) collective-permute-start(bf16[8,120,256]{2,1,0:T(8,128)(2,1)S(1)} %pad_maximum_fusion), channel_id=1, source_target_pairs={{0,4},{1,5},{2,6},{3,7},{4,8},{5,9},{6,10},{7,11},{8,12},{9,13},{1... | collective-permute-start | bytes 1474568 | tf_op jit(solution)/shard_map/ppermute | solution.py:294
  58.7 10.6 %collective-permute-start.15 = (bf16[4,120,256]{2,1,0:T(8,128)(2,1)S(1)}, bf16[4,120,256]{2,1,0:T(8,128)(2,1)S(1)}, u32[]{:S(2)}, u32[]{:S(2)}) collective-permute-start(bf16[4,120,256]{2,1,0:T(8,128)(2,1)S(1)} %get-tuple-element.66), channel_id=1, source_target_pairs={{0,4},{1,5},{2,6},{3,7},{4,8},{5,9},{6,10},{7,11},{8,12},{9,13},{1... | collective-permute-start | bytes 737288 | tf_op jit(solution)/shard_map/ppermute | solution.py:294
  59.1 1.5 %collective-permute-start.23 = (bf16[2,120,256]{2,1,0:T(8,128)(2,1)S(1)}, bf16[2,120,256]{2,1,0:T(8,128)(2,1)S(1)}, u32[]{:S(2)}, u32[]{:S(2)}) collective-permute-start(bf16[2,120,256]{2,1,0:T(8,128)(2,1)S(1)} %get-tuple-element.93), channel_id=1, source_target_pairs={{0,16},{1,17},{2,18},{3,19},{4,20},{5,21},{6,22},{7,23},{8,24},{9,... | collective-permute-start | bytes 368648 | tf_op jit(solution)/shard_map/ppermute | solution.py:294
  60.4 30.5 %copy-start = (f32[96,300]{1,0:T(8,128)S(1)}, f32[96,300]{1,0:T(8,128)}, u32[]{:S(2)}) copy-start(f32[96,300]{1,0:T(8,128)} %rest_0_.1) | copy-start | bytes 345604
  60.4 30.5 %copy-start.2 = (f32[96,300]{1,0:T(8,128)S(1)}, f32[96,300]{1,0:T(8,128)}, u32[]{:S(2)}) copy-start(f32[96,300]{1,0:T(8,128)} %rest_2_.1) | copy-start | bytes 345604
  60.5 30.5 %copy-start.5 = (f32[96]{0:T(128)S(1)}, f32[96]{0:T(128)}, u32[]{:S(2)}) copy-start(f32[96]{0:T(128)} %param.15) | copy-start | bytes 1156
  60.5 30.5 %copy-start.7 = (f32[96]{0:T(128)S(1)}, f32[96]{0:T(128)}, u32[]{:S(2)}) copy-start(f32[96]{0:T(128)} %param.17) | copy-start | bytes 1156
  60.5 31.3 %copy-start.1 = (f32[96,300]{1,0:T(8,128)S(1)}, f32[96,300]{1,0:T(8,128)}, u32[]{:S(2)}) copy-start(f32[96,300]{1,0:T(8,128)} %vec_ref.1) | copy-start | bytes 345604
  60.5 31.3 %copy-start.3 = (f32[96,300]{1,0:T(8,128)S(1)}, f32[96,300]{1,0:T(8,128)}, u32[]{:S(2)}) copy-start(f32[96,300]{1,0:T(8,128)} %acc_ref.1) | copy-start | bytes 345604
  60.5 31.3 %copy-start.4 = (f32[96]{0:T(128)S(1)}, f32[96]{0:T(128)}, u32[]{:S(2)}) copy-start(f32[96]{0:T(128)} %param.11) | copy-start | bytes 1156
  60.5 31.3 %copy-start.6 = (f32[96]{0:T(128)S(1)}, f32[96]{0:T(128)}, u32[]{:S(2)}) copy-start(f32[96]{0:T(128)} %param.13) | copy-start | bytes 1156
  60.6 10.0 %collective-permute-start.24 = (bf16[4,120,256]{2,1,0:T(8,128)(2,1)S(1)}, bf16[4,120,256]{2,1,0:T(8,128)(2,1)S(1)}, u32[]{:S(2)}, u32[]{:S(2)}) collective-permute-start(bf16[4,120,256]{2,1,0:T(8,128)(2,1)S(1)} %pad_maximum_fusion.3), channel_id=1, source_target_pairs={{0,32},{1,33},{2,34},{3,35},{4,36},{5,37},{6,38},{7,39},{8,40},{9,... | collective-permute-start | bytes 737288 | tf_op jit(solution)/shard_map/ppermute | solution.py:294
  69.3 5.3 %collective-permute-start.16 = (bf16[4,120,256]{2,1,0:T(8,128)(2,1)S(1)}, bf16[4,120,256]{2,1,0:T(8,128)(2,1)S(1)}, u32[]{:S(2)}, u32[]{:S(2)}) collective-permute-start(bf16[4,120,256]{2,1,0:T(8,128)(2,1)S(1)} %collective-permute-done.15), channel_id=1, source_target_pairs={{0,4},{1,5},{2,6},{3,7},{4,8},{5,9},{6,10},{7,11},{8,12},{9,13},{1... | collective-permute-start | bytes 737288 | tf_op jit(solution)/shard_map/ppermute | solution.py:294
  70.3 4.4 %collective-permute-start.13 = (bf16[4,120,256]{2,1,0:T(8,128)(2,1)S(1)}, bf16[4,120,256]{2,1,0:T(8,128)(2,1)S(1)}, u32[]{:S(2)}, u32[]{:S(2)}) collective-permute-start(bf16[4,120,256]{2,1,0:T(8,128)(2,1)S(1)} %slice.87), channel_id=1, source_target_pairs={{0,16},{1,17},{2,18},{3,19},{4,20},{5,21},{6,22},{7,23},{8,24},{9,... | collective-permute-start | bytes 737288 | tf_op jit(solution)/shard_map/ppermute | solution.py:294
  70.6 7.0 %collective-permute-start.25 = (bf16[2,120,256]{2,1,0:T(8,128)(2,1)S(1)}, bf16[2,120,256]{2,1,0:T(8,128)(2,1)S(1)}, u32[]{:S(2)}, u32[]{:S(2)}) collective-permute-start(bf16[2,120,256]{2,1,0:T(8,128)(2,1)S(1)} %slice.95), channel_id=1, source_target_pairs={{0,16},{1,17},{2,18},{3,19},{4,20},{5,21},{6,22},{7,23},{8,24},{9,... | collective-permute-start | bytes 368648 | tf_op jit(solution)/shard_map/ppermute | solution.py:294
  74.8 4.4 %collective-permute-start.17 = (bf16[120,256]{1,0:T(8,128)(2,1)S(1)}, bf16[120,256]{1,0:T(8,128)(2,1)S(1)}, u32[]{:S(2)}, u32[]{:S(2)}) collective-permute-start(bf16[120,256]{1,0:T(8,128)(2,1)S(1)} %get-tuple-element.69), channel_id=1, source_target_pairs={{0,1},{1,2},{2,3},{3,0},{4,5},{5,6},{6,7},{7,4},{8,9},{9,10},{10,1... | collective-permute-start | bytes 184328 | tf_op jit(solution)/shard_map/ppermute | solution.py:294
  77.7 2.3 %collective-permute-start.18 = (bf16[120,256]{1,0:T(8,128)(2,1)S(1)}, bf16[120,256]{1,0:T(8,128)(2,1)S(1)}, u32[]{:S(2)}, u32[]{:S(2)}) collective-permute-start(bf16[120,256]{1,0:T(8,128)(2,1)S(1)} %get-tuple-element.70), channel_id=1, source_target_pairs={{0,16},{1,17},{2,18},{3,19},{4,20},{5,21},{6,22},{7,23},{8,24},{9,... | collective-permute-start | bytes 184328 | tf_op jit(solution)/shard_map/ppermute | solution.py:294
  80.0 6.7 %collective-permute-start.19 = (bf16[2,120,256]{2,1,0:T(8,128)(2,1)S(1)}, bf16[2,120,256]{2,1,0:T(8,128)(2,1)S(1)}, u32[]{:S(2)}, u32[]{:S(2)}) collective-permute-start(bf16[2,120,256]{2,1,0:T(8,128)(2,1)S(1)} %pad_maximum_fusion.7), channel_id=1, source_target_pairs={{0,1},{1,2},{2,3},{3,0},{4,5},{5,6},{6,7},{7,4},{8,9},{9,10},{10,1... | collective-permute-start | bytes 368648 | tf_op jit(solution)/shard_map/ppermute | solution.py:294
  83.7 7.2 %collective-permute-start.26 = (bf16[120,256]{1,0:T(8,128)(2,1)S(1)}, bf16[120,256]{1,0:T(8,128)(2,1)S(1)}, u32[]{:S(2)}, u32[]{:S(2)}) collective-permute-start(bf16[120,256]{1,0:T(8,128)(2,1)S(1)} %fusion.3), channel_id=1, source_target_pairs={{0,128},{1,129},{2,130},{3,131},{4,132},{5,133},{6,134},{7,135},{8... | collective-permute-start | bytes 184328 | tf_op jit(solution)/shard_map/ppermute | solution.py:294
  86.7 5.1 %collective-permute-start.20 = (bf16[120,256]{1,0:T(8,128)(2,1)S(1)}, bf16[120,256]{1,0:T(8,128)(2,1)S(1)}, u32[]{:S(2)}, u32[]{:S(2)}) collective-permute-start(bf16[120,256]{1,0:T(8,128)(2,1)S(1)} %slice_bitcast_fusion.1), channel_id=1, source_target_pairs={{0,16},{1,17},{2,18},{3,19},{4,20},{5,21},{6,22},{7,23},{8,24},{9,... | collective-permute-start | bytes 184328 | tf_op jit(solution)/shard_map/ppermute | solution.py:294

commit v2 on v1

--- a/solution.py
+++ b/solution.py
@@ -150,7 +150,7 @@
     return [pack_rows(part[:, :LO], part[:, LO:]) for part in parts]
 
 
-def own_kernel(index_ref, w0, c0, c1, weight, log_count, grad, scaled, words_t, ctx_full, ctx_t, words):
+def build(index_ref, c0, c1, ctx_full, ctx_t):
     lane = lax.broadcasted_iota(jnp.int32, (ROWS, 128), 1)
     bw, bc = D - LO, D - LO + 1
     for i in range(16):
@@ -160,24 +160,17 @@
         ctx_full[rows_of(index_ref, i), :LO] = packed[:ROWS].astype(jnp.bfloat16)
         ctx_full[rows_of(index_ref, i), LO:] = tail.astype(jnp.bfloat16)
     ctx_t[...] = ctx_full[...].T
-    blocks = [w0[j] for j in range(4)]
+
+
+def chunk_kernel(w, weight, log_count, ctx_full, ctx_t, grad, scaled, words_t, words):
+    blocks = [w[j] for j in range(4)]
     for j, packed in enumerate(word_chunk(blocks, weight, log_count, ctx_full, ctx_t, words, words_t, scaled)):
-        grad[j] = packed
-
-
-def near_kernel(w1, w3, k1, l1, k3, l3, ctx_full, ctx_t, g1, g3, scaled1, scaled3, words_t1, words_t3, words):
-    for w, weight, log_count, grad, scaled, words_t in (
-        (w1, k1, l1, g1, scaled1, words_t1), (w3, k3, l3, g3, scaled3, words_t3)
-    ):
-        blocks = [w[j] for j in range(4)]
-        for j, packed in enumerate(word_chunk(blocks, weight, log_count, ctx_full, ctx_t, words, words_t, scaled)):
-            grad[j] = packed.astype(jnp.bfloat16)
-
-
-def far_kernel(w2, weight, log_count, ctx_full, ctx_t, grad, scaled, words_t, words):
-    blocks = [w2[j] for j in range(4)]
-    for j, packed in enumerate(word_chunk(blocks, weight, log_count, ctx_full, ctx_t, words, words_t, scaled)):
-        grad[j] = packed.astype(jnp.bfloat16)
+        grad[j] = packed.astype(grad.dtype)
+
+
+def first_kernel(index_ref, w, c0, c1, weight, log_count, grad, scaled, words_t, ctx_full, ctx_t, words):
+    build(index_ref, c0, c1, ctx_full, ctx_t)
+    chunk_kernel(w, weight, log_count, ctx_full, ctx_t, grad, scaled, words_t, words)
 
 
 def ctx_kernel(index_ref, s0, s1, s2, s3, t0, t1, t2, t3, h_own, h_other, ctx_grad, back):
@@ -329,24 +322,25 @@
     w2 = go(yr1[:4], "y")
     w1 = go(yr1[4:], "core")
 
-    k0, l0, k1, l1 = keep(weights((0, 1), row_index, counts))
-    k3, l3, k2, l2 = keep(weights((3, 2), row_index, counts))
+    k0, l0 = keep(weights((0,), row_index, counts))
+    k3, l3 = keep(weights((3,), row_index, counts))
+    k1, l1, k2, l2 = keep(weights((1, 2), row_index, counts))
     scaled_shape, words_t_shape = low_shape(CHUNK, COLUMNS), low_shape(384, CHUNK)
-    g0, s0, t0, ctx_full, ctx_t = call(
-        own_kernel, (piece_index,), (wy, c0, c1, k0, l0),
-        [blocks_shape(4, f32), scaled_shape, words_t_shape, low_shape(COLUMNS, 384), low_shape(384, COLUMNS)],
+    g3, s3, t3, ctx_full, ctx_t = call(
+        first_kernel, (piece_index,), (yr1, c0, c1, k3, l3),
+        [blocks_shape(4, low), scaled_shape, words_t_shape, low_shape(COLUMNS, 384), low_shape(384, COLUMNS)],
         WORDS_SCRATCH, CHUNK_FLOPS, 16,
     )
-    g1, g3, s1, s3, t1, t3 = call(
-        near_kernel, (), (w1, yr1, k1, l1, k3, l3, ctx_full, ctx_t),
-        [blocks_shape(4, low)] * 2 + [scaled_shape] * 2 + [words_t_shape] * 2,
-        WORDS_SCRATCH, 2 * CHUNK_FLOPS, 16,
-    )
-    g2, s2, t2 = call(
-        far_kernel, (), (w2, k2, l2, ctx_full, ctx_t),
-        [blocks_shape(4, low), scaled_shape, words_t_shape],
-        WORDS_SCRATCH, CHUNK_FLOPS, 16,
-    )
+
+    def chunk(w, weight, log_count, dtype):
+        return call(
+            chunk_kernel, (), (w, weight, log_count, ctx_full, ctx_t),
+            [blocks_shape(4, dtype), scaled_shape, words_t_shape], WORDS_SCRATCH, CHUNK_FLOPS, 16,
+        )
+
+    g1, s1, t1 = chunk(w1, k1, l1, low)
+    g2, s2, t2 = chunk(w2, k2, l2, low)
+    g0, s0, t0 = chunk(wy, k0, l0, f32)
     h_own, h_other = call(
         ctx_kernel, (result_index,), (s0, s1, s2, s3, t0, t1, t2, t3),
         [blocks_shape(8, f32), blocks_shape(8, low)],

time: 93.5 us -> 95.9 us (1.026)
  starting transfers between devices: 45.6 us -> 54.6 us
  waiting for transfers between devices: 23.6 us -> 15.7 us
  Pallas kernels: 21.9 us -> 23.6 us
    ppermute x27, starting transfers between devices: 45.6 us -> 54.6 us  [move(): return lax.ppermute(value, ('word', 'ctx'), perm)]
    ppermute x27, waiting for transfers between devices: 23.6 us -> 15.7 us  [move(): return lax.ppermute(value, ('word', 'ctx'), perm)]
    pallas_call x2 -> x3, Pallas kernels: 8.13 us -> 9.73 us  [weights(): pl.pallas_call(functools.partial(weight_kernel, chunks), in_specs=[pl.Blo...]
    pallas_call x5 -> x6, Pallas kernels: 10.2 us -> 10.4 us  [call(): pl.pallas_call(kernel, in_specs=[SMEM_SPEC] * len(scalars) + [VMEM_SPEC]...]
  transfers between devices with their start and end apart: 27 -> 27, of which waited for: 11 -> 13; matrix products, arithmetic and copies ran while one was open for 1% -> 1% of each run, Pallas kernels for 14% -> 17%
where the time goes in v2:
time: 95.9 us; the launch traced here: 95.7 us
  starting transfers between devices  54.6 us (57%)
  Pallas kernels  23.6 us (25%)
  waiting for transfers between devices  15.7 us (16%)
  between operations  1.04 us (1%)
    ppermute x27, starting transfers between devices, move(): return lax.ppermute(value, ('word', 'ctx'), perm)  54.6 us
    ppermute x27, waiting for transfers between devices, move(): return lax.ppermute(value, ('word', 'ctx'), perm)  15.7 us
    pallas_call x6, Pallas kernels, call(): pl.pallas_call(kernel, in_specs=[SMEM_SPEC] * len(scalars) + [VMEM_SPEC]...  10.4 us
    pallas_call x3, Pallas kernels, weights(): pl.pallas_call(functools.partial(weight_kernel, chunks), in_specs=[pl.Blo...  9.73 us
  transfers between devices with their start and end apart: 27, of which 13 were waited for; matrix products, arithmetic and copies ran while one was open for 1% of the time, Pallas kernels for 17%

profile of v2, /device:TPU:1, one launch (start us, length us, event | category | flops | bytes accessed | tf_op | source)
XLA Modules:
  0.0 95.7 jit_solution(10861411468828936879)
XLA Ops:
  0.6 1.8 %pack.1 = (bf16[120,256]{1,0:T(8,128)(2,1)S(1)}, bf16[120,256]{1,0:T(8,128)(2,1)S(1)}, s32[16]{0:T(128)S(1)}, s32[16]{0:T(128)S(1)}, s32[16]{0:T(128)S(1)}) custom-call(f32[96,300]{1,0:T(8,128)} %vec_ref.1, f32[1,96]{1,0:T(1,128)} %bitcast.28, f32[96,300]{1,0:T(8,128)} %rest_0_.1, f32[1,96]{1,0:T(1,128)} %bitcast.30), custom_call_target="tpu_custom_call" | custom-call | flops 100000 | bytes 400000 | tf_op jit(solution)/shard_map/pack/pallas_call | solution.py:78
  2.4 3.3 %collective-permute-start = (bf16[120,256]{1,0:T(8,128)(2,1)S(1)}, bf16[120,256]{1,0:T(8,128)(2,1)S(1)}, u32[]{:S(2)}, u32[]{:S(2)}) collective-permute-start(bf16[120,256]{1,0:T(8,128)(2,1)S(1)} %get-tuple-element.49), channel_id=1, source_target_pairs={{0,16},{1,17},{2,18},{3,19},{4,20},{5,21},{6,22},{7,23},{8,24},{9,... | collective-permute-start | bytes 184328 | tf_op jit(solution)/shard_map/ppermute | solution.py:287
  5.7 0.9 collective-permute-done
  6.6 4.4 %collective-permute-start.1 = (bf16[2,120,256]{2,1,0:T(8,128)(2,1)S(1)}, bf16[2,120,256]{2,1,0:T(8,128)(2,1)S(1)}, u32[]{:S(2)}, u32[]{:S(2)}) collective-permute-start(bf16[2,120,256]{2,1,0:T(8,128)(2,1)S(1)} %pad_maximum_fusion.5), channel_id=1, source_target_pairs={{0,1},{1,2},{2,3},{3,0},{4,5},{5,6},{6,7},{7,4},{8,9},{9,10},{10,1... | collective-permute-start | bytes 368648 | tf_op jit(solution)/shard_map/ppermute | solution.py:287
  11.0 3.1 %collective-permute-done.1 = bf16[2,120,256]{2,1,0:T(8,128)(2,1)S(1)} collective-permute-done((bf16[2,120,256]{2,1,0:T(8,128)(2,1)S(1)}, bf16[2,120,256]{2,1,0:T(8,128)(2,1)S(1)}, u32[]{:S(2)}, u32[]{:S(2)}) %collective-permute-start.1) | collective-permute-done | bytes 122912 | tf_op jit(solution)/shard_map/ppermute | solution.py:287
  14.2 4.1 %collective-permute-start.2 = (bf16[1,120,256]{2,1,0:T(8,128)(2,1)S(1)}, bf16[1,120,256]{2,1,0:T(8,128)(2,1)S(1)}, u32[]{:S(2)}, u32[]{:S(2)}) collective-permute-start(bf16[1,120,256]{2,1,0:T(8,128)(2,1)S(1)} %get-tuple-element.97), channel_id=1, source_target_pairs={{0,1},{1,2},{2,3},{3,0},{4,5},{5,6},{6,7},{7,4},{8,9},{9,10},{10,1... | collective-permute-start | bytes 184328 | tf_op jit(solution)/shard_map/ppermute | solution.py:287
  18.4 1.2 %collective-permute-done.2 = bf16[1,120,256]{2,1,0:T(8,128)(2,1)S(1)} collective-permute-done((bf16[1,120,256]{2,1,0:T(8,128)(2,1)S(1)}, bf16[1,120,256]{2,1,0:T(8,128)(2,1)S(1)}, u32[]{:S(2)}, u32[]{:S(2)}) %collective-permute-start.2) | collective-permute-done | bytes 61472 | tf_op jit(solution)/shard_map/ppermute | solution.py:287
  19.6 2.1 %collective-permute-start.3 = (bf16[3,120,256]{2,1,0:T(8,128)(2,1)S(1)}, bf16[3,120,256]{2,1,0:T(8,128)(2,1)S(1)}, u32[]{:S(2)}, u32[]{:S(2)}) collective-permute-start(bf16[3,120,256]{2,1,0:T(8,128)(2,1)S(1)} %pad_maximum_fusion.4), channel_id=1, source_target_pairs={{0,16},{1,17},{2,18},{3,19},{4,20},{5,21},{6,22},{7,23},{8,24},{9,... | collective-permute-start | bytes 552968 | tf_op jit(solution)/shard_map/ppermute | solution.py:287
  21.7 2.8 %shard_map.153 = (f32[384,1536]{1,0:T(8,128)S(1)}, f32[384,1536]{1,0:T(8,128)S(1)}) custom-call(s32[16]{0:T(128)S(1)} %get-tuple-element.50.index_ref, s32[1536,1536]{1,0:T(8,128)} %counts.5), custom_call_target="tpu_custom_call" | custom-call | flops 11796480 | bytes 7077888 | tf_op jit(solution)/shard_map/pallas_call | solution.py:118
  24.6 2.8 %shard_map.152 = (f32[384,1536]{1,0:T(8,128)S(1)}, f32[384,1536]{1,0:T(8,128)S(1)}) custom-call(s32[16]{0:T(128)S(1)} %get-tuple-element.50.index_ref, s32[1536,1536]{1,0:T(8,128)} %counts.5), custom_call_target="tpu_custom_call" | custom-call | flops 11796480 | bytes 7077888 | tf_op jit(solution)/shard_map/pallas_call | solution.py:118
  27.4 4.1 %shard_map.156 = (f32[384,1536]{1,0:T(8,128)S(1)}, f32[384,1536]{1,0:T(8,128)S(1)}, f32[384,1536]{1,0:T(8,128)S(1)}, f32[384,1536]{1,0:T(8,128)S(1)}) custom-call(s32[16]{0:T(128)S(1)} %get-tuple-element.50.index_ref, s32[1536,1536]{1,0:T(8,128)} %counts.5), custom_call_target="tpu_custom_call" | custom-call | flops 23592960 | bytes 14155776 | tf_op jit(solution)/shard_map/pallas_call | solution.py:118
  31.5 2.6 %collective-permute-start.7 = (bf16[4,120,256]{2,1,0:T(8,128)(2,1)S(1)}, bf16[4,120,256]{2,1,0:T(8,128)(2,1)S(1)}, u32[]{:S(2)}, u32[]{:S(2)}) collective-permute-start(bf16[4,120,256]{2,1,0:T(8,128)(2,1)S(1)} %pad_maximum_fusion.2), channel_id=1, source_target_pairs={{0,32},{1,33},{2,34},{3,35},{4,36},{5,37},{6,38},{7,39},{8,40},{9,... | collective-permute-start | bytes 737288 | tf_op jit(solution)/shard_map/ppermute | solution.py:287
  34.2 2.8 %collective-permute-start.4 = (bf16[8,120,256]{2,1,0:T(8,128)(2,1)S(1)}, bf16[8,120,256]{2,1,0:T(8,128)(2,1)S(1)}, u32[]{:S(2)}, u32[]{:S(2)}) collective-permute-start(bf16[8,120,256]{2,1,0:T(8,128)(2,1)S(1)} %slice_dynamic-update-slice_fusion.w), channel_id=1, source_target_pairs={{0,4},{1,5},{2,6},{3,7},{4,8},{5,9},{6,10},{7,11},{8,12},{9,13},{1... | collective-permute-start | bytes 1474568 | tf_op jit(solution)/shard_map/ppermute | solution.py:287
  37.0 0.2 collective-permute-done.7
  37.2 3.5 %collective-permute-start.8 = (bf16[2,120,256]{2,1,0:T(8,128)(2,1)S(1)}, bf16[2,120,256]{2,1,0:T(8,128)(2,1)S(1)}, u32[]{:S(2)}, u32[]{:S(2)}) collective-permute-start(bf16[2,120,256]{2,1,0:T(8,128)(2,1)S(1)} %slice.85), channel_id=1, source_target_pairs={{0,32},{1,33},{2,34},{3,35},{4,36},{5,37},{6,38},{7,39},{8,40},{9,... | collective-permute-start | bytes 368648 | tf_op jit(solution)/shard_map/ppermute | solution.py:287
  40.7 1.9 %collective-permute-done.8 = bf16[2,120,256]{2,1,0:T(8,128)(2,1)S(1)} collective-permute-done((bf16[2,120,256]{2,1,0:T(8,128)(2,1)S(1)}, bf16[2,120,256]{2,1,0:T(8,128)(2,1)S(1)}, u32[]{:S(2)}, u32[]{:S(2)}) %collective-permute-start.8) | collective-permute-done | bytes 122912 | tf_op jit(solution)/shard_map/ppermute | solution.py:287
  42.6 2.7 %collective-permute-start.9 = (bf16[6,120,256]{2,1,0:T(8,128)(2,1)S(1)}, bf16[6,120,256]{2,1,0:T(8,128)(2,1)S(1)}, u32[]{:S(2)}, u32[]{:S(2)}) collective-permute-start(bf16[6,120,256]{2,1,0:T(8,128)(2,1)S(1)} %pad_maximum_fusion.1), channel_id=1, source_target_pairs={{0,16},{1,17},{2,18},{3,19},{4,20},{5,21},{6,22},{7,23},{8,24},{9,... | collective-permute-start | bytes 1105928 | tf_op jit(solution)/shard_map/ppermute | solution.py:287
  45.4 2.8 %collective-permute-start.14 = (bf16[4,120,256]{2,1,0:T(8,128)(2,1)S(1)}, bf16[4,120,256]{2,1,0:T(8,128)(2,1)S(1)}, u32[]{:S(2)}, u32[]{:S(2)}) collective-permute-start(bf16[4,120,256]{2,1,0:T(8,128)(2,1)S(1)} %get-tuple-element.94), channel_id=1, source_target_pairs={{0,4},{1,5},{2,6},{3,7},{4,8},{5,9},{6,10},{7,11},{8,12},{9,13},{1... | collective-permute-start | bytes 737288 | tf_op jit(solution)/shard_map/ppermute | solution.py:287
  48.2 0.3 collective-permute-start.10
  48.5 2.3 %shard_map.154 = (bf16[4,120,256]{2,1,0:T(8,128)(2,1)S(1)}, bf16[384,1536]{1,0:T(8,128)(2,1)S(1)}, bf16[384,384]{1,0:T(8,128)(2,1)S(1)}, bf16[1536,384]{1,0:T(8,128)(2,1)S(1)}, bf16[384,1536]{1,0:T(8,128)(2,1)S(1)}) custom-call(s32[16]{0:T(128)S(1)} %get-tuple-element.53.index_ref, bf16[8,120,256]{2,1,0:T(8,128)(2,1)S(1)} %collective-permute-done.4.w, ...), custom_call_target="tpu_custom_call" | custom-call | flops 905969664 | bytes 4194304 | tf_op jit(solution)/shard_map/pallas_call | solution.py:211
  50.8 1.5 %shard_map.155 = (f32[4,120,256]{2,1,0:T(8,128)S(1)}, bf16[384,1536]{1,0:T(8,128)(2,1)S(1)}, bf16[384,384]{1,0:T(8,128)(2,1)S(1)}) custom-call(bf16[8,120,256]{2,1,0:T(8,128)(2,1)S(1)} %slice_dynamic-update-slice_fusion.w, f32[384,1536]{1,0:T(8,128)S(1)} %get-tuple-element.51.weight, f32[384,1536]{1,0:T(8,128)S(1)} %get-tuple-element.52.log_count, ...), custom_call_target="tpu_custom_call" | custom-call | flops 905969664 | bytes 4194304 | tf_op jit(solution)/shard_map/pallas_call | solution.py:211
  52.3 1.5 %shard_map.158 = (bf16[4,120,256]{2,1,0:T(8,128)(2,1)S(1)}, bf16[384,1536]{1,0:T(8,128)(2,1)S(1)}, bf16[384,384]{1,0:T(8,128)(2,1)S(1)}) custom-call(bf16[4,120,256]{2,1,0:T(8,128)(2,1)S(1)} %collective-permute-done.14.w, f32[384,1536]{1,0:T(8,128)S(1)} %get-tuple-element.64.weight, f32[384,1536]{1,0:T(8,128)S(1)} %get-tuple-element.65.log_count, ...), custom_call_target="tpu_custom_call" | custom-call | flops 905969664 | bytes 4194304 | tf_op jit(solution)/shard_map/pallas_call | solution.py:211
  53.8 1.5 %shard_map.157 = (bf16[4,120,256]{2,1,0:T(8,128)(2,1)S(1)}, bf16[384,1536]{1,0:T(8,128)(2,1)S(1)}, bf16[384,384]{1,0:T(8,128)(2,1)S(1)}) custom-call(bf16[4,120,256]{2,1,0:T(8,128)(2,1)S(1)} %collective-permute-done.10.w, f32[384,1536]{1,0:T(8,128)S(1)} %get-tuple-element.60.weight, f32[384,1536]{1,0:T(8,128)S(1)} %get-tuple-element.61.log_count, ...), custom_call_target="tpu_custom_call" | custom-call | flops 905969664 | bytes 4194304 | tf_op jit(solution)/shard_map/pallas_call | solution.py:211
  55.3 3.5 %shard_map.161 = (f32[8,120,256]{2,1,0:T(8,128)S(1)}, bf16[8,120,256]{2,1,0:T(8,128)(2,1)S(1)}) custom-call(s32[16]{0:T(128)S(1)} %get-tuple-element.75.index_ref, bf16[384,1536]{1,0:T(8,128)(2,1)S(1)} %get-tuple-element.76.s0, bf16[384,1536]{1,0:T(8,128)(2,1)S(1)} %get-tuple-element.77.s1, bf16[384,1536]{1,0:T(8,128)(2,1)S(1)} %get-tuple-element.78.s2, ...), custom_call_target="tpu_custom_call" | custom-call | flops 1811939328 | bytes 4194304 | tf_op jit(solution)/shard_map/pallas_call | solution.py:211
  58.8 0.7 collective-permute-start.21
  59.6 2.0 %collective-permute-start.15 = (bf16[4,120,256]{2,1,0:T(8,128)(2,1)S(1)}, bf16[4,120,256]{2,1,0:T(8,128)(2,1)S(1)}, u32[]{:S(2)}, u32[]{:S(2)}) collective-permute-start(bf16[4,120,256]{2,1,0:T(8,128)(2,1)S(1)} %get-tuple-element.66), channel_id=1, source_target_pairs={{0,4},{1,5},{2,6},{3,7},{4,8},{5,9},{6,10},{7,11},{8,12},{9,13},{1... | collective-permute-start | bytes 737288 | tf_op jit(solution)/shard_map/ppermute | solution.py:287
  61.6 1.8 %collective-permute-start.12 = (bf16[8,120,256]{2,1,0:T(8,128)(2,1)S(1)}, bf16[8,120,256]{2,1,0:T(8,128)(2,1)S(1)}, u32[]{:S(2)}, u32[]{:S(2)}) collective-permute-start(bf16[8,120,256]{2,1,0:T(8,128)(2,1)S(1)} %pad_maximum_fusion), channel_id=1, source_target_pairs={{0,4},{1,5},{2,6},{3,7},{4,8},{5,9},{6,10},{7,11},{8,12},{9,13},{1... | collective-permute-start | bytes 1474568 | tf_op jit(solution)/shard_map/ppermute | solution.py:287
  63.4 0.1 fusion.4
  63.6 0.3 collective-permute-start.22
  64.0 1.0 %collective-permute-done.15 = bf16[4,120,256]{2,1,0:T(8,128)(2,1)S(1)} collective-permute-done((bf16[4,120,256]{2,1,0:T(8,128)(2,1)S(1)}, bf16[4,120,256]{2,1,0:T(8,128)(2,1)S(1)}, u32[]{:S(2)}, u32[]{:S(2)}) %collective-permute-start.15) | collective-permute-done | bytes 245792 | tf_op jit(solution)/shard_map/ppermute | solution.py:287
  65.0 2.9 %collective-permute-start.16 = (bf16[4,120,256]{2,1,0:T(8,128)(2,1)S(1)}, bf16[4,120,256]{2,1,0:T(8,128)(2,1)S(1)}, u32[]{:S(2)}, u32[]{:S(2)}) collective-permute-start(bf16[4,120,256]{2,1,0:T(8,128)(2,1)S(1)} %collective-permute-done.15), channel_id=1, source_target_pairs={{0,4},{1,5},{2,6},{3,7},{4,8},{5,9},{6,10},{7,11},{8,12},{9,13},{1... | collective-permute-start | bytes 737288 | tf_op jit(solution)/shard_map/ppermute | solution.py:287
  67.8 2.4 %collective-permute-done.12.rn = bf16[8,120,256]{2,1,0:T(8,128)(2,1)S(1)} collective-permute-done((bf16[8,120,256]{2,1,0:T(8,128)(2,1)S(1)}, bf16[8,120,256]{2,1,0:T(8,128)(2,1)S(1)}, u32[]{:S(2)}, u32[]{:S(2)}) %collective-permute-start.12) | collective-permute-done | bytes 491552 | tf_op jit(solution)/shard_map/ppermute | solution.py:287
  70.2 2.6 %collective-permute-start.13 = (bf16[4,120,256]{2,1,0:T(8,128)(2,1)S(1)}, bf16[4,120,256]{2,1,0:T(8,128)(2,1)S(1)}, u32[]{:S(2)}, u32[]{:S(2)}) collective-permute-start(bf16[4,120,256]{2,1,0:T(8,128)(2,1)S(1)} %slice.87), channel_id=1, source_target_pairs={{0,16},{1,17},{2,18},{3,19},{4,20},{5,21},{6,22},{7,23},{8,24},{9,... | collective-permute-start | bytes 737288 | tf_op jit(solution)/shard_map/ppermute | solution.py:287
  73.0 0.9 collective-permute-done.13.f2
  73.9 0.1 shard_map.159
  74.1 2.7 %collective-permute-start.17 = (bf16[120,256]{1,0:T(8,128)(2,1)S(1)}, bf16[120,256]{1,0:T(8,128)(2,1)S(1)}, u32[]{:S(2)}, u32[]{:S(2)}) collective-permute-start(bf16[120,256]{1,0:T(8,128)(2,1)S(1)} %get-tuple-element.69), channel_id=1, source_target_pairs={{0,1},{1,2},{2,3},{3,0},{4,5},{5,6},{6,7},{7,4},{8,9},{9,10},{10,1... | collective-permute-start | bytes 184328 | tf_op jit(solution)/shard_map/ppermute | solution.py:287
  76.8 0.5 collective-permute-start.24
  77.3 1.0 %collective-permute-done.17 = bf16[120,256]{1,0:T(8,128)(2,1)S(1)} collective-permute-done((bf16[120,256]{1,0:T(8,128)(2,1)S(1)}, bf16[120,256]{1,0:T(8,128)(2,1)S(1)}, u32[]{:S(2)}, u32[]{:S(2)}) %collective-permute-start.17) | collective-permute-done | bytes 61472 | tf_op jit(solution)/shard_map/ppermute | solution.py:287
  78.3 0.2 collective-permute-done.18
  78.6 3.5 %collective-permute-start.19 = (bf16[2,120,256]{2,1,0:T(8,128)(2,1)S(1)}, bf16[2,120,256]{2,1,0:T(8,128)(2,1)S(1)}, u32[]{:S(2)}, u32[]{:S(2)}) collective-permute-start(bf16[2,120,256]{2,1,0:T(8,128)(2,1)S(1)} %pad_maximum_fusion.7), channel_id=1, source_target_pairs={{0,1},{1,2},{2,3},{3,0},{4,5},{5,6},{6,7},{7,4},{8,9},{9,10},{10,1... | collective-permute-start | bytes 368648 | tf_op jit(solution)/shard_map/ppermute | solution.py:287
  82.0 0.1 collective-permute-done.24
  82.2 2.5 %collective-permute-start.25 = (bf16[2,120,256]{2,1,0:T(8,128)(2,1)S(1)}, bf16[2,120,256]{2,1,0:T(8,128)(2,1)S(1)}, u32[]{:S(2)}, u32[]{:S(2)}) collective-permute-start(bf16[2,120,256]{2,1,0:T(8,128)(2,1)S(1)} %slice.95), channel_id=1, source_target_pairs={{0,16},{1,17},{2,18},{3,19},{4,20},{5,21},{6,22},{7,23},{8,24},{9,... | collective-permute-start | bytes 368648 | tf_op jit(solution)/shard_map/ppermute | solution.py:287
  84.7 1.3 %collective-permute-done.19.add_a = bf16[2,120,256]{2,1,0:T(8,128)(2,1)S(1)} collective-permute-done((bf16[2,120,256]{2,1,0:T(8,128)(2,1)S(1)}, bf16[2,120,256]{2,1,0:T(8,128)(2,1)S(1)}, u32[]{:S(2)}, u32[]{:S(2)}) %collective-permute-start.19) | collective-permute-done | bytes 122912 | tf_op jit(solution)/shard_map/ppermute | solution.py:287
  86.0 4.5 %collective-permute-start.20 = (bf16[120,256]{1,0:T(8,128)(2,1)S(1)}, bf16[120,256]{1,0:T(8,128)(2,1)S(1)}, u32[]{:S(2)}, u32[]{:S(2)}) collective-permute-start(bf16[120,256]{1,0:T(8,128)(2,1)S(1)} %slice_bitcast_fusion.1), channel_id=1, source_target_pairs={{0,16},{1,17},{2,18},{3,19},{4,20},{5,21},{6,22},{7,23},{8,24},{9,... | collective-permute-start | bytes 184328 | tf_op jit(solution)/shard_map/ppermute | solution.py:287
  90.6 1.9 %collective-permute-start.26 = (bf16[120,256]{1,0:T(8,128)(2,1)S(1)}, bf16[120,256]{1,0:T(8,128)(2,1)S(1)}, u32[]{:S(2)}, u32[]{:S(2)}) collective-permute-start(bf16[120,256]{1,0:T(8,128)(2,1)S(1)} %fusion.3), channel_id=1, source_target_pairs={{0,128},{1,129},{2,130},{3,131},{4,132},{5,133},{6,134},{7,135},{8... | collective-permute-start | bytes 184328 | tf_op jit(solution)/shard_map/ppermute | solution.py:287
  92.5 0.9 shard_map.160
  93.4 1.4 %collective-permute-done.26.a = bf16[120,256]{1,0:T(8,128)(2,1)S(1)} collective-permute-done((bf16[120,256]{1,0:T(8,128)(2,1)S(1)}, bf16[120,256]{1,0:T(8,128)(2,1)S(1)}, u32[]{:S(2)}, u32[]{:S(2)}) %collective-permute-start.26) | collective-permute-done | bytes 61472 | tf_op jit(solution)/shard_map/ppermute | solution.py:287
  94.9 0.9 shard_map.162
  (68 shorter events, 0.9 us)
Async XLA Ops:
  2.4 4.2 %collective-permute-start = (bf16[120,256]{1,0:T(8,128)(2,1)S(1)}, bf16[120,256]{1,0:T(8,128)(2,1)S(1)}, u32[]{:S(2)}, u32[]{:S(2)}) collective-permute-start(bf16[120,256]{1,0:T(8,128)(2,1)S(1)} %get-tuple-element.49), channel_id=1, source_target_pairs={{0,16},{1,17},{2,18},{3,19},{4,20},{5,21},{6,22},{7,23},{8,24},{9,... | collective-permute-start | bytes 184328 | tf_op jit(solution)/shard_map/ppermute | solution.py:287
  5.7 12.6 %collective-permute-start.5 = (bf16[120,256]{1,0:T(8,128)(2,1)S(1)}, bf16[120,256]{1,0:T(8,128)(2,1)S(1)}, u32[]{:S(2)}, u32[]{:S(2)}) collective-permute-start(bf16[120,256]{1,0:T(8,128)(2,1)S(1)} %get-tuple-element.54), channel_id=1, source_target_pairs={{0,128},{1,129},{2,130},{3,131},{4,132},{5,133},{6,134},{7,135},{8... | collective-permute-start | bytes 184328 | tf_op jit(solution)/shard_map/ppermute | solution.py:287
  6.6 7.5 %collective-permute-start.1 = (bf16[2,120,256]{2,1,0:T(8,128)(2,1)S(1)}, bf16[2,120,256]{2,1,0:T(8,128)(2,1)S(1)}, u32[]{:S(2)}, u32[]{:S(2)}) collective-permute-start(bf16[2,120,256]{2,1,0:T(8,128)(2,1)S(1)} %pad_maximum_fusion.5), channel_id=1, source_target_pairs={{0,1},{1,2},{2,3},{3,0},{4,5},{5,6},{6,7},{7,4},{8,9},{9,10},{10,1... | collective-permute-start | bytes 368648 | tf_op jit(solution)/shard_map/ppermute | solution.py:287
  14.2 5.4 %collective-permute-start.2 = (bf16[1,120,256]{2,1,0:T(8,128)(2,1)S(1)}, bf16[1,120,256]{2,1,0:T(8,128)(2,1)S(1)}, u32[]{:S(2)}, u32[]{:S(2)}) collective-permute-start(bf16[1,120,256]{2,1,0:T(8,128)(2,1)S(1)} %get-tuple-element.97), channel_id=1, source_target_pairs={{0,1},{1,2},{2,3},{3,0},{4,5},{5,6},{6,7},{7,4},{8,9},{9,10},{10,1... | collective-permute-start | bytes 184328 | tf_op jit(solution)/shard_map/ppermute | solution.py:287
  18.3 13.2 %collective-permute-start.6 = (bf16[2,120,256]{2,1,0:T(8,128)(2,1)S(1)}, bf16[2,120,256]{2,1,0:T(8,128)(2,1)S(1)}, u32[]{:S(2)}, u32[]{:S(2)}) collective-permute-start(bf16[2,120,256]{2,1,0:T(8,128)(2,1)S(1)} %pad_maximum_fusion.6), channel_id=1, source_target_pairs={{0,16},{1,17},{2,18},{3,19},{4,20},{5,21},{6,22},{7,23},{8,24},{9,... | collective-permute-start | bytes 368648 | tf_op jit(solution)/shard_map/ppermute | solution.py:287
  19.6 14.5 %collective-permute-start.3 = (bf16[3,120,256]{2,1,0:T(8,128)(2,1)S(1)}, bf16[3,120,256]{2,1,0:T(8,128)(2,1)S(1)}, u32[]{:S(2)}, u32[]{:S(2)}) collective-permute-start(bf16[3,120,256]{2,1,0:T(8,128)(2,1)S(1)} %pad_maximum_fusion.4), channel_id=1, source_target_pairs={{0,16},{1,17},{2,18},{3,19},{4,20},{5,21},{6,22},{7,23},{8,24},{9,... | collective-permute-start | bytes 552968 | tf_op jit(solution)/shard_map/ppermute | solution.py:287
  31.5 5.7 %collective-permute-start.7 = (bf16[4,120,256]{2,1,0:T(8,128)(2,1)S(1)}, bf16[4,120,256]{2,1,0:T(8,128)(2,1)S(1)}, u32[]{:S(2)}, u32[]{:S(2)}) collective-permute-start(bf16[4,120,256]{2,1,0:T(8,128)(2,1)S(1)} %pad_maximum_fusion.2), channel_id=1, source_target_pairs={{0,32},{1,33},{2,34},{3,35},{4,36},{5,37},{6,38},{7,39},{8,40},{9,... | collective-permute-start | bytes 737288 | tf_op jit(solution)/shard_map/ppermute | solution.py:287
  34.2 11.2 %collective-permute-start.4 = (bf16[8,120,256]{2,1,0:T(8,128)(2,1)S(1)}, bf16[8,120,256]{2,1,0:T(8,128)(2,1)S(1)}, u32[]{:S(2)}, u32[]{:S(2)}) collective-permute-start(bf16[8,120,256]{2,1,0:T(8,128)(2,1)S(1)} %slice_dynamic-update-slice_fusion.w), channel_id=1, source_target_pairs={{0,4},{1,5},{2,6},{3,7},{4,8},{5,9},{6,10},{7,11},{8,12},{9,13},{1... | collective-permute-start | bytes 1474568 | tf_op jit(solution)/shard_map/ppermute | solution.py:287
  37.2 5.4 %collective-permute-start.8 = (bf16[2,120,256]{2,1,0:T(8,128)(2,1)S(1)}, bf16[2,120,256]{2,1,0:T(8,128)(2,1)S(1)}, u32[]{:S(2)}, u32[]{:S(2)}) collective-permute-start(bf16[2,120,256]{2,1,0:T(8,128)(2,1)S(1)} %slice.85), channel_id=1, source_target_pairs={{0,32},{1,33},{2,34},{3,35},{4,36},{5,37},{6,38},{7,39},{8,40},{9,... | collective-permute-start | bytes 368648 | tf_op jit(solution)/shard_map/ppermute | solution.py:287
  42.6 5.9 %collective-permute-start.9 = (bf16[6,120,256]{2,1,0:T(8,128)(2,1)S(1)}, bf16[6,120,256]{2,1,0:T(8,128)(2,1)S(1)}, u32[]{:S(2)}, u32[]{:S(2)}) collective-permute-start(bf16[6,120,256]{2,1,0:T(8,128)(2,1)S(1)} %pad_maximum_fusion.1), channel_id=1, source_target_pairs={{0,16},{1,17},{2,18},{3,19},{4,20},{5,21},{6,22},{7,23},{8,24},{9,... | collective-permute-start | bytes 1105928 | tf_op jit(solution)/shard_map/ppermute | solution.py:287
  45.4 6.9 %collective-permute-start.14 = (bf16[4,120,256]{2,1,0:T(8,128)(2,1)S(1)}, bf16[4,120,256]{2,1,0:T(8,128)(2,1)S(1)}, u32[]{:S(2)}, u32[]{:S(2)}) collective-permute-start(bf16[4,120,256]{2,1,0:T(8,128)(2,1)S(1)} %get-tuple-element.94), channel_id=1, source_target_pairs={{0,4},{1,5},{2,6},{3,7},{4,8},{5,9},{6,10},{7,11},{8,12},{9,13},{1... | collective-permute-start | bytes 737288 | tf_op jit(solution)/shard_map/ppermute | solution.py:287
  48.2 5.6 %collective-permute-start.10 = (bf16[4,120,256]{2,1,0:T(8,128)(2,1)S(1)}, bf16[4,120,256]{2,1,0:T(8,128)(2,1)S(1)}, u32[]{:S(2)}, u32[]{:S(2)}) collective-permute-start(bf16[4,120,256]{2,1,0:T(8,128)(2,1)S(1)} %get-tuple-element.95), channel_id=1, source_target_pairs={{0,16},{1,17},{2,18},{3,19},{4,20},{5,21},{6,22},{7,23},{8,24},{9,... | collective-permute-start | bytes 737288 | tf_op jit(solution)/shard_map/ppermute | solution.py:287
  58.8 4.6 %collective-permute-start.21 = (bf16[8,120,256]{2,1,0:T(8,128)(2,1)S(1)}, bf16[8,120,256]{2,1,0:T(8,128)(2,1)S(1)}, u32[]{:S(2)}, u32[]{:S(2)}) collective-permute-start(bf16[8,120,256]{2,1,0:T(8,128)(2,1)S(1)} %get-tuple-element.85), channel_id=1, source_target_pairs={{0,16},{1,17},{2,18},{3,19},{4,20},{5,21},{6,22},{7,23},{8,24},{9,... | collective-permute-start | bytes 1474568 | tf_op jit(solution)/shard_map/ppermute | solution.py:287
  59.5 2.1 %collective-permute-start.11 = (bf16[4,120,256]{2,1,0:T(8,128)(2,1)S(1)}, bf16[4,120,256]{2,1,0:T(8,128)(2,1)S(1)}, u32[]{:S(2)}, u32[]{:S(2)}) collective-permute-start(bf16[4,120,256]{2,1,0:T(8,128)(2,1)S(1)} %get-tuple-element.63), channel_id=1, source_target_pairs={{0,16},{1,17},{2,18},{3,19},{4,20},{5,21},{6,22},{7,23},{8,24},{9,... | collective-permute-start | bytes 737288 | tf_op jit(solution)/shard_map/ppermute | solution.py:287
  59.6 5.3 %collective-permute-start.15 = (bf16[4,120,256]{2,1,0:T(8,128)(2,1)S(1)}, bf16[4,120,256]{2,1,0:T(8,128)(2,1)S(1)}, u32[]{:S(2)}, u32[]{:S(2)}) collective-permute-start(bf16[4,120,256]{2,1,0:T(8,128)(2,1)S(1)} %get-tuple-element.66), channel_id=1, source_target_pairs={{0,4},{1,5},{2,6},{3,7},{4,8},{5,9},{6,10},{7,11},{8,12},{9,13},{1... | collective-permute-start | bytes 737288 | tf_op jit(solution)/shard_map/ppermute | solution.py:287
  61.6 8.6 %collective-permute-start.12 = (bf16[8,120,256]{2,1,0:T(8,128)(2,1)S(1)}, bf16[8,120,256]{2,1,0:T(8,128)(2,1)S(1)}, u32[]{:S(2)}, u32[]{:S(2)}) collective-permute-start(bf16[8,120,256]{2,1,0:T(8,128)(2,1)S(1)} %pad_maximum_fusion), channel_id=1, source_target_pairs={{0,4},{1,5},{2,6},{3,7},{4,8},{5,9},{6,10},{7,11},{8,12},{9,13},{1... | collective-permute-start | bytes 1474568 | tf_op jit(solution)/shard_map/ppermute | solution.py:287
  63.6 28.9 %copy-start = (f32[96,300]{1,0:T(8,128)S(1)}, f32[96,300]{1,0:T(8,128)}, u32[]{:S(2)}) copy-start(f32[96,300]{1,0:T(8,128)} %vec_ref.1) | copy-start | bytes 345604
  63.6 28.9 %copy-start.2 = (f32[96,300]{1,0:T(8,128)S(1)}, f32[96,300]{1,0:T(8,128)}, u32[]{:S(2)}) copy-start(f32[96,300]{1,0:T(8,128)} %acc_ref.1) | copy-start | bytes 345604
  63.6 28.9 %copy-start.4 = (f32[96]{0:T(128)S(1)}, f32[96]{0:T(128)}, u32[]{:S(2)}) copy-start(f32[96]{0:T(128)} %param.11) | copy-start | bytes 1156
  63.6 28.9 %copy-start.6 = (f32[96]{0:T(128)S(1)}, f32[96]{0:T(128)}, u32[]{:S(2)}) copy-start(f32[96]{0:T(128)} %param.13) | copy-start | bytes 1156
  63.6 9.3 %collective-permute-start.22 = (bf16[2,120,256]{2,1,0:T(8,128)(2,1)S(1)}, bf16[2,120,256]{2,1,0:T(8,128)(2,1)S(1)}, u32[]{:S(2)}, u32[]{:S(2)}) collective-permute-start(bf16[2,120,256]{2,1,0:T(8,128)(2,1)S(1)} %get-tuple-element.92), channel_id=1, source_target_pairs={{0,32},{1,33},{2,34},{3,35},{4,36},{5,37},{6,38},{7,39},{8,40},{9,... | collective-permute-start | bytes 368648 | tf_op jit(solution)/shard_map/ppermute | solution.py:287
  65.0 8.0 %collective-permute-start.16 = (bf16[4,120,256]{2,1,0:T(8,128)(2,1)S(1)}, bf16[4,120,256]{2,1,0:T(8,128)(2,1)S(1)}, u32[]{:S(2)}, u32[]{:S(2)}) collective-permute-start(bf16[4,120,256]{2,1,0:T(8,128)(2,1)S(1)} %collective-permute-done.15), channel_id=1, source_target_pairs={{0,4},{1,5},{2,6},{3,7},{4,8},{5,9},{6,10},{7,11},{8,12},{9,13},{1... | collective-permute-start | bytes 737288 | tf_op jit(solution)/shard_map/ppermute | solution.py:287
  70.2 3.7 %collective-permute-start.13 = (bf16[4,120,256]{2,1,0:T(8,128)(2,1)S(1)}, bf16[4,120,256]{2,1,0:T(8,128)(2,1)S(1)}, u32[]{:S(2)}, u32[]{:S(2)}) collective-permute-start(bf16[4,120,256]{2,1,0:T(8,128)(2,1)S(1)} %slice.87), channel_id=1, source_target_pairs={{0,16},{1,17},{2,18},{3,19},{4,20},{5,21},{6,22},{7,23},{8,24},{9,... | collective-permute-start | bytes 737288 | tf_op jit(solution)/shard_map/ppermute | solution.py:287
  72.8 3.9 %collective-permute-start.23 = (bf16[2,120,256]{2,1,0:T(8,128)(2,1)S(1)}, bf16[2,120,256]{2,1,0:T(8,128)(2,1)S(1)}, u32[]{:S(2)}, u32[]{:S(2)}) collective-permute-start(bf16[2,120,256]{2,1,0:T(8,128)(2,1)S(1)} %get-tuple-element.93), channel_id=1, source_target_pairs={{0,16},{1,17},{2,18},{3,19},{4,20},{5,21},{6,22},{7,23},{8,24},{9,... | collective-permute-start | bytes 368648 | tf_op jit(solution)/shard_map/ppermute | solution.py:287
  72.9 21.9 %copy-start.1 = (f32[96,300]{1,0:T(8,128)S(1)}, f32[96,300]{1,0:T(8,128)}, u32[]{:S(2)}) copy-start(f32[96,300]{1,0:T(8,128)} %rest_0_.1) | copy-start | bytes 345604
  73.0 21.9 %copy-start.3 = (f32[96,300]{1,0:T(8,128)S(1)}, f32[96,300]{1,0:T(8,128)}, u32[]{:S(2)}) copy-start(f32[96,300]{1,0:T(8,128)} %rest_2_.1) | copy-start | bytes 345604
  73.0 21.9 %copy-start.5 = (f32[96]{0:T(128)S(1)}, f32[96]{0:T(128)}, u32[]{:S(2)}) copy-start(f32[96]{0:T(128)} %param.15) | copy-start | bytes 1156
  73.0 21.9 %copy-start.7 = (f32[96]{0:T(128)S(1)}, f32[96]{0:T(128)}, u32[]{:S(2)}) copy-start(f32[96]{0:T(128)} %param.17) | copy-start | bytes 1156
  74.1 4.3 %collective-permute-start.17 = (bf16[120,256]{1,0:T(8,128)(2,1)S(1)}, bf16[120,256]{1,0:T(8,128)(2,1)S(1)}, u32[]{:S(2)}, u32[]{:S(2)}) collective-permute-start(bf16[120,256]{1,0:T(8,128)(2,1)S(1)} %get-tuple-element.69), channel_id=1, source_target_pairs={{0,1},{1,2},{2,3},{3,0},{4,5},{5,6},{6,7},{7,4},{8,9},{9,10},{10,1... | collective-permute-start | bytes 184328 | tf_op jit(solution)/shard_map/ppermute | solution.py:287
  76.8 5.4 %collective-permute-start.24 = (bf16[4,120,256]{2,1,0:T(8,128)(2,1)S(1)}, bf16[4,120,256]{2,1,0:T(8,128)(2,1)S(1)}, u32[]{:S(2)}, u32[]{:S(2)}) collective-permute-start(bf16[4,120,256]{2,1,0:T(8,128)(2,1)S(1)} %pad_maximum_fusion.3), channel_id=1, source_target_pairs={{0,32},{1,33},{2,34},{3,35},{4,36},{5,37},{6,38},{7,39},{8,40},{9,... | collective-permute-start | bytes 737288 | tf_op jit(solution)/shard_map/ppermute | solution.py:287
  77.3 1.2 %collective-permute-start.18 = (bf16[120,256]{1,0:T(8,128)(2,1)S(1)}, bf16[120,256]{1,0:T(8,128)(2,1)S(1)}, u32[]{:S(2)}, u32[]{:S(2)}) collective-permute-start(bf16[120,256]{1,0:T(8,128)(2,1)S(1)} %get-tuple-element.70), channel_id=1, source_target_pairs={{0,16},{1,17},{2,18},{3,19},{4,20},{5,21},{6,22},{7,23},{8,24},{9,... | collective-permute-start | bytes 184328 | tf_op jit(solution)/shard_map/ppermute | solution.py:287
  78.6 7.4 %collective-permute-start.19 = (bf16[2,120,256]{2,1,0:T(8,128)(2,1)S(1)}, bf16[2,120,256]{2,1,0:T(8,128)(2,1)S(1)}, u32[]{:S(2)}, u32[]{:S(2)}) collective-permute-start(bf16[2,120,256]{2,1,0:T(8,128)(2,1)S(1)} %pad_maximum_fusion.7), channel_id=1, source_target_pairs={{0,1},{1,2},{2,3},{3,0},{4,5},{5,6},{6,7},{7,4},{8,9},{9,10},{10,1... | collective-permute-start | bytes 368648 | tf_op jit(solution)/shard_map/ppermute | solution.py:287
  82.2 8.3 %collective-permute-start.25 = (bf16[2,120,256]{2,1,0:T(8,128)(2,1)S(1)}, bf16[2,120,256]{2,1,0:T(8,128)(2,1)S(1)}, u32[]{:S(2)}, u32[]{:S(2)}) collective-permute-start(bf16[2,120,256]{2,1,0:T(8,128)(2,1)S(1)} %slice.95), channel_id=1, source_target_pairs={{0,16},{1,17},{2,18},{3,19},{4,20},{5,21},{6,22},{7,23},{8,24},{9,... | collective-permute-start | bytes 368648 | tf_op jit(solution)/shard_map/ppermute | solution.py:287
  86.0 6.5 %collective-permute-start.20 = (bf16[120,256]{1,0:T(8,128)(2,1)S(1)}, bf16[120,256]{1,0:T(8,128)(2,1)S(1)}, u32[]{:S(2)}, u32[]{:S(2)}) collective-permute-start(bf16[120,256]{1,0:T(8,128)(2,1)S(1)} %slice_bitcast_fusion.1), channel_id=1, source_target_pairs={{0,16},{1,17},{2,18},{3,19},{4,20},{5,21},{6,22},{7,23},{8,24},{9,... | collective-permute-start | bytes 184328 | tf_op jit(solution)/shard_map/ppermute | solution.py:287
  90.6 4.2 %collective-permute-start.26 = (bf16[120,256]{1,0:T(8,128)(2,1)S(1)}, bf16[120,256]{1,0:T(8,128)(2,1)S(1)}, u32[]{:S(2)}, u32[]{:S(2)}) collective-permute-start(bf16[120,256]{1,0:T(8,128)(2,1)S(1)} %fusion.3), channel_id=1, source_target_pairs={{0,128},{1,129},{2,130},{3,131},{4,132},{5,133},{6,134},{7,135},{8... | collective-permute-start | bytes 184328 | tf_op jit(solution)/shard_map/ppermute | solution.py:287

commit v3 on v2

--- a/solution.py
+++ b/solution.py
@@ -17,6 +17,7 @@
 BLOCK = 120
 D = 300
 LO = 256
+USED = 320
 MIB = 1 << 20
 
 
@@ -56,7 +57,9 @@
     (0, 0, 0), (0, 0, 1), (1, 0, 0), (1, 0, 1), (0, -1, 0), (0, -1, 1), (1, -1, 0), (1, -1, 1), (0, 2, 0), (0, 2, 1),
     (1, 1, 0), (1, 1, 1), (0, 1, 0), (0, 1, 1), (1, 2, 0), (1, 2, 1),
 )
-RESULTS = tuple((d, b if d == 0 else -b, a) for d in (0, 1) for b in range(4) for a in (0, 1))
+RESULTS = tuple(
+    (d, b, a) for d, b in ((0, 0), (0, 1), (1, 1), (0, 2), (1, 0), (1, -1), (0, -1), (1, 2)) for a in (0, 1)
+)
 
 
 def pack_kernel(wv, wb, cv, cb, word_out, ctx_out, row_index, piece_index, result_index, tail_ref):
@@ -103,8 +106,9 @@
         def step(i, _):
             rows = pl.ds(pl.multiple_of(i * 8, 8), 8)
             count = held[n, rows, :]
-            log_count = jnp.log(jnp.maximum(count, 1).astype(jnp.float32))
-            power = jnp.exp(jnp.minimum(power_law * (log_count - math.log(count_cap)), 0.0))
+            log_count = jnp.log(jnp.maximum(count.astype(jnp.float32), 1.0))
+            exponent = log_count * (power_law / math.log(2.0)) - power_law * math.log2(count_cap)
+            power = jnp.exp2(jnp.minimum(exponent, 0.0))
             to = pl.ds(pl.multiple_of(n % 4 * ROWS + i * 8, 8), 8)
             weight_ref[to, :] = jnp.where(count > 0, power, 0.0)
             log_ref[to, :] = log_count
@@ -175,8 +179,8 @@
 
 def ctx_kernel(index_ref, s0, s1, s2, s3, t0, t1, t2, t3, h_own, h_other, ctx_grad, back):
     for k, (t, s) in enumerate(((t0, s0), (t1, s1), (t2, s2), (t3, s3))):
-        term = jnp.dot(t[...], s[...], preferred_element_type=jnp.float32)
-        ctx_grad[...] = term if k == 0 else ctx_grad[...] + term
+        term = jnp.dot(t[:USED, :], s[...], preferred_element_type=jnp.float32)
+        ctx_grad[:USED, :] = term if k == 0 else ctx_grad[:USED, :] + term
     back[...] = ctx_grad[...].T
     for i in range(16):
         term = back[rows_of(index_ref, i), :]
@@ -192,6 +196,11 @@
     for j, out in enumerate((own, nxt, far, back)):
         total = g0[j] + rn[j].astype(f32) + f2[j].astype(f32) + ya[j].astype(f32)
         out[...] = total.astype(out.dtype)
+
+
+def last_kernel(s, xr, x4, own, far):
+    for j, out in enumerate((own, far)):
+        out[...] = (s[j] + xr[j].astype(jnp.float32) + x4[j].astype(jnp.float32)).astype(out.dtype)
 
 
 CHUNK, COLUMNS = 4 * ROWS, 16 * ROWS
@@ -353,24 +362,27 @@
     hc = go(h_other, "core")
     ya2 = go(ya, "y")
     s = h_own + hc.astype(f32)
-    xa, x3 = go(s[4:6].astype(low), "x"), go(s[6:8].astype(low), "core")
+    xa = go(s[6:].astype(low), "x")
     f2 = go(rn[4:], "core")
     z_own, z_next, z_far, z_back = call(
         sum_kernel, (), (g0, rn, f2, ya2),
         [jax.ShapeDtypeStruct((BLOCK, LO), f32)] * 2 + [low_shape(BLOCK, LO)] * 2, [], 4 * BLOCK * LO * 4, 8,
     )
     za, f3 = go(z_far, "z"), go(z_back, "core")
-    xr = go(jnp.concatenate([(s[2:4] + xa.astype(f32)).astype(low), x3]), "x")
+    xr = go(jnp.concatenate([s[2:4] + xa.astype(f32), s[4:6]]).astype(low), "x")
     x4 = go(xr[2:], "core")
     rz = go(jnp.stack([(z_next + za.astype(f32)).astype(low), f3]), "z")
-    t = s[:2] + xr[:2].astype(f32) + x4.astype(f32)
-    rl = go(t[1].astype(low), "zl")
+    t_own, t_far = call(
+        last_kernel, (), (s, xr, x4), [jax.ShapeDtypeStruct((BLOCK, LO), f32), low_shape(BLOCK, LO)],
+        [], 4 * BLOCK * LO, 8,
+    )
+    rl = go(t_far, "zl")
     f4 = go(rz[1], "core")
 
     word_scale = 2.0 / (counts.shape[1] * lax.axis_size("ctx"))
     ctx_scale = 2.0 / (counts.shape[0] * lax.axis_size("word"))
     new_ctx_vecs, new_ctx_bias, new_ctx_accum, new_ctx_bias_accum = update(
-        t[0], rl, None, ctx_vecs, ctx_bias, ctx_accum, ctx_bias_accum, D - LO + 1, ctx_scale
+        t_own, rl, None, ctx_vecs, ctx_bias, ctx_accum, ctx_bias_accum, D - LO + 1, ctx_scale
     )
     new_word_vecs, new_word_bias, new_word_accum, new_word_bias_accum = update(
         z_own, rz, f4, word_vecs, word_bias, word_accum, word_bias_accum, D - LO, word_scale

time: 95.9 us -> 94.7 us (0.987)
    pallas_call x6 -> x7, Pallas kernels: 10.4 us -> 10.1 us  [call(): pl.pallas_call(kernel, in_specs=[SMEM_SPEC] * len(scalars) + [VMEM_SPEC]...]
    ppermute x27 -> x26, starting transfers between devices: 54.6 us -> 54.4 us  [move(): return lax.ppermute(value, ('word', 'ctx'), perm)]
    ppermute x27 -> x26, waiting for transfers between devices: 15.7 us -> 15.9 us  [move(): return lax.ppermute(value, ('word', 'ctx'), perm)]
  transfers between devices with their start and end apart: 27 -> 26, of which waited for: 13 -> 13; matrix products, arithmetic and copies ran while one was open for 1% -> 1% of each run, Pallas kernels for 17% -> 16%
where the time goes in v3:
time: 94.7 us; the launch traced here: 94.5 us
  starting transfers between devices  54.4 us (57%)
  Pallas kernels  22.7 us (24%)
  waiting for transfers between devices  15.9 us (17%)
  between operations  0.97 us (1%)
    ppermute x26, starting transfers between devices, move(): return lax.ppermute(value, ('word', 'ctx'), perm)  54.4 us
    ppermute x26, waiting for transfers between devices, move(): return lax.ppermute(value, ('word', 'ctx'), perm)  15.9 us
    pallas_call x7, Pallas kernels, call(): pl.pallas_call(kernel, in_specs=[SMEM_SPEC] * len(scalars) + [VMEM_SPEC]...  10.1 us
    pallas_call x3, Pallas kernels, weights(): pl.pallas_call(functools.partial(weight_kernel, chunks), in_specs=[pl.Blo...  9.08 us
  transfers between devices with their start and end apart: 26, of which 13 were waited for; matrix products, arithmetic and copies ran while one was open for 1% of the time, Pallas kernels for 16%

profile of v3, /device:TPU:1, one launch (start us, length us, event | category | flops | bytes accessed | tf_op | source)
XLA Modules:
  0.0 94.5 jit_solution(1319598042801366342)
XLA Ops:
  0.6 1.7 %pack.1 = (bf16[120,256]{1,0:T(8,128)(2,1)S(1)}, bf16[120,256]{1,0:T(8,128)(2,1)S(1)}, s32[16]{0:T(128)S(1)}, s32[16]{0:T(128)S(1)}, s32[16]{0:T(128)S(1)}) custom-call(f32[96,300]{1,0:T(8,128)} %vec_ref.1, f32[1,96]{1,0:T(1,128)} %bitcast.24, f32[96,300]{1,0:T(8,128)} %rest_0_.1, f32[1,96]{1,0:T(1,128)} %bitcast.26), custom_call_target="tpu_custom_call" | custom-call | flops 100000 | bytes 400000 | tf_op jit(solution)/shard_map/pack/pallas_call | solution.py:81
  2.4 3.3 %collective-permute-start = (bf16[120,256]{1,0:T(8,128)(2,1)S(1)}, bf16[120,256]{1,0:T(8,128)(2,1)S(1)}, u32[]{:S(2)}, u32[]{:S(2)}) collective-permute-start(bf16[120,256]{1,0:T(8,128)(2,1)S(1)} %get-tuple-element.51), channel_id=1, source_target_pairs={{0,16},{1,17},{2,18},{3,19},{4,20},{5,21},{6,22},{7,23},{8,24},{9,... | collective-permute-start | bytes 184328 | tf_op jit(solution)/shard_map/ppermute | solution.py:296
  5.7 0.9 collective-permute-done
  6.6 4.4 %collective-permute-start.1 = (bf16[2,120,256]{2,1,0:T(8,128)(2,1)S(1)}, bf16[2,120,256]{2,1,0:T(8,128)(2,1)S(1)}, u32[]{:S(2)}, u32[]{:S(2)}) collective-permute-start(bf16[2,120,256]{2,1,0:T(8,128)(2,1)S(1)} %pad_maximum_fusion.5), channel_id=1, source_target_pairs={{0,1},{1,2},{2,3},{3,0},{4,5},{5,6},{6,7},{7,4},{8,9},{9,10},{10,1... | collective-permute-start | bytes 368648 | tf_op jit(solution)/shard_map/ppermute | solution.py:296
  11.0 3.1 %collective-permute-done.1 = bf16[2,120,256]{2,1,0:T(8,128)(2,1)S(1)} collective-permute-done((bf16[2,120,256]{2,1,0:T(8,128)(2,1)S(1)}, bf16[2,120,256]{2,1,0:T(8,128)(2,1)S(1)}, u32[]{:S(2)}, u32[]{:S(2)}) %collective-permute-start.1) | collective-permute-done | bytes 122912 | tf_op jit(solution)/shard_map/ppermute | solution.py:296
  14.1 4.1 %collective-permute-start.2 = (bf16[1,120,256]{2,1,0:T(8,128)(2,1)S(1)}, bf16[1,120,256]{2,1,0:T(8,128)(2,1)S(1)}, u32[]{:S(2)}, u32[]{:S(2)}) collective-permute-start(bf16[1,120,256]{2,1,0:T(8,128)(2,1)S(1)} %get-tuple-element.101), channel_id=1, source_target_pairs={{0,1},{1,2},{2,3},{3,0},{4,5},{5,6},{6,7},{7,4},{8,9},{9,10},{10,1... | collective-permute-start | bytes 184328 | tf_op jit(solution)/shard_map/ppermute | solution.py:296
  18.3 1.2 %collective-permute-done.2 = bf16[1,120,256]{2,1,0:T(8,128)(2,1)S(1)} collective-permute-done((bf16[1,120,256]{2,1,0:T(8,128)(2,1)S(1)}, bf16[1,120,256]{2,1,0:T(8,128)(2,1)S(1)}, u32[]{:S(2)}, u32[]{:S(2)}) %collective-permute-start.2) | collective-permute-done | bytes 61472 | tf_op jit(solution)/shard_map/ppermute | solution.py:296
  19.5 2.1 %collective-permute-start.3 = (bf16[3,120,256]{2,1,0:T(8,128)(2,1)S(1)}, bf16[3,120,256]{2,1,0:T(8,128)(2,1)S(1)}, u32[]{:S(2)}, u32[]{:S(2)}) collective-permute-start(bf16[3,120,256]{2,1,0:T(8,128)(2,1)S(1)} %pad_maximum_fusion.4), channel_id=1, source_target_pairs={{0,16},{1,17},{2,18},{3,19},{4,20},{5,21},{6,22},{7,23},{8,24},{9,... | collective-permute-start | bytes 552968 | tf_op jit(solution)/shard_map/ppermute | solution.py:296
  21.7 2.7 %shard_map.153 = (f32[384,1536]{1,0:T(8,128)S(1)}, f32[384,1536]{1,0:T(8,128)S(1)}) custom-call(s32[16]{0:T(128)S(1)} %get-tuple-element.52.index_ref, s32[1536,1536]{1,0:T(8,128)} %counts.5), custom_call_target="tpu_custom_call" | custom-call | flops 11796480 | bytes 7077888 | tf_op jit(solution)/shard_map/pallas_call | solution.py:122
  24.4 2.7 %shard_map.152 = (f32[384,1536]{1,0:T(8,128)S(1)}, f32[384,1536]{1,0:T(8,128)S(1)}) custom-call(s32[16]{0:T(128)S(1)} %get-tuple-element.52.index_ref, s32[1536,1536]{1,0:T(8,128)} %counts.5), custom_call_target="tpu_custom_call" | custom-call | flops 11796480 | bytes 7077888 | tf_op jit(solution)/shard_map/pallas_call | solution.py:122
  27.0 3.7 %shard_map.156 = (f32[384,1536]{1,0:T(8,128)S(1)}, f32[384,1536]{1,0:T(8,128)S(1)}, f32[384,1536]{1,0:T(8,128)S(1)}, f32[384,1536]{1,0:T(8,128)S(1)}) custom-call(s32[16]{0:T(128)S(1)} %get-tuple-element.52.index_ref, s32[1536,1536]{1,0:T(8,128)} %counts.5), custom_call_target="tpu_custom_call" | custom-call | flops 23592960 | bytes 14155776 | tf_op jit(solution)/shard_map/pallas_call | solution.py:122
  30.8 2.6 %collective-permute-start.7 = (bf16[4,120,256]{2,1,0:T(8,128)(2,1)S(1)}, bf16[4,120,256]{2,1,0:T(8,128)(2,1)S(1)}, u32[]{:S(2)}, u32[]{:S(2)}) collective-permute-start(bf16[4,120,256]{2,1,0:T(8,128)(2,1)S(1)} %pad_maximum_fusion.2), channel_id=1, source_target_pairs={{0,32},{1,33},{2,34},{3,35},{4,36},{5,37},{6,38},{7,39},{8,40},{9,... | collective-permute-start | bytes 737288 | tf_op jit(solution)/shard_map/ppermute | solution.py:296
  33.5 2.8 %collective-permute-start.4 = (bf16[8,120,256]{2,1,0:T(8,128)(2,1)S(1)}, bf16[8,120,256]{2,1,0:T(8,128)(2,1)S(1)}, u32[]{:S(2)}, u32[]{:S(2)}) collective-permute-start(bf16[8,120,256]{2,1,0:T(8,128)(2,1)S(1)} %slice_dynamic-update-slice_fusion.w), channel_id=1, source_target_pairs={{0,4},{1,5},{2,6},{3,7},{4,8},{5,9},{6,10},{7,11},{8,12},{9,13},{1... | collective-permute-start | bytes 1474568 | tf_op jit(solution)/shard_map/ppermute | solution.py:296
  36.3 0.2 collective-permute-done.7
  36.6 3.5 %collective-permute-start.8 = (bf16[2,120,256]{2,1,0:T(8,128)(2,1)S(1)}, bf16[2,120,256]{2,1,0:T(8,128)(2,1)S(1)}, u32[]{:S(2)}, u32[]{:S(2)}) collective-permute-start(bf16[2,120,256]{2,1,0:T(8,128)(2,1)S(1)} %slice.68), channel_id=1, source_target_pairs={{0,32},{1,33},{2,34},{3,35},{4,36},{5,37},{6,38},{7,39},{8,40},{9,... | collective-permute-start | bytes 368648 | tf_op jit(solution)/shard_map/ppermute | solution.py:296
  40.1 1.9 %collective-permute-done.8 = bf16[2,120,256]{2,1,0:T(8,128)(2,1)S(1)} collective-permute-done((bf16[2,120,256]{2,1,0:T(8,128)(2,1)S(1)}, bf16[2,120,256]{2,1,0:T(8,128)(2,1)S(1)}, u32[]{:S(2)}, u32[]{:S(2)}) %collective-permute-start.8) | collective-permute-done | bytes 122912 | tf_op jit(solution)/shard_map/ppermute | solution.py:296
  42.0 2.7 %collective-permute-start.9 = (bf16[6,120,256]{2,1,0:T(8,128)(2,1)S(1)}, bf16[6,120,256]{2,1,0:T(8,128)(2,1)S(1)}, u32[]{:S(2)}, u32[]{:S(2)}) collective-permute-start(bf16[6,120,256]{2,1,0:T(8,128)(2,1)S(1)} %pad_maximum_fusion.1), channel_id=1, source_target_pairs={{0,16},{1,17},{2,18},{3,19},{4,20},{5,21},{6,22},{7,23},{8,24},{9,... | collective-permute-start | bytes 1105928 | tf_op jit(solution)/shard_map/ppermute | solution.py:296
  44.7 2.8 %collective-permute-start.14 = (bf16[4,120,256]{2,1,0:T(8,128)(2,1)S(1)}, bf16[4,120,256]{2,1,0:T(8,128)(2,1)S(1)}, u32[]{:S(2)}, u32[]{:S(2)}) collective-permute-start(bf16[4,120,256]{2,1,0:T(8,128)(2,1)S(1)} %get-tuple-element.98), channel_id=1, source_target_pairs={{0,4},{1,5},{2,6},{3,7},{4,8},{5,9},{6,10},{7,11},{8,12},{9,13},{1... | collective-permute-start | bytes 737288 | tf_op jit(solution)/shard_map/ppermute | solution.py:296
  47.6 0.3 collective-permute-start.10
  47.8 2.3 %shard_map.154 = (bf16[4,120,256]{2,1,0:T(8,128)(2,1)S(1)}, bf16[384,1536]{1,0:T(8,128)(2,1)S(1)}, bf16[384,384]{1,0:T(8,128)(2,1)S(1)}, bf16[1536,384]{1,0:T(8,128)(2,1)S(1)}, bf16[384,1536]{1,0:T(8,128)(2,1)S(1)}) custom-call(s32[16]{0:T(128)S(1)} %get-tuple-element.55.index_ref, bf16[8,120,256]{2,1,0:T(8,128)(2,1)S(1)} %collective-permute-done.4.w, ...), custom_call_target="tpu_custom_call" | custom-call | flops 905969664 | bytes 4194304 | tf_op jit(solution)/shard_map/pallas_call | solution.py:220
  50.1 1.5 %shard_map.155 = (f32[4,120,256]{2,1,0:T(8,128)S(1)}, bf16[384,1536]{1,0:T(8,128)(2,1)S(1)}, bf16[384,384]{1,0:T(8,128)(2,1)S(1)}) custom-call(bf16[8,120,256]{2,1,0:T(8,128)(2,1)S(1)} %slice_dynamic-update-slice_fusion.w, f32[384,1536]{1,0:T(8,128)S(1)} %get-tuple-element.53.weight, f32[384,1536]{1,0:T(8,128)S(1)} %get-tuple-element.54.log_count, ...), custom_call_target="tpu_custom_call" | custom-call | flops 905969664 | bytes 4194304 | tf_op jit(solution)/shard_map/pallas_call | solution.py:220
  51.6 1.5 %shard_map.158 = (bf16[4,120,256]{2,1,0:T(8,128)(2,1)S(1)}, bf16[384,1536]{1,0:T(8,128)(2,1)S(1)}, bf16[384,384]{1,0:T(8,128)(2,1)S(1)}) custom-call(bf16[4,120,256]{2,1,0:T(8,128)(2,1)S(1)} %collective-permute-done.14.w, f32[384,1536]{1,0:T(8,128)S(1)} %get-tuple-element.66.weight, f32[384,1536]{1,0:T(8,128)S(1)} %get-tuple-element.67.log_count, ...), custom_call_target="tpu_custom_call" | custom-call | flops 905969664 | bytes 4194304 | tf_op jit(solution)/shard_map/pallas_call | solution.py:220
  53.1 1.5 %shard_map.157 = (bf16[4,120,256]{2,1,0:T(8,128)(2,1)S(1)}, bf16[384,1536]{1,0:T(8,128)(2,1)S(1)}, bf16[384,384]{1,0:T(8,128)(2,1)S(1)}) custom-call(bf16[4,120,256]{2,1,0:T(8,128)(2,1)S(1)} %collective-permute-done.10.w, f32[384,1536]{1,0:T(8,128)S(1)} %get-tuple-element.62.weight, f32[384,1536]{1,0:T(8,128)S(1)} %get-tuple-element.63.log_count, ...), custom_call_target="tpu_custom_call" | custom-call | flops 905969664 | bytes 4194304 | tf_op jit(solution)/shard_map/pallas_call | solution.py:220
  54.6 3.2 %shard_map.161 = (f32[8,120,256]{2,1,0:T(8,128)S(1)}, bf16[8,120,256]{2,1,0:T(8,128)(2,1)S(1)}) custom-call(s32[16]{0:T(128)S(1)} %get-tuple-element.77.index_ref, bf16[384,1536]{1,0:T(8,128)(2,1)S(1)} %get-tuple-element.78.s0, bf16[384,1536]{1,0:T(8,128)(2,1)S(1)} %get-tuple-element.79.s1, bf16[384,1536]{1,0:T(8,128)(2,1)S(1)} %get-tuple-element.80.s2, ...), custom_call_target="tpu_custom_call" | custom-call | flops 1811939328 | bytes 4194304 | tf_op jit(solution)/shard_map/pallas_call | solution.py:220
  57.8 0.7 collective-permute-start.21
  58.6 2.0 %collective-permute-start.15 = (bf16[4,120,256]{2,1,0:T(8,128)(2,1)S(1)}, bf16[4,120,256]{2,1,0:T(8,128)(2,1)S(1)}, u32[]{:S(2)}, u32[]{:S(2)}) collective-permute-start(bf16[4,120,256]{2,1,0:T(8,128)(2,1)S(1)} %get-tuple-element.68), channel_id=1, source_target_pairs={{0,4},{1,5},{2,6},{3,7},{4,8},{5,9},{6,10},{7,11},{8,12},{9,13},{1... | collective-permute-start | bytes 737288 | tf_op jit(solution)/shard_map/ppermute | solution.py:296
  60.6 1.8 %collective-permute-start.12 = (bf16[8,120,256]{2,1,0:T(8,128)(2,1)S(1)}, bf16[8,120,256]{2,1,0:T(8,128)(2,1)S(1)}, u32[]{:S(2)}, u32[]{:S(2)}) collective-permute-start(bf16[8,120,256]{2,1,0:T(8,128)(2,1)S(1)} %pad_maximum_fusion), channel_id=1, source_target_pairs={{0,4},{1,5},{2,6},{3,7},{4,8},{5,9},{6,10},{7,11},{8,12},{9,13},{1... | collective-permute-start | bytes 1474568 | tf_op jit(solution)/shard_map/ppermute | solution.py:296
  62.4 0.1 fusion.2
  62.6 0.3 collective-permute-start.22
  62.9 1.0 %collective-permute-done.15 = bf16[4,120,256]{2,1,0:T(8,128)(2,1)S(1)} collective-permute-done((bf16[4,120,256]{2,1,0:T(8,128)(2,1)S(1)}, bf16[4,120,256]{2,1,0:T(8,128)(2,1)S(1)}, u32[]{:S(2)}, u32[]{:S(2)}) %collective-permute-start.15) | collective-permute-done | bytes 245792 | tf_op jit(solution)/shard_map/ppermute | solution.py:296
  64.0 2.9 %collective-permute-start.16 = (bf16[4,120,256]{2,1,0:T(8,128)(2,1)S(1)}, bf16[4,120,256]{2,1,0:T(8,128)(2,1)S(1)}, u32[]{:S(2)}, u32[]{:S(2)}) collective-permute-start(bf16[4,120,256]{2,1,0:T(8,128)(2,1)S(1)} %collective-permute-done.15), channel_id=1, source_target_pairs={{0,4},{1,5},{2,6},{3,7},{4,8},{5,9},{6,10},{7,11},{8,12},{9,13},{1... | collective-permute-start | bytes 737288 | tf_op jit(solution)/shard_map/ppermute | solution.py:296
  66.8 2.4 %collective-permute-done.12.rn = bf16[8,120,256]{2,1,0:T(8,128)(2,1)S(1)} collective-permute-done((bf16[8,120,256]{2,1,0:T(8,128)(2,1)S(1)}, bf16[8,120,256]{2,1,0:T(8,128)(2,1)S(1)}, u32[]{:S(2)}, u32[]{:S(2)}) %collective-permute-start.12) | collective-permute-done | bytes 491552 | tf_op jit(solution)/shard_map/ppermute | solution.py:296
  69.3 2.6 %collective-permute-start.13 = (bf16[4,120,256]{2,1,0:T(8,128)(2,1)S(1)}, bf16[4,120,256]{2,1,0:T(8,128)(2,1)S(1)}, u32[]{:S(2)}, u32[]{:S(2)}) collective-permute-start(bf16[4,120,256]{2,1,0:T(8,128)(2,1)S(1)} %slice.70), channel_id=1, source_target_pairs={{0,16},{1,17},{2,18},{3,19},{4,20},{5,21},{6,22},{7,23},{8,24},{9,... | collective-permute-start | bytes 737288 | tf_op jit(solution)/shard_map/ppermute | solution.py:296
  71.9 1.1 %collective-permute-done.13.f2 = bf16[4,120,256]{2,1,0:T(8,128)(2,1)S(1)} collective-permute-done((bf16[4,120,256]{2,1,0:T(8,128)(2,1)S(1)}, bf16[4,120,256]{2,1,0:T(8,128)(2,1)S(1)}, u32[]{:S(2)}, u32[]{:S(2)}) %collective-permute-start.13) | collective-permute-done | bytes 245792 | tf_op jit(solution)/shard_map/ppermute | solution.py:296
  73.0 0.1 shard_map.159
  73.1 2.4 %collective-permute-start.17 = (bf16[120,256]{1,0:T(8,128)(2,1)S(1)}, bf16[120,256]{1,0:T(8,128)(2,1)S(1)}, u32[]{:S(2)}, u32[]{:S(2)}) collective-permute-start(bf16[120,256]{1,0:T(8,128)(2,1)S(1)} %get-tuple-element.71), channel_id=1, source_target_pairs={{0,1},{1,2},{2,3},{3,0},{4,5},{5,6},{6,7},{7,4},{8,9},{9,10},{10,1... | collective-permute-start | bytes 184328 | tf_op jit(solution)/shard_map/ppermute | solution.py:296
  75.6 0.8 collective-permute-start.23
  76.4 0.8 collective-permute-done.17
  77.2 0.4 collective-permute-done.18
  77.6 3.4 %collective-permute-start.19 = (bf16[2,120,256]{2,1,0:T(8,128)(2,1)S(1)}, bf16[2,120,256]{2,1,0:T(8,128)(2,1)S(1)}, u32[]{:S(2)}, u32[]{:S(2)}) collective-permute-start(bf16[2,120,256]{2,1,0:T(8,128)(2,1)S(1)} %pad_maximum_fusion.7), channel_id=1, source_target_pairs={{0,1},{1,2},{2,3},{3,0},{4,5},{5,6},{6,7},{7,4},{8,9},{9,10},{10,1... | collective-permute-start | bytes 368648 | tf_op jit(solution)/shard_map/ppermute | solution.py:296
  81.1 0.2 collective-permute-done.23.xr
  81.2 2.5 %collective-permute-start.24 = (bf16[2,120,256]{2,1,0:T(8,128)(2,1)S(1)}, bf16[2,120,256]{2,1,0:T(8,128)(2,1)S(1)}, u32[]{:S(2)}, u32[]{:S(2)}) collective-permute-start(bf16[2,120,256]{2,1,0:T(8,128)(2,1)S(1)} %slice.76), channel_id=1, source_target_pairs={{0,16},{1,17},{2,18},{3,19},{4,20},{5,21},{6,22},{7,23},{8,24},{9,... | collective-permute-start | bytes 368648 | tf_op jit(solution)/shard_map/ppermute | solution.py:296
  83.7 1.2 %collective-permute-done.19.add_a = bf16[2,120,256]{2,1,0:T(8,128)(2,1)S(1)} collective-permute-done((bf16[2,120,256]{2,1,0:T(8,128)(2,1)S(1)}, bf16[2,120,256]{2,1,0:T(8,128)(2,1)S(1)}, u32[]{:S(2)}, u32[]{:S(2)}) %collective-permute-start.19) | collective-permute-done | bytes 122912 | tf_op jit(solution)/shard_map/ppermute | solution.py:296
  84.9 4.4 %collective-permute-start.20 = (bf16[120,256]{1,0:T(8,128)(2,1)S(1)}, bf16[120,256]{1,0:T(8,128)(2,1)S(1)}, u32[]{:S(2)}, u32[]{:S(2)}) collective-permute-start(bf16[120,256]{1,0:T(8,128)(2,1)S(1)} %slice_bitcast_fusion), channel_id=1, source_target_pairs={{0,16},{1,17},{2,18},{3,19},{4,20},{5,21},{6,22},{7,23},{8,24},{9,... | collective-permute-start | bytes 184328 | tf_op jit(solution)/shard_map/ppermute | solution.py:296
  89.4 1.9 %collective-permute-start.25 = (bf16[120,256]{1,0:T(8,128)(2,1)S(1)}, bf16[120,256]{1,0:T(8,128)(2,1)S(1)}, u32[]{:S(2)}, u32[]{:S(2)}) collective-permute-start(bf16[120,256]{1,0:T(8,128)(2,1)S(1)} %get-tuple-element.89), channel_id=1, source_target_pairs={{0,128},{1,129},{2,130},{3,131},{4,132},{5,133},{6,134},{7,135},{8... | collective-permute-start | bytes 184328 | tf_op jit(solution)/shard_map/ppermute | solution.py:296
  91.3 0.9 shard_map.160
  92.2 1.4 %collective-permute-done.25.a = bf16[120,256]{1,0:T(8,128)(2,1)S(1)} collective-permute-done((bf16[120,256]{1,0:T(8,128)(2,1)S(1)}, bf16[120,256]{1,0:T(8,128)(2,1)S(1)}, u32[]{:S(2)}, u32[]{:S(2)}) %collective-permute-start.25) | collective-permute-done | bytes 61472 | tf_op jit(solution)/shard_map/ppermute | solution.py:296
  93.6 0.9 shard_map.163
  (64 shorter events, 0.8 us)
Async XLA Ops:
  2.4 4.2 %collective-permute-start = (bf16[120,256]{1,0:T(8,128)(2,1)S(1)}, bf16[120,256]{1,0:T(8,128)(2,1)S(1)}, u32[]{:S(2)}, u32[]{:S(2)}) collective-permute-start(bf16[120,256]{1,0:T(8,128)(2,1)S(1)} %get-tuple-element.51), channel_id=1, source_target_pairs={{0,16},{1,17},{2,18},{3,19},{4,20},{5,21},{6,22},{7,23},{8,24},{9,... | collective-permute-start | bytes 184328 | tf_op jit(solution)/shard_map/ppermute | solution.py:296
  5.7 12.6 %collective-permute-start.5 = (bf16[120,256]{1,0:T(8,128)(2,1)S(1)}, bf16[120,256]{1,0:T(8,128)(2,1)S(1)}, u32[]{:S(2)}, u32[]{:S(2)}) collective-permute-start(bf16[120,256]{1,0:T(8,128)(2,1)S(1)} %get-tuple-element.56), channel_id=1, source_target_pairs={{0,128},{1,129},{2,130},{3,131},{4,132},{5,133},{6,134},{7,135},{8... | collective-permute-start | bytes 184328 | tf_op jit(solution)/shard_map/ppermute | solution.py:296
  6.6 7.5 %collective-permute-start.1 = (bf16[2,120,256]{2,1,0:T(8,128)(2,1)S(1)}, bf16[2,120,256]{2,1,0:T(8,128)(2,1)S(1)}, u32[]{:S(2)}, u32[]{:S(2)}) collective-permute-start(bf16[2,120,256]{2,1,0:T(8,128)(2,1)S(1)} %pad_maximum_fusion.5), channel_id=1, source_target_pairs={{0,1},{1,2},{2,3},{3,0},{4,5},{5,6},{6,7},{7,4},{8,9},{9,10},{10,1... | collective-permute-start | bytes 368648 | tf_op jit(solution)/shard_map/ppermute | solution.py:296
  14.1 5.4 %collective-permute-start.2 = (bf16[1,120,256]{2,1,0:T(8,128)(2,1)S(1)}, bf16[1,120,256]{2,1,0:T(8,128)(2,1)S(1)}, u32[]{:S(2)}, u32[]{:S(2)}) collective-permute-start(bf16[1,120,256]{2,1,0:T(8,128)(2,1)S(1)} %get-tuple-element.101), channel_id=1, source_target_pairs={{0,1},{1,2},{2,3},{3,0},{4,5},{5,6},{6,7},{7,4},{8,9},{9,10},{10,1... | collective-permute-start | bytes 184328 | tf_op jit(solution)/shard_map/ppermute | solution.py:296
  18.2 12.6 %collective-permute-start.6 = (bf16[2,120,256]{2,1,0:T(8,128)(2,1)S(1)}, bf16[2,120,256]{2,1,0:T(8,128)(2,1)S(1)}, u32[]{:S(2)}, u32[]{:S(2)}) collective-permute-start(bf16[2,120,256]{2,1,0:T(8,128)(2,1)S(1)} %pad_maximum_fusion.6), channel_id=1, source_target_pairs={{0,16},{1,17},{2,18},{3,19},{4,20},{5,21},{6,22},{7,23},{8,24},{9,... | collective-permute-start | bytes 368648 | tf_op jit(solution)/shard_map/ppermute | solution.py:296
  19.5 13.9 %collective-permute-start.3 = (bf16[3,120,256]{2,1,0:T(8,128)(2,1)S(1)}, bf16[3,120,256]{2,1,0:T(8,128)(2,1)S(1)}, u32[]{:S(2)}, u32[]{:S(2)}) collective-permute-start(bf16[3,120,256]{2,1,0:T(8,128)(2,1)S(1)} %pad_maximum_fusion.4), channel_id=1, source_target_pairs={{0,16},{1,17},{2,18},{3,19},{4,20},{5,21},{6,22},{7,23},{8,24},{9,... | collective-permute-start | bytes 552968 | tf_op jit(solution)/shard_map/ppermute | solution.py:296
  30.8 5.7 %collective-permute-start.7 = (bf16[4,120,256]{2,1,0:T(8,128)(2,1)S(1)}, bf16[4,120,256]{2,1,0:T(8,128)(2,1)S(1)}, u32[]{:S(2)}, u32[]{:S(2)}) collective-permute-start(bf16[4,120,256]{2,1,0:T(8,128)(2,1)S(1)} %pad_maximum_fusion.2), channel_id=1, source_target_pairs={{0,32},{1,33},{2,34},{3,35},{4,36},{5,37},{6,38},{7,39},{8,40},{9,... | collective-permute-start | bytes 737288 | tf_op jit(solution)/shard_map/ppermute | solution.py:296
  33.5 11.2 %collective-permute-start.4 = (bf16[8,120,256]{2,1,0:T(8,128)(2,1)S(1)}, bf16[8,120,256]{2,1,0:T(8,128)(2,1)S(1)}, u32[]{:S(2)}, u32[]{:S(2)}) collective-permute-start(bf16[8,120,256]{2,1,0:T(8,128)(2,1)S(1)} %slice_dynamic-update-slice_fusion.w), channel_id=1, source_target_pairs={{0,4},{1,5},{2,6},{3,7},{4,8},{5,9},{6,10},{7,11},{8,12},{9,13},{1... | collective-permute-start | bytes 1474568 | tf_op jit(solution)/shard_map/ppermute | solution.py:296
  36.6 5.4 %collective-permute-start.8 = (bf16[2,120,256]{2,1,0:T(8,128)(2,1)S(1)}, bf16[2,120,256]{2,1,0:T(8,128)(2,1)S(1)}, u32[]{:S(2)}, u32[]{:S(2)}) collective-permute-start(bf16[2,120,256]{2,1,0:T(8,128)(2,1)S(1)} %slice.68), channel_id=1, source_target_pairs={{0,32},{1,33},{2,34},{3,35},{4,36},{5,37},{6,38},{7,39},{8,40},{9,... | collective-permute-start | bytes 368648 | tf_op jit(solution)/shard_map/ppermute | solution.py:296
  42.0 5.9 %collective-permute-start.9 = (bf16[6,120,256]{2,1,0:T(8,128)(2,1)S(1)}, bf16[6,120,256]{2,1,0:T(8,128)(2,1)S(1)}, u32[]{:S(2)}, u32[]{:S(2)}) collective-permute-start(bf16[6,120,256]{2,1,0:T(8,128)(2,1)S(1)} %pad_maximum_fusion.1), channel_id=1, source_target_pairs={{0,16},{1,17},{2,18},{3,19},{4,20},{5,21},{6,22},{7,23},{8,24},{9,... | collective-permute-start | bytes 1105928 | tf_op jit(solution)/shard_map/ppermute | solution.py:296
  44.7 6.9 %collective-permute-start.14 = (bf16[4,120,256]{2,1,0:T(8,128)(2,1)S(1)}, bf16[4,120,256]{2,1,0:T(8,128)(2,1)S(1)}, u32[]{:S(2)}, u32[]{:S(2)}) collective-permute-start(bf16[4,120,256]{2,1,0:T(8,128)(2,1)S(1)} %get-tuple-element.98), channel_id=1, source_target_pairs={{0,4},{1,5},{2,6},{3,7},{4,8},{5,9},{6,10},{7,11},{8,12},{9,13},{1... | collective-permute-start | bytes 737288 | tf_op jit(solution)/shard_map/ppermute | solution.py:296
  47.6 5.6 %collective-permute-start.10 = (bf16[4,120,256]{2,1,0:T(8,128)(2,1)S(1)}, bf16[4,120,256]{2,1,0:T(8,128)(2,1)S(1)}, u32[]{:S(2)}, u32[]{:S(2)}) collective-permute-start(bf16[4,120,256]{2,1,0:T(8,128)(2,1)S(1)} %get-tuple-element.99), channel_id=1, source_target_pairs={{0,16},{1,17},{2,18},{3,19},{4,20},{5,21},{6,22},{7,23},{8,24},{9,... | collective-permute-start | bytes 737288 | tf_op jit(solution)/shard_map/ppermute | solution.py:296
  57.8 4.6 %collective-permute-start.21 = (bf16[8,120,256]{2,1,0:T(8,128)(2,1)S(1)}, bf16[8,120,256]{2,1,0:T(8,128)(2,1)S(1)}, u32[]{:S(2)}, u32[]{:S(2)}) collective-permute-start(bf16[8,120,256]{2,1,0:T(8,128)(2,1)S(1)} %get-tuple-element.87), channel_id=1, source_target_pairs={{0,16},{1,17},{2,18},{3,19},{4,20},{5,21},{6,22},{7,23},{8,24},{9,... | collective-permute-start | bytes 1474568 | tf_op jit(solution)/shard_map/ppermute | solution.py:296
  58.5 2.1 %collective-permute-start.11 = (bf16[4,120,256]{2,1,0:T(8,128)(2,1)S(1)}, bf16[4,120,256]{2,1,0:T(8,128)(2,1)S(1)}, u32[]{:S(2)}, u32[]{:S(2)}) collective-permute-start(bf16[4,120,256]{2,1,0:T(8,128)(2,1)S(1)} %get-tuple-element.65), channel_id=1, source_target_pairs={{0,16},{1,17},{2,18},{3,19},{4,20},{5,21},{6,22},{7,23},{8,24},{9,... | collective-permute-start | bytes 737288 | tf_op jit(solution)/shard_map/ppermute | solution.py:296
  58.6 5.3 %collective-permute-start.15 = (bf16[4,120,256]{2,1,0:T(8,128)(2,1)S(1)}, bf16[4,120,256]{2,1,0:T(8,128)(2,1)S(1)}, u32[]{:S(2)}, u32[]{:S(2)}) collective-permute-start(bf16[4,120,256]{2,1,0:T(8,128)(2,1)S(1)} %get-tuple-element.68), channel_id=1, source_target_pairs={{0,4},{1,5},{2,6},{3,7},{4,8},{5,9},{6,10},{7,11},{8,12},{9,13},{1... | collective-permute-start | bytes 737288 | tf_op jit(solution)/shard_map/ppermute | solution.py:296
  60.6 8.6 %collective-permute-start.12 = (bf16[8,120,256]{2,1,0:T(8,128)(2,1)S(1)}, bf16[8,120,256]{2,1,0:T(8,128)(2,1)S(1)}, u32[]{:S(2)}, u32[]{:S(2)}) collective-permute-start(bf16[8,120,256]{2,1,0:T(8,128)(2,1)S(1)} %pad_maximum_fusion), channel_id=1, source_target_pairs={{0,4},{1,5},{2,6},{3,7},{4,8},{5,9},{6,10},{7,11},{8,12},{9,13},{1... | collective-permute-start | bytes 1474568 | tf_op jit(solution)/shard_map/ppermute | solution.py:296
  62.6 9.3 %collective-permute-start.22 = (bf16[2,120,256]{2,1,0:T(8,128)(2,1)S(1)}, bf16[2,120,256]{2,1,0:T(8,128)(2,1)S(1)}, u32[]{:S(2)}, u32[]{:S(2)}) collective-permute-start(bf16[2,120,256]{2,1,0:T(8,128)(2,1)S(1)} %get-tuple-element.96), channel_id=1, source_target_pairs={{0,32},{1,33},{2,34},{3,35},{4,36},{5,37},{6,38},{7,39},{8,40},{9,... | collective-permute-start | bytes 368648 | tf_op jit(solution)/shard_map/ppermute | solution.py:296
  64.0 7.9 %collective-permute-start.16 = (bf16[4,120,256]{2,1,0:T(8,128)(2,1)S(1)}, bf16[4,120,256]{2,1,0:T(8,128)(2,1)S(1)}, u32[]{:S(2)}, u32[]{:S(2)}) collective-permute-start(bf16[4,120,256]{2,1,0:T(8,128)(2,1)S(1)} %collective-permute-done.15), channel_id=1, source_target_pairs={{0,4},{1,5},{2,6},{3,7},{4,8},{5,9},{6,10},{7,11},{8,12},{9,13},{1... | collective-permute-start | bytes 737288 | tf_op jit(solution)/shard_map/ppermute | solution.py:296
  69.2 22.0 %copy-start = (f32[96,300]{1,0:T(8,128)S(1)}, f32[96,300]{1,0:T(8,128)}, u32[]{:S(2)}) copy-start(f32[96,300]{1,0:T(8,128)} %vec_ref.1) | copy-start | bytes 345604
  69.3 22.0 %copy-start.2 = (f32[96,300]{1,0:T(8,128)S(1)}, f32[96,300]{1,0:T(8,128)}, u32[]{:S(2)}) copy-start(f32[96,300]{1,0:T(8,128)} %acc_ref.1) | copy-start | bytes 345604
  69.3 22.0 %copy-start.4 = (f32[96]{0:T(128)S(1)}, f32[96]{0:T(128)}, u32[]{:S(2)}) copy-start(f32[96]{0:T(128)} %param.11) | copy-start | bytes 1156
  69.3 22.0 %copy-start.6 = (f32[96]{0:T(128)S(1)}, f32[96]{0:T(128)}, u32[]{:S(2)}) copy-start(f32[96]{0:T(128)} %param.13) | copy-start | bytes 1156
  69.3 3.7 %collective-permute-start.13 = (bf16[4,120,256]{2,1,0:T(8,128)(2,1)S(1)}, bf16[4,120,256]{2,1,0:T(8,128)(2,1)S(1)}, u32[]{:S(2)}, u32[]{:S(2)}) collective-permute-start(bf16[4,120,256]{2,1,0:T(8,128)(2,1)S(1)} %slice.70), channel_id=1, source_target_pairs={{0,16},{1,17},{2,18},{3,19},{4,20},{5,21},{6,22},{7,23},{8,24},{9,... | collective-permute-start | bytes 737288 | tf_op jit(solution)/shard_map/ppermute | solution.py:296
  73.0 20.6 %copy-start.1 = (f32[96,300]{1,0:T(8,128)S(1)}, f32[96,300]{1,0:T(8,128)}, u32[]{:S(2)}) copy-start(f32[96,300]{1,0:T(8,128)} %rest_0_.1) | copy-start | bytes 345604
  73.0 20.6 %copy-start.3 = (f32[96,300]{1,0:T(8,128)S(1)}, f32[96,300]{1,0:T(8,128)}, u32[]{:S(2)}) copy-start(f32[96,300]{1,0:T(8,128)} %rest_2_.1) | copy-start | bytes 345604
  73.0 20.6 %copy-start.5 = (f32[96]{0:T(128)S(1)}, f32[96]{0:T(128)}, u32[]{:S(2)}) copy-start(f32[96]{0:T(128)} %param.15) | copy-start | bytes 1156
  73.0 20.6 %copy-start.7 = (f32[96]{0:T(128)S(1)}, f32[96]{0:T(128)}, u32[]{:S(2)}) copy-start(f32[96]{0:T(128)} %param.17) | copy-start | bytes 1156
  73.1 4.0 %collective-permute-start.17 = (bf16[120,256]{1,0:T(8,128)(2,1)S(1)}, bf16[120,256]{1,0:T(8,128)(2,1)S(1)}, u32[]{:S(2)}, u32[]{:S(2)}) collective-permute-start(bf16[120,256]{1,0:T(8,128)(2,1)S(1)} %get-tuple-element.71), channel_id=1, source_target_pairs={{0,1},{1,2},{2,3},{3,0},{4,5},{5,6},{6,7},{7,4},{8,9},{9,10},{10,1... | collective-permute-start | bytes 184328 | tf_op jit(solution)/shard_map/ppermute | solution.py:296
  75.6 5.6 %collective-permute-start.23 = (bf16[4,120,256]{2,1,0:T(8,128)(2,1)S(1)}, bf16[4,120,256]{2,1,0:T(8,128)(2,1)S(1)}, u32[]{:S(2)}, u32[]{:S(2)}) collective-permute-start(bf16[4,120,256]{2,1,0:T(8,128)(2,1)S(1)} %pad_maximum_fusion.3), channel_id=1, source_target_pairs={{0,32},{1,33},{2,34},{3,35},{4,36},{5,37},{6,38},{7,39},{8,40},{9,... | collective-permute-start | bytes 737288 | tf_op jit(solution)/shard_map/ppermute | solution.py:296
  76.4 1.2 %collective-permute-start.18 = (bf16[120,256]{1,0:T(8,128)(2,1)S(1)}, bf16[120,256]{1,0:T(8,128)(2,1)S(1)}, u32[]{:S(2)}, u32[]{:S(2)}) collective-permute-start(bf16[120,256]{1,0:T(8,128)(2,1)S(1)} %get-tuple-element.72), channel_id=1, source_target_pairs={{0,16},{1,17},{2,18},{3,19},{4,20},{5,21},{6,22},{7,23},{8,24},{9,... | collective-permute-start | bytes 184328 | tf_op jit(solution)/shard_map/ppermute | solution.py:296
  77.6 7.3 %collective-permute-start.19 = (bf16[2,120,256]{2,1,0:T(8,128)(2,1)S(1)}, bf16[2,120,256]{2,1,0:T(8,128)(2,1)S(1)}, u32[]{:S(2)}, u32[]{:S(2)}) collective-permute-start(bf16[2,120,256]{2,1,0:T(8,128)(2,1)S(1)} %pad_maximum_fusion.7), channel_id=1, source_target_pairs={{0,1},{1,2},{2,3},{3,0},{4,5},{5,6},{6,7},{7,4},{8,9},{9,10},{10,1... | collective-permute-start | bytes 368648 | tf_op jit(solution)/shard_map/ppermute | solution.py:296
  81.2 8.1 %collective-permute-start.24 = (bf16[2,120,256]{2,1,0:T(8,128)(2,1)S(1)}, bf16[2,120,256]{2,1,0:T(8,128)(2,1)S(1)}, u32[]{:S(2)}, u32[]{:S(2)}) collective-permute-start(bf16[2,120,256]{2,1,0:T(8,128)(2,1)S(1)} %slice.76), channel_id=1, source_target_pairs={{0,16},{1,17},{2,18},{3,19},{4,20},{5,21},{6,22},{7,23},{8,24},{9,... | collective-permute-start | bytes 368648 | tf_op jit(solution)/shard_map/ppermute | solution.py:296
  84.9 6.4 %collective-permute-start.20 = (bf16[120,256]{1,0:T(8,128)(2,1)S(1)}, bf16[120,256]{1,0:T(8,128)(2,1)S(1)}, u32[]{:S(2)}, u32[]{:S(2)}) collective-permute-start(bf16[120,256]{1,0:T(8,128)(2,1)S(1)} %slice_bitcast_fusion), channel_id=1, source_target_pairs={{0,16},{1,17},{2,18},{3,19},{4,20},{5,21},{6,22},{7,23},{8,24},{9,... | collective-permute-start | bytes 184328 | tf_op jit(solution)/shard_map/ppermute | solution.py:296
  89.4 4.2 %collective-permute-start.25 = (bf16[120,256]{1,0:T(8,128)(2,1)S(1)}, bf16[120,256]{1,0:T(8,128)(2,1)S(1)}, u32[]{:S(2)}, u32[]{:S(2)}) collective-permute-start(bf16[120,256]{1,0:T(8,128)(2,1)S(1)} %get-tuple-element.89), channel_id=1, source_target_pairs={{0,128},{1,129},{2,130},{3,131},{4,132},{5,133},{6,134},{7,135},{8... | collective-permute-start | bytes 184328 | tf_op jit(solution)/shard_map/ppermute | solution.py:296

commit v4 on v3

--- a/solution.py
+++ b/solution.py
@@ -196,6 +196,11 @@
     for j, out in enumerate((own, nxt, far, back)):
         total = g0[j] + rn[j].astype(f32) + f2[j].astype(f32) + ya[j].astype(f32)
         out[...] = total.astype(out.dtype)
+
+
+def near_kernel(s, xa, _, out):
+    for j in range(4):
+        out[j] = (s[2 + j] + xa[j].astype(jnp.float32) if j < 2 else s[2 + j]).astype(jnp.bfloat16)
 
 
 def last_kernel(s, xr, x4, own, far):
@@ -319,24 +324,26 @@
     both = jnp.stack([word_block, go(word_block, "core")])
     pair = jnp.stack([ctx_block, go(ctx_block, "zl")])
     zr1 = go(both, "z")
+    y1a = go(both, "y")
     four = jnp.concatenate([pair, go(pair, "core")])
     zr2 = go(zr1[:1], "z")
     xr1 = go(four, "x")
+    y1b = go(zr1, "y")
     e1 = go(jnp.concatenate([zr1[1:], zr1[:1], zr2]), "core")
-    wy = jnp.concatenate([both[:1], e1[:1], zr2, zr1[:1], both[1:], zr1[1:], e1[2:], e1[1:2]])
-    yr1 = go(wy, "y")
+    y1c = go(jnp.concatenate([e1, zr2]), "y")
     xr2 = go(xr1[:2], "x")
     c0 = jnp.concatenate([four, xr1, xr2])
     c1 = go(c0[4:], "core")
-    w2 = go(yr1[:4], "y")
-    w1 = go(yr1[4:], "core")
-
-    k0, l0 = keep(weights((0,), row_index, counts))
-    k3, l3 = keep(weights((3,), row_index, counts))
+    w0 = jnp.concatenate([both[:1], e1[:1], zr2, zr1[:1]])
+    w3 = jnp.concatenate([y1a[:1], y1c[:1], y1c[3:], y1b[:1]])
+    w2 = go(w3, "y")
+    w1 = go(jnp.concatenate([y1a[1:], y1b[1:], y1c[2:3], y1c[1:2]]), "core")
+
+    k0, l0, k3, l3 = keep(weights((0, 3), row_index, counts))
     k1, l1, k2, l2 = keep(weights((1, 2), row_index, counts))
     scaled_shape, words_t_shape = low_shape(CHUNK, COLUMNS), low_shape(384, CHUNK)
     g3, s3, t3, ctx_full, ctx_t = call(
-        first_kernel, (piece_index,), (yr1, c0, c1, k3, l3),
+        first_kernel, (piece_index,), (w3, c0, c1, k3, l3),
         [blocks_shape(4, low), scaled_shape, words_t_shape, low_shape(COLUMNS, 384), low_shape(384, COLUMNS)],
         WORDS_SCRATCH, CHUNK_FLOPS, 16,
     )
@@ -349,7 +356,7 @@
 
     g1, s1, t1 = chunk(w1, k1, l1, low)
     g2, s2, t2 = chunk(w2, k2, l2, low)
-    g0, s0, t0 = chunk(wy, k0, l0, f32)
+    g0, s0, t0 = chunk(w0, k0, l0, f32)
     h_own, h_other = call(
         ctx_kernel, (result_index,), (s0, s1, s2, s3, t0, t1, t2, t3),
         [blocks_shape(8, f32), blocks_shape(8, low)],
@@ -369,7 +376,8 @@
         [jax.ShapeDtypeStruct((BLOCK, LO), f32)] * 2 + [low_shape(BLOCK, LO)] * 2, [], 4 * BLOCK * LO * 4, 8,
     )
     za, f3 = go(z_far, "z"), go(z_back, "core")
-    xr = go(jnp.concatenate([s[2:4] + xa.astype(f32), s[4:6]]).astype(low), "x")
+    (near_x,) = call(near_kernel, (), (s, xa, z_back), [blocks_shape(4, low)], [], 4 * BLOCK * LO * 2, 8)
+    xr = go(near_x, "x")
     x4 = go(xr[2:], "core")
     rz = go(jnp.stack([(z_next + za.astype(f32)).astype(low), f3]), "z")
     t_own, t_far = call(

time: 94.7 us -> 91.1 us (0.962)
  starting transfers between devices: 54.4 us -> 51.6 us
  Pallas kernels: 22.7 us -> 21.1 us
    ppermute x26 -> x28, starting transfers between devices: 54.4 us -> 51.6 us  [move(): return lax.ppermute(value, ('word', 'ctx'), perm)]
    pallas_call x3 -> x2, Pallas kernels: 9.08 us -> 7.48 us  [weights(): pl.pallas_call(functools.partial(weight_kernel, chunks), in_specs=[pl.Blo...]
    ppermute x26 -> x28, waiting for transfers between devices: 15.9 us -> 16.7 us  [move(): return lax.ppermute(value, ('word', 'ctx'), perm)]
    pallas_call x7 -> x8, Pallas kernels: 10.1 us -> 10.1 us  [call(): pl.pallas_call(kernel, in_specs=[SMEM_SPEC] * len(scalars) + [VMEM_SPEC]...]
  transfers between devices with their start and end apart: 26 -> 28, of which waited for: 13 -> 8; matrix products, arithmetic and copies ran while one was open for 1% -> 1% of each run, Pallas kernels for 16% -> 20%
where the time goes in v4:
time: 91.1 us; the launch traced here: 91 us
  starting transfers between devices  51.6 us (57%)
  Pallas kernels  21.1 us (23%)
  waiting for transfers between devices  16.7 us (18%)
  between operations  1.02 us (1%)
    ppermute x28, starting transfers between devices, move(): return lax.ppermute(value, ('word', 'ctx'), perm)  51.6 us
    ppermute x28, waiting for transfers between devices, move(): return lax.ppermute(value, ('word', 'ctx'), perm)  16.7 us
    pallas_call x8, Pallas kernels, call(): pl.pallas_call(kernel, in_specs=[SMEM_SPEC] * len(scalars) + [VMEM_SPEC]...  10.1 us
    pallas_call x2, Pallas kernels, weights(): pl.pallas_call(functools.partial(weight_kernel, chunks), in_specs=[pl.Blo...  7.48 us
  transfers between devices with their start and end apart: 28, of which 8 were waited for; matrix products, arithmetic and copies ran while one was open for 1% of the time, Pallas kernels for 20%

profile of v4, /device:TPU:1, one launch (start us, length us, event | category | flops | bytes accessed | tf_op | source)
XLA Modules:
  0.0 91.0 jit_solution(10533718286568351697)
XLA Ops:
  0.6 1.7 %pack.1 = (bf16[120,256]{1,0:T(8,128)(2,1)S(1)}, bf16[120,256]{1,0:T(8,128)(2,1)S(1)}, s32[16]{0:T(128)S(1)}, s32[16]{0:T(128)S(1)}, s32[16]{0:T(128)S(1)}) custom-call(f32[96,300]{1,0:T(8,128)} %vec_ref.1, f32[1,96]{1,0:T(1,128)} %bitcast.23, f32[96,300]{1,0:T(8,128)} %rest_0_.1, f32[1,96]{1,0:T(1,128)} %bitcast.25), custom_call_target="tpu_custom_call" | custom-call | flops 100000 | bytes 400000 | tf_op jit(solution)/shard_map/pack/pallas_call | solution.py:81
  2.4 3.3 %collective-permute-start = (bf16[120,256]{1,0:T(8,128)(2,1)S(1)}, bf16[120,256]{1,0:T(8,128)(2,1)S(1)}, u32[]{:S(2)}, u32[]{:S(2)}) collective-permute-start(bf16[120,256]{1,0:T(8,128)(2,1)S(1)} %get-tuple-element.51), channel_id=1, source_target_pairs={{0,16},{1,17},{2,18},{3,19},{4,20},{5,21},{6,22},{7,23},{8,24},{9,... | collective-permute-start | bytes 184328 | tf_op jit(solution)/shard_map/ppermute | solution.py:301
  5.7 3.7 %shard_map.152 = (f32[384,1536]{1,0:T(8,128)S(1)}, f32[384,1536]{1,0:T(8,128)S(1)}, f32[384,1536]{1,0:T(8,128)S(1)}, f32[384,1536]{1,0:T(8,128)S(1)}) custom-call(s32[16]{0:T(128)S(1)} %get-tuple-element.52.index_ref, s32[1536,1536]{1,0:T(8,128)} %counts.3), custom_call_target="tpu_custom_call" | custom-call | flops 23592960 | bytes 14155776 | tf_op jit(solution)/shard_map/pallas_call | solution.py:122
  9.4 3.7 %shard_map.155 = (f32[384,1536]{1,0:T(8,128)S(1)}, f32[384,1536]{1,0:T(8,128)S(1)}, f32[384,1536]{1,0:T(8,128)S(1)}, f32[384,1536]{1,0:T(8,128)S(1)}) custom-call(s32[16]{0:T(128)S(1)} %get-tuple-element.52.index_ref, s32[1536,1536]{1,0:T(8,128)} %counts.3), custom_call_target="tpu_custom_call" | custom-call | flops 23592960 | bytes 14155776 | tf_op jit(solution)/shard_map/pallas_call | solution.py:122
  13.2 5.1 %collective-permute-start.1 = (bf16[2,120,256]{2,1,0:T(8,128)(2,1)S(1)}, bf16[2,120,256]{2,1,0:T(8,128)(2,1)S(1)}, u32[]{:S(2)}, u32[]{:S(2)}) collective-permute-start(bf16[2,120,256]{2,1,0:T(8,128)(2,1)S(1)} %pad_maximum_fusion.8), channel_id=1, source_target_pairs={{0,1},{1,2},{2,3},{3,0},{4,5},{5,6},{6,7},{7,4},{8,9},{9,10},{10,1... | collective-permute-start | bytes 368648 | tf_op jit(solution)/shard_map/ppermute | solution.py:301
  18.3 2.7 %collective-permute-start.4 = (bf16[2,120,256]{2,1,0:T(8,128)(2,1)S(1)}, bf16[2,120,256]{2,1,0:T(8,128)(2,1)S(1)}, u32[]{:S(2)}, u32[]{:S(2)}) collective-permute-start(bf16[2,120,256]{2,1,0:T(8,128)(2,1)S(1)} %pad_maximum_fusion.8), channel_id=1, source_target_pairs={{0,4},{1,5},{2,6},{3,7},{4,8},{5,9},{6,10},{7,11},{8,12},{9,13},{1... | collective-permute-start | bytes 368648 | tf_op jit(solution)/shard_map/ppermute | solution.py:301
  21.1 0.1 collective-permute-start.8
  21.2 0.3 collective-permute-done.1
  21.5 4.1 %collective-permute-start.2 = (bf16[1,120,256]{2,1,0:T(8,128)(2,1)S(1)}, bf16[1,120,256]{2,1,0:T(8,128)(2,1)S(1)}, u32[]{:S(2)}, u32[]{:S(2)}) collective-permute-start(bf16[1,120,256]{2,1,0:T(8,128)(2,1)S(1)} %get-tuple-element.103), channel_id=1, source_target_pairs={{0,1},{1,2},{2,3},{3,0},{4,5},{5,6},{6,7},{7,4},{8,9},{9,10},{10,1... | collective-permute-start | bytes 184328 | tf_op jit(solution)/shard_map/ppermute | solution.py:301
  25.6 2.6 %collective-permute-start.9 = (bf16[4,120,256]{2,1,0:T(8,128)(2,1)S(1)}, bf16[4,120,256]{2,1,0:T(8,128)(2,1)S(1)}, u32[]{:S(2)}, u32[]{:S(2)}) collective-permute-start(bf16[4,120,256]{2,1,0:T(8,128)(2,1)S(1)} %pad_maximum_fusion.5), channel_id=1, source_target_pairs={{0,32},{1,33},{2,34},{3,35},{4,36},{5,37},{6,38},{7,39},{8,40},{9,... | collective-permute-start | bytes 737288 | tf_op jit(solution)/shard_map/ppermute | solution.py:301
  28.2 2.7 %collective-permute-start.6 = (bf16[2,120,256]{2,1,0:T(8,128)(2,1)S(1)}, bf16[2,120,256]{2,1,0:T(8,128)(2,1)S(1)}, u32[]{:S(2)}, u32[]{:S(2)}) collective-permute-start(bf16[2,120,256]{2,1,0:T(8,128)(2,1)S(1)} %collective-permute-done.1), channel_id=1, source_target_pairs={{0,4},{1,5},{2,6},{3,7},{4,8},{5,9},{6,10},{7,11},{8,12},{9,13},{1... | collective-permute-start | bytes 368648 | tf_op jit(solution)/shard_map/ppermute | solution.py:301
  31.0 0.1 collective-permute-start.3
  31.1 1.7 %collective-permute-done.6 = bf16[2,120,256]{2,1,0:T(8,128)(2,1)S(1)} collective-permute-done((bf16[2,120,256]{2,1,0:T(8,128)(2,1)S(1)}, bf16[2,120,256]{2,1,0:T(8,128)(2,1)S(1)}, u32[]{:S(2)}, u32[]{:S(2)}) %collective-permute-start.6) | collective-permute-done | bytes 122912 | tf_op jit(solution)/shard_map/ppermute | solution.py:301
  32.8 1.7 %collective-permute-start.10 = (bf16[2,120,256]{2,1,0:T(8,128)(2,1)S(1)}, bf16[2,120,256]{2,1,0:T(8,128)(2,1)S(1)}, u32[]{:S(2)}, u32[]{:S(2)}) collective-permute-start(bf16[2,120,256]{2,1,0:T(8,128)(2,1)S(1)} %slice.76), channel_id=1, source_target_pairs={{0,32},{1,33},{2,34},{3,35},{4,36},{5,37},{6,38},{7,39},{8,40},{9,... | collective-permute-start | bytes 368648 | tf_op jit(solution)/shard_map/ppermute | solution.py:301
  34.5 0.1 pad_maximum_fusion.3
  34.6 2.8 %collective-permute-start.5 = (bf16[4,120,256]{2,1,0:T(8,128)(2,1)S(1)}, bf16[4,120,256]{2,1,0:T(8,128)(2,1)S(1)}, u32[]{:S(2)}, u32[]{:S(2)}) collective-permute-start(bf16[4,120,256]{2,1,0:T(8,128)(2,1)S(1)} %get-tuple-element.104), channel_id=1, source_target_pairs={{0,4},{1,5},{2,6},{3,7},{4,8},{5,9},{6,10},{7,11},{8,12},{9,13},{1... | collective-permute-start | bytes 737288 | tf_op jit(solution)/shard_map/ppermute | solution.py:301
  37.5 0.4 collective-permute-start.11
  37.9 2.6 %collective-permute-done.5 = bf16[4,120,256]{2,1,0:T(8,128)(2,1)S(1)} collective-permute-done((bf16[4,120,256]{2,1,0:T(8,128)(2,1)S(1)}, bf16[4,120,256]{2,1,0:T(8,128)(2,1)S(1)}, u32[]{:S(2)}, u32[]{:S(2)}) %collective-permute-start.5) | collective-permute-done | bytes 245792 | tf_op jit(solution)/shard_map/ppermute | solution.py:301
  40.6 0.1 collective-permute-start.12
  40.8 3.4 %collective-permute-start.16 = (bf16[4,120,256]{2,1,0:T(8,128)(2,1)S(1)}, bf16[4,120,256]{2,1,0:T(8,128)(2,1)S(1)}, u32[]{:S(2)}, u32[]{:S(2)}) collective-permute-start(bf16[4,120,256]{2,1,0:T(8,128)(2,1)S(1)} %pad_maximum_fusion.4.w), channel_id=1, source_target_pairs={{0,4},{1,5},{2,6},{3,7},{4,8},{5,9},{6,10},{7,11},{8,12},{9,13},{1... | collective-permute-start | bytes 737288 | tf_op jit(solution)/shard_map/ppermute | solution.py:301
  44.1 2.3 %shard_map.153 = (bf16[4,120,256]{2,1,0:T(8,128)(2,1)S(1)}, bf16[384,1536]{1,0:T(8,128)(2,1)S(1)}, bf16[384,384]{1,0:T(8,128)(2,1)S(1)}, bf16[1536,384]{1,0:T(8,128)(2,1)S(1)}, bf16[384,1536]{1,0:T(8,128)(2,1)S(1)}) custom-call(s32[16]{0:T(128)S(1)} %get-tuple-element.55.index_ref, bf16[4,120,256]{2,1,0:T(8,128)(2,1)S(1)} %pad_maximum_fusion.4.w, ...), custom_call_target="tpu_custom_call" | custom-call | flops 905969664 | bytes 4194304 | tf_op jit(solution)/shard_map/pallas_call | solution.py:225
  46.4 0.1 collective-permute-start.13
  46.5 1.5 %shard_map.154 = (f32[4,120,256]{2,1,0:T(8,128)S(1)}, bf16[384,1536]{1,0:T(8,128)(2,1)S(1)}, bf16[384,384]{1,0:T(8,128)(2,1)S(1)}) custom-call(bf16[4,120,256]{2,1,0:T(8,128)(2,1)S(1)} %get-tuple-element.105.w, f32[384,1536]{1,0:T(8,128)S(1)} %get-tuple-element.53.weight, f32[384,1536]{1,0:T(8,128)S(1)} %get-tuple-element.54.log_count, ...), custom_call_target="tpu_custom_call" | custom-call | flops 905969664 | bytes 4194304 | tf_op jit(solution)/shard_map/pallas_call | solution.py:225
  48.0 1.5 %shard_map.156 = (bf16[4,120,256]{2,1,0:T(8,128)(2,1)S(1)}, bf16[384,1536]{1,0:T(8,128)(2,1)S(1)}, bf16[384,384]{1,0:T(8,128)(2,1)S(1)}) custom-call(bf16[4,120,256]{2,1,0:T(8,128)(2,1)S(1)} %collective-permute-done.12.w, f32[384,1536]{1,0:T(8,128)S(1)} %get-tuple-element.62.weight, f32[384,1536]{1,0:T(8,128)S(1)} %get-tuple-element.63.log_count, ...), custom_call_target="tpu_custom_call" | custom-call | flops 905969664 | bytes 4194304 | tf_op jit(solution)/shard_map/pallas_call | solution.py:225
  49.5 1.5 %shard_map.157 = (bf16[4,120,256]{2,1,0:T(8,128)(2,1)S(1)}, bf16[384,1536]{1,0:T(8,128)(2,1)S(1)}, bf16[384,384]{1,0:T(8,128)(2,1)S(1)}) custom-call(bf16[4,120,256]{2,1,0:T(8,128)(2,1)S(1)} %collective-permute-done.16.w, f32[384,1536]{1,0:T(8,128)S(1)} %get-tuple-element.66.weight, f32[384,1536]{1,0:T(8,128)S(1)} %get-tuple-element.67.log_count, ...), custom_call_target="tpu_custom_call" | custom-call | flops 905969664 | bytes 4194304 | tf_op jit(solution)/shard_map/pallas_call | solution.py:225
  51.1 0.9 %collective-permute-start.14 = (bf16[8,120,256]{2,1,0:T(8,128)(2,1)S(1)}, bf16[8,120,256]{2,1,0:T(8,128)(2,1)S(1)}, u32[]{:S(2)}, u32[]{:S(2)}) collective-permute-start(bf16[8,120,256]{2,1,0:T(8,128)(2,1)S(1)} %pad_maximum_fusion), channel_id=1, source_target_pairs={{0,4},{1,5},{2,6},{3,7},{4,8},{5,9},{6,10},{7,11},{8,12},{9,13},{1... | collective-permute-start | bytes 1474568 | tf_op jit(solution)/shard_map/ppermute | solution.py:301
  52.0 3.2 %shard_map.160 = (f32[8,120,256]{2,1,0:T(8,128)S(1)}, bf16[8,120,256]{2,1,0:T(8,128)(2,1)S(1)}) custom-call(s32[16]{0:T(128)S(1)} %get-tuple-element.77.index_ref, bf16[384,1536]{1,0:T(8,128)(2,1)S(1)} %get-tuple-element.78.s0, bf16[384,1536]{1,0:T(8,128)(2,1)S(1)} %get-tuple-element.79.s1, bf16[384,1536]{1,0:T(8,128)(2,1)S(1)} %get-tuple-element.80.s2, ...), custom_call_target="tpu_custom_call" | custom-call | flops 1811939328 | bytes 4194304 | tf_op jit(solution)/shard_map/pallas_call | solution.py:225
  55.2 0.1 collective-permute-start.23
  55.3 2.6 %collective-permute-start.17 = (bf16[4,120,256]{2,1,0:T(8,128)(2,1)S(1)}, bf16[4,120,256]{2,1,0:T(8,128)(2,1)S(1)}, u32[]{:S(2)}, u32[]{:S(2)}) collective-permute-start(bf16[4,120,256]{2,1,0:T(8,128)(2,1)S(1)} %get-tuple-element.68), channel_id=1, source_target_pairs={{0,4},{1,5},{2,6},{3,7},{4,8},{5,9},{6,10},{7,11},{8,12},{9,13},{1... | collective-permute-start | bytes 737288 | tf_op jit(solution)/shard_map/ppermute | solution.py:301
  57.9 3.9 %collective-permute-done.17 = bf16[4,120,256]{2,1,0:T(8,128)(2,1)S(1)} collective-permute-done((bf16[4,120,256]{2,1,0:T(8,128)(2,1)S(1)}, bf16[4,120,256]{2,1,0:T(8,128)(2,1)S(1)}, u32[]{:S(2)}, u32[]{:S(2)}) %collective-permute-start.17) | collective-permute-done | bytes 245792 | tf_op jit(solution)/shard_map/ppermute | solution.py:301
  61.8 2.4 %collective-permute-start.18 = (bf16[4,120,256]{2,1,0:T(8,128)(2,1)S(1)}, bf16[4,120,256]{2,1,0:T(8,128)(2,1)S(1)}, u32[]{:S(2)}, u32[]{:S(2)}) collective-permute-start(bf16[4,120,256]{2,1,0:T(8,128)(2,1)S(1)} %collective-permute-done.17), channel_id=1, source_target_pairs={{0,4},{1,5},{2,6},{3,7},{4,8},{5,9},{6,10},{7,11},{8,12},{9,13},{1... | collective-permute-start | bytes 737288 | tf_op jit(solution)/shard_map/ppermute | solution.py:301
  64.2 0.3 collective-permute-start.15
  64.4 0.1 convert_add_fusion.s
  64.6 0.2 collective-permute-start.24
  64.7 2.5 %collective-permute-done.18.ya = bf16[4,120,256]{2,1,0:T(8,128)(2,1)S(1)} collective-permute-done((bf16[4,120,256]{2,1,0:T(8,128)(2,1)S(1)}, bf16[4,120,256]{2,1,0:T(8,128)(2,1)S(1)}, u32[]{:S(2)}, u32[]{:S(2)}) %collective-permute-start.18) | collective-permute-done | bytes 245792 | tf_op jit(solution)/shard_map/ppermute | solution.py:301
  67.3 0.1 shard_map.158
  67.5 0.7 collective-permute-start.19
  68.2 6.2 %collective-permute-start.20 = (bf16[120,256]{1,0:T(8,128)(2,1)S(1)}, bf16[120,256]{1,0:T(8,128)(2,1)S(1)}, u32[]{:S(2)}, u32[]{:S(2)}) collective-permute-start(bf16[120,256]{1,0:T(8,128)(2,1)S(1)} %get-tuple-element.72._), channel_id=1, source_target_pairs={{0,16},{1,17},{2,18},{3,19},{4,20},{5,21},{6,22},{7,23},{8,24},{9,... | collective-permute-start | bytes 184328 | tf_op jit(solution)/shard_map/ppermute | solution.py:301
  74.4 1.6 %collective-permute-start.25 = (bf16[4,120,256]{2,1,0:T(8,128)(2,1)S(1)}, bf16[4,120,256]{2,1,0:T(8,128)(2,1)S(1)}, u32[]{:S(2)}, u32[]{:S(2)}) collective-permute-start(bf16[4,120,256]{2,1,0:T(8,128)(2,1)S(1)} %shard_map.161), channel_id=1, source_target_pairs={{0,32},{1,33},{2,34},{3,35},{4,36},{5,37},{6,38},{7,39},{8,40},{9,... | collective-permute-start | bytes 737288 | tf_op jit(solution)/shard_map/ppermute | solution.py:301
  76.0 0.8 collective-permute-start.21
  76.9 3.0 %collective-permute-done.25.xr = bf16[4,120,256]{2,1,0:T(8,128)(2,1)S(1)} collective-permute-done((bf16[4,120,256]{2,1,0:T(8,128)(2,1)S(1)}, bf16[4,120,256]{2,1,0:T(8,128)(2,1)S(1)}, u32[]{:S(2)}, u32[]{:S(2)}) %collective-permute-start.25) | collective-permute-done | bytes 245792 | tf_op jit(solution)/shard_map/ppermute | solution.py:301
  79.8 2.2 %collective-permute-start.26 = (bf16[2,120,256]{2,1,0:T(8,128)(2,1)S(1)}, bf16[2,120,256]{2,1,0:T(8,128)(2,1)S(1)}, u32[]{:S(2)}, u32[]{:S(2)}) collective-permute-start(bf16[2,120,256]{2,1,0:T(8,128)(2,1)S(1)} %slice.84), channel_id=1, source_target_pairs={{0,16},{1,17},{2,18},{3,19},{4,20},{5,21},{6,22},{7,23},{8,24},{9,... | collective-permute-start | bytes 368648 | tf_op jit(solution)/shard_map/ppermute | solution.py:301
  82.0 4.4 %collective-permute-start.22 = (bf16[120,256]{1,0:T(8,128)(2,1)S(1)}, bf16[120,256]{1,0:T(8,128)(2,1)S(1)}, u32[]{:S(2)}, u32[]{:S(2)}) collective-permute-start(bf16[120,256]{1,0:T(8,128)(2,1)S(1)} %slice_bitcast_fusion), channel_id=1, source_target_pairs={{0,16},{1,17},{2,18},{3,19},{4,20},{5,21},{6,22},{7,23},{8,24},{9,... | collective-permute-start | bytes 184328 | tf_op jit(solution)/shard_map/ppermute | solution.py:301
  86.5 0.1 collective-permute-start.27
  86.6 0.7 collective-permute-done.22.add_b
  87.4 0.9 shard_map.159
  88.3 1.9 %collective-permute-done.27.a = bf16[120,256]{1,0:T(8,128)(2,1)S(1)} collective-permute-done((bf16[120,256]{1,0:T(8,128)(2,1)S(1)}, bf16[120,256]{1,0:T(8,128)(2,1)S(1)}, u32[]{:S(2)}, u32[]{:S(2)}) %collective-permute-start.27) | collective-permute-done | bytes 61472 | tf_op jit(solution)/shard_map/ppermute | solution.py:301
  90.2 0.9 shard_map.163
  (64 shorter events, 0.6 us)
Async XLA Ops:
  2.4 10.8 %collective-permute-start = (bf16[120,256]{1,0:T(8,128)(2,1)S(1)}, bf16[120,256]{1,0:T(8,128)(2,1)S(1)}, u32[]{:S(2)}, u32[]{:S(2)}) collective-permute-start(bf16[120,256]{1,0:T(8,128)(2,1)S(1)} %get-tuple-element.51), channel_id=1, source_target_pairs={{0,16},{1,17},{2,18},{3,19},{4,20},{5,21},{6,22},{7,23},{8,24},{9,... | collective-permute-start | bytes 184328 | tf_op jit(solution)/shard_map/ppermute | solution.py:301
  5.7 15.4 %collective-permute-start.7 = (bf16[120,256]{1,0:T(8,128)(2,1)S(1)}, bf16[120,256]{1,0:T(8,128)(2,1)S(1)}, u32[]{:S(2)}, u32[]{:S(2)}) collective-permute-start(bf16[120,256]{1,0:T(8,128)(2,1)S(1)} %get-tuple-element.56), channel_id=1, source_target_pairs={{0,128},{1,129},{2,130},{3,131},{4,132},{5,133},{6,134},{7,135},{8... | collective-permute-start | bytes 184328 | tf_op jit(solution)/shard_map/ppermute | solution.py:301
  13.2 8.3 %collective-permute-start.1 = (bf16[2,120,256]{2,1,0:T(8,128)(2,1)S(1)}, bf16[2,120,256]{2,1,0:T(8,128)(2,1)S(1)}, u32[]{:S(2)}, u32[]{:S(2)}) collective-permute-start(bf16[2,120,256]{2,1,0:T(8,128)(2,1)S(1)} %pad_maximum_fusion.8), channel_id=1, source_target_pairs={{0,1},{1,2},{2,3},{3,0},{4,5},{5,6},{6,7},{7,4},{8,9},{9,10},{10,1... | collective-permute-start | bytes 368648 | tf_op jit(solution)/shard_map/ppermute | solution.py:301
  18.3 12.6 %collective-permute-start.4 = (bf16[2,120,256]{2,1,0:T(8,128)(2,1)S(1)}, bf16[2,120,256]{2,1,0:T(8,128)(2,1)S(1)}, u32[]{:S(2)}, u32[]{:S(2)}) collective-permute-start(bf16[2,120,256]{2,1,0:T(8,128)(2,1)S(1)} %pad_maximum_fusion.8), channel_id=1, source_target_pairs={{0,4},{1,5},{2,6},{3,7},{4,8},{5,9},{6,10},{7,11},{8,12},{9,13},{1... | collective-permute-start | bytes 368648 | tf_op jit(solution)/shard_map/ppermute | solution.py:301
  21.1 4.5 %collective-permute-start.8 = (bf16[2,120,256]{2,1,0:T(8,128)(2,1)S(1)}, bf16[2,120,256]{2,1,0:T(8,128)(2,1)S(1)}, u32[]{:S(2)}, u32[]{:S(2)}) collective-permute-start(bf16[2,120,256]{2,1,0:T(8,128)(2,1)S(1)} %pad_maximum_fusion.9), channel_id=1, source_target_pairs={{0,16},{1,17},{2,18},{3,19},{4,20},{5,21},{6,22},{7,23},{8,24},{9,... | collective-permute-start | bytes 368648 | tf_op jit(solution)/shard_map/ppermute | solution.py:301
  21.5 9.5 %collective-permute-start.2 = (bf16[1,120,256]{2,1,0:T(8,128)(2,1)S(1)}, bf16[1,120,256]{2,1,0:T(8,128)(2,1)S(1)}, u32[]{:S(2)}, u32[]{:S(2)}) collective-permute-start(bf16[1,120,256]{2,1,0:T(8,128)(2,1)S(1)} %get-tuple-element.103), channel_id=1, source_target_pairs={{0,1},{1,2},{2,3},{3,0},{4,5},{5,6},{6,7},{7,4},{8,9},{9,10},{10,1... | collective-permute-start | bytes 184328 | tf_op jit(solution)/shard_map/ppermute | solution.py:301
  25.6 7.2 %collective-permute-start.9 = (bf16[4,120,256]{2,1,0:T(8,128)(2,1)S(1)}, bf16[4,120,256]{2,1,0:T(8,128)(2,1)S(1)}, u32[]{:S(2)}, u32[]{:S(2)}) collective-permute-start(bf16[4,120,256]{2,1,0:T(8,128)(2,1)S(1)} %pad_maximum_fusion.5), channel_id=1, source_target_pairs={{0,32},{1,33},{2,34},{3,35},{4,36},{5,37},{6,38},{7,39},{8,40},{9,... | collective-permute-start | bytes 737288 | tf_op jit(solution)/shard_map/ppermute | solution.py:301
  28.2 4.6 %collective-permute-start.6 = (bf16[2,120,256]{2,1,0:T(8,128)(2,1)S(1)}, bf16[2,120,256]{2,1,0:T(8,128)(2,1)S(1)}, u32[]{:S(2)}, u32[]{:S(2)}) collective-permute-start(bf16[2,120,256]{2,1,0:T(8,128)(2,1)S(1)} %collective-permute-done.1), channel_id=1, source_target_pairs={{0,4},{1,5},{2,6},{3,7},{4,8},{5,9},{6,10},{7,11},{8,12},{9,13},{1... | collective-permute-start | bytes 368648 | tf_op jit(solution)/shard_map/ppermute | solution.py:301
  31.0 3.5 %collective-permute-start.3 = (bf16[3,120,256]{2,1,0:T(8,128)(2,1)S(1)}, bf16[3,120,256]{2,1,0:T(8,128)(2,1)S(1)}, u32[]{:S(2)}, u32[]{:S(2)}) collective-permute-start(bf16[3,120,256]{2,1,0:T(8,128)(2,1)S(1)} %pad_maximum_fusion.7), channel_id=1, source_target_pairs={{0,16},{1,17},{2,18},{3,19},{4,20},{5,21},{6,22},{7,23},{8,24},{9,... | collective-permute-start | bytes 552968 | tf_op jit(solution)/shard_map/ppermute | solution.py:301
  32.8 4.6 %collective-permute-start.10 = (bf16[2,120,256]{2,1,0:T(8,128)(2,1)S(1)}, bf16[2,120,256]{2,1,0:T(8,128)(2,1)S(1)}, u32[]{:S(2)}, u32[]{:S(2)}) collective-permute-start(bf16[2,120,256]{2,1,0:T(8,128)(2,1)S(1)} %slice.76), channel_id=1, source_target_pairs={{0,32},{1,33},{2,34},{3,35},{4,36},{5,37},{6,38},{7,39},{8,40},{9,... | collective-permute-start | bytes 368648 | tf_op jit(solution)/shard_map/ppermute | solution.py:301
  34.6 6.0 %collective-permute-start.5 = (bf16[4,120,256]{2,1,0:T(8,128)(2,1)S(1)}, bf16[4,120,256]{2,1,0:T(8,128)(2,1)S(1)}, u32[]{:S(2)}, u32[]{:S(2)}) collective-permute-start(bf16[4,120,256]{2,1,0:T(8,128)(2,1)S(1)} %get-tuple-element.104), channel_id=1, source_target_pairs={{0,4},{1,5},{2,6},{3,7},{4,8},{5,9},{6,10},{7,11},{8,12},{9,13},{1... | collective-permute-start | bytes 737288 | tf_op jit(solution)/shard_map/ppermute | solution.py:301
  37.5 6.7 %collective-permute-start.11 = (bf16[6,120,256]{2,1,0:T(8,128)(2,1)S(1)}, bf16[6,120,256]{2,1,0:T(8,128)(2,1)S(1)}, u32[]{:S(2)}, u32[]{:S(2)}) collective-permute-start(bf16[6,120,256]{2,1,0:T(8,128)(2,1)S(1)} %pad_maximum_fusion.1), channel_id=1, source_target_pairs={{0,16},{1,17},{2,18},{3,19},{4,20},{5,21},{6,22},{7,23},{8,24},{9,... | collective-permute-start | bytes 1105928 | tf_op jit(solution)/shard_map/ppermute | solution.py:301
  40.6 7.4 %collective-permute-start.12 = (bf16[4,120,256]{2,1,0:T(8,128)(2,1)S(1)}, bf16[4,120,256]{2,1,0:T(8,128)(2,1)S(1)}, u32[]{:S(2)}, u32[]{:S(2)}) collective-permute-start(bf16[4,120,256]{2,1,0:T(8,128)(2,1)S(1)} %pad_maximum_fusion.6), channel_id=1, source_target_pairs={{0,16},{1,17},{2,18},{3,19},{4,20},{5,21},{6,22},{7,23},{8,24},{9,... | collective-permute-start | bytes 737288 | tf_op jit(solution)/shard_map/ppermute | solution.py:301
  40.8 8.7 %collective-permute-start.16 = (bf16[4,120,256]{2,1,0:T(8,128)(2,1)S(1)}, bf16[4,120,256]{2,1,0:T(8,128)(2,1)S(1)}, u32[]{:S(2)}, u32[]{:S(2)}) collective-permute-start(bf16[4,120,256]{2,1,0:T(8,128)(2,1)S(1)} %pad_maximum_fusion.4.w), channel_id=1, source_target_pairs={{0,4},{1,5},{2,6},{3,7},{4,8},{5,9},{6,10},{7,11},{8,12},{9,13},{1... | collective-permute-start | bytes 737288 | tf_op jit(solution)/shard_map/ppermute | solution.py:301
  46.4 4.6 %collective-permute-start.13 = (bf16[4,120,256]{2,1,0:T(8,128)(2,1)S(1)}, bf16[4,120,256]{2,1,0:T(8,128)(2,1)S(1)}, u32[]{:S(2)}, u32[]{:S(2)}) collective-permute-start(bf16[4,120,256]{2,1,0:T(8,128)(2,1)S(1)} %get-tuple-element.65), channel_id=1, source_target_pairs={{0,16},{1,17},{2,18},{3,19},{4,20},{5,21},{6,22},{7,23},{8,24},{9,... | collective-permute-start | bytes 737288 | tf_op jit(solution)/shard_map/ppermute | solution.py:301
  51.1 13.1 %collective-permute-start.14 = (bf16[8,120,256]{2,1,0:T(8,128)(2,1)S(1)}, bf16[8,120,256]{2,1,0:T(8,128)(2,1)S(1)}, u32[]{:S(2)}, u32[]{:S(2)}) collective-permute-start(bf16[8,120,256]{2,1,0:T(8,128)(2,1)S(1)} %pad_maximum_fusion), channel_id=1, source_target_pairs={{0,4},{1,5},{2,6},{3,7},{4,8},{5,9},{6,10},{7,11},{8,12},{9,13},{1... | collective-permute-start | bytes 1474568 | tf_op jit(solution)/shard_map/ppermute | solution.py:301
  55.2 9.2 %collective-permute-start.23 = (bf16[8,120,256]{2,1,0:T(8,128)(2,1)S(1)}, bf16[8,120,256]{2,1,0:T(8,128)(2,1)S(1)}, u32[]{:S(2)}, u32[]{:S(2)}) collective-permute-start(bf16[8,120,256]{2,1,0:T(8,128)(2,1)S(1)} %get-tuple-element.87), channel_id=1, source_target_pairs={{0,16},{1,17},{2,18},{3,19},{4,20},{5,21},{6,22},{7,23},{8,24},{9,... | collective-permute-start | bytes 1474568 | tf_op jit(solution)/shard_map/ppermute | solution.py:301
  55.3 6.5 %collective-permute-start.17 = (bf16[4,120,256]{2,1,0:T(8,128)(2,1)S(1)}, bf16[4,120,256]{2,1,0:T(8,128)(2,1)S(1)}, u32[]{:S(2)}, u32[]{:S(2)}) collective-permute-start(bf16[4,120,256]{2,1,0:T(8,128)(2,1)S(1)} %get-tuple-element.68), channel_id=1, source_target_pairs={{0,4},{1,5},{2,6},{3,7},{4,8},{5,9},{6,10},{7,11},{8,12},{9,13},{1... | collective-permute-start | bytes 737288 | tf_op jit(solution)/shard_map/ppermute | solution.py:301
  61.8 5.5 %collective-permute-start.18 = (bf16[4,120,256]{2,1,0:T(8,128)(2,1)S(1)}, bf16[4,120,256]{2,1,0:T(8,128)(2,1)S(1)}, u32[]{:S(2)}, u32[]{:S(2)}) collective-permute-start(bf16[4,120,256]{2,1,0:T(8,128)(2,1)S(1)} %collective-permute-done.17), channel_id=1, source_target_pairs={{0,4},{1,5},{2,6},{3,7},{4,8},{5,9},{6,10},{7,11},{8,12},{9,13},{1... | collective-permute-start | bytes 737288 | tf_op jit(solution)/shard_map/ppermute | solution.py:301
  64.2 3.1 %collective-permute-start.15 = (bf16[4,120,256]{2,1,0:T(8,128)(2,1)S(1)}, bf16[4,120,256]{2,1,0:T(8,128)(2,1)S(1)}, u32[]{:S(2)}, u32[]{:S(2)}) collective-permute-start(bf16[4,120,256]{2,1,0:T(8,128)(2,1)S(1)} %slice.81), channel_id=1, source_target_pairs={{0,16},{1,17},{2,18},{3,19},{4,20},{5,21},{6,22},{7,23},{8,24},{9,... | collective-permute-start | bytes 737288 | tf_op jit(solution)/shard_map/ppermute | solution.py:301
  64.6 9.8 %collective-permute-start.24 = (bf16[2,120,256]{2,1,0:T(8,128)(2,1)S(1)}, bf16[2,120,256]{2,1,0:T(8,128)(2,1)S(1)}, u32[]{:S(2)}, u32[]{:S(2)}) collective-permute-start(bf16[2,120,256]{2,1,0:T(8,128)(2,1)S(1)} %slice.87), channel_id=1, source_target_pairs={{0,32},{1,33},{2,34},{3,35},{4,36},{5,37},{6,38},{7,39},{8,40},{9,... | collective-permute-start | bytes 368648 | tf_op jit(solution)/shard_map/ppermute | solution.py:301
  67.3 20.1 %copy-start = (f32[96,300]{1,0:T(8,128)S(1)}, f32[96,300]{1,0:T(8,128)}, u32[]{:S(2)}) copy-start(f32[96,300]{1,0:T(8,128)} %vec_ref.1) | copy-start | bytes 345604
  67.3 20.1 %copy-start.2 = (f32[96,300]{1,0:T(8,128)S(1)}, f32[96,300]{1,0:T(8,128)}, u32[]{:S(2)}) copy-start(f32[96,300]{1,0:T(8,128)} %acc_ref.1) | copy-start | bytes 345604
  67.3 20.1 %copy-start.4 = (f32[96]{0:T(128)S(1)}, f32[96]{0:T(128)}, u32[]{:S(2)}) copy-start(f32[96]{0:T(128)} %param.11) | copy-start | bytes 1156
  67.3 20.1 %copy-start.6 = (f32[96]{0:T(128)S(1)}, f32[96]{0:T(128)}, u32[]{:S(2)}) copy-start(f32[96]{0:T(128)} %param.13) | copy-start | bytes 1156
  67.4 22.7 %copy-start.1 = (f32[96,300]{1,0:T(8,128)S(1)}, f32[96,300]{1,0:T(8,128)}, u32[]{:S(2)}) copy-start(f32[96,300]{1,0:T(8,128)} %rest_0_.1) | copy-start | bytes 345604
  67.4 22.7 %copy-start.3 = (f32[96,300]{1,0:T(8,128)S(1)}, f32[96,300]{1,0:T(8,128)}, u32[]{:S(2)}) copy-start(f32[96,300]{1,0:T(8,128)} %rest_2_.1) | copy-start | bytes 345604
  67.5 22.7 %copy-start.5 = (f32[96]{0:T(128)S(1)}, f32[96]{0:T(128)}, u32[]{:S(2)}) copy-start(f32[96]{0:T(128)} %param.15) | copy-start | bytes 1156
  67.5 22.7 %copy-start.7 = (f32[96]{0:T(128)S(1)}, f32[96]{0:T(128)}, u32[]{:S(2)}) copy-start(f32[96]{0:T(128)} %param.17) | copy-start | bytes 1156
  67.5 8.5 %collective-permute-start.19 = (bf16[120,256]{1,0:T(8,128)(2,1)S(1)}, bf16[120,256]{1,0:T(8,128)(2,1)S(1)}, u32[]{:S(2)}, u32[]{:S(2)}) collective-permute-start(bf16[120,256]{1,0:T(8,128)(2,1)S(1)} %get-tuple-element.71), channel_id=1, source_target_pairs={{0,1},{1,2},{2,3},{3,0},{4,5},{5,6},{6,7},{7,4},{8,9},{9,10},{10,1... | collective-permute-start | bytes 184328 | tf_op jit(solution)/shard_map/ppermute | solution.py:301
  68.2 7.8 %collective-permute-start.20 = (bf16[120,256]{1,0:T(8,128)(2,1)S(1)}, bf16[120,256]{1,0:T(8,128)(2,1)S(1)}, u32[]{:S(2)}, u32[]{:S(2)}) collective-permute-start(bf16[120,256]{1,0:T(8,128)(2,1)S(1)} %get-tuple-element.72._), channel_id=1, source_target_pairs={{0,16},{1,17},{2,18},{3,19},{4,20},{5,21},{6,22},{7,23},{8,24},{9,... | collective-permute-start | bytes 184328 | tf_op jit(solution)/shard_map/ppermute | solution.py:301
  74.4 5.4 %collective-permute-start.25 = (bf16[4,120,256]{2,1,0:T(8,128)(2,1)S(1)}, bf16[4,120,256]{2,1,0:T(8,128)(2,1)S(1)}, u32[]{:S(2)}, u32[]{:S(2)}) collective-permute-start(bf16[4,120,256]{2,1,0:T(8,128)(2,1)S(1)} %shard_map.161), channel_id=1, source_target_pairs={{0,32},{1,33},{2,34},{3,35},{4,36},{5,37},{6,38},{7,39},{8,40},{9,... | collective-permute-start | bytes 737288 | tf_op jit(solution)/shard_map/ppermute | solution.py:301
  76.0 6.0 %collective-permute-start.21 = (bf16[2,120,256]{2,1,0:T(8,128)(2,1)S(1)}, bf16[2,120,256]{2,1,0:T(8,128)(2,1)S(1)}, u32[]{:S(2)}, u32[]{:S(2)}) collective-permute-start(bf16[2,120,256]{2,1,0:T(8,128)(2,1)S(1)} %pad_maximum_fusion.10), channel_id=1, source_target_pairs={{0,1},{1,2},{2,3},{3,0},{4,5},{5,6},{6,7},{7,4},{8,9},{9,10},{10,1... | collective-permute-start | bytes 368648 | tf_op jit(solution)/shard_map/ppermute | solution.py:301
  79.8 6.6 %collective-permute-start.26 = (bf16[2,120,256]{2,1,0:T(8,128)(2,1)S(1)}, bf16[2,120,256]{2,1,0:T(8,128)(2,1)S(1)}, u32[]{:S(2)}, u32[]{:S(2)}) collective-permute-start(bf16[2,120,256]{2,1,0:T(8,128)(2,1)S(1)} %slice.84), channel_id=1, source_target_pairs={{0,16},{1,17},{2,18},{3,19},{4,20},{5,21},{6,22},{7,23},{8,24},{9,... | collective-permute-start | bytes 368648 | tf_op jit(solution)/shard_map/ppermute | solution.py:301
  82.0 5.3 %collective-permute-start.22 = (bf16[120,256]{1,0:T(8,128)(2,1)S(1)}, bf16[120,256]{1,0:T(8,128)(2,1)S(1)}, u32[]{:S(2)}, u32[]{:S(2)}) collective-permute-start(bf16[120,256]{1,0:T(8,128)(2,1)S(1)} %slice_bitcast_fusion), channel_id=1, source_target_pairs={{0,16},{1,17},{2,18},{3,19},{4,20},{5,21},{6,22},{7,23},{8,24},{9,... | collective-permute-start | bytes 184328 | tf_op jit(solution)/shard_map/ppermute | solution.py:301
  86.5 3.6 %collective-permute-start.27 = (bf16[120,256]{1,0:T(8,128)(2,1)S(1)}, bf16[120,256]{1,0:T(8,128)(2,1)S(1)}, u32[]{:S(2)}, u32[]{:S(2)}) collective-permute-start(bf16[120,256]{1,0:T(8,128)(2,1)S(1)} %get-tuple-element.89), channel_id=1, source_target_pairs={{0,128},{1,129},{2,130},{3,131},{4,132},{5,133},{6,134},{7,135},{8... | collective-permute-start | bytes 184328 | tf_op jit(solution)/shard_map/ppermute | solution.py:301

commit v5 on v4

--- a/solution.py
+++ b/solution.py
@@ -58,7 +58,7 @@
     (1, 1, 0), (1, 1, 1), (0, 1, 0), (0, 1, 1), (1, 2, 0), (1, 2, 1),
 )
 RESULTS = tuple(
-    (d, b, a) for d, b in ((0, 0), (0, 1), (1, 1), (0, 2), (1, 0), (1, -1), (0, -1), (1, 2)) for a in (0, 1)
+    (d, b, a) for d, b in ((0, 0), (0, 1), (0, -1), (0, 2), (1, 0), (1, -1), (1, 1), (1, 2)) for a in (0, 1)
 )
 
 
@@ -198,14 +198,19 @@
         out[...] = total.astype(out.dtype)
 
 
+def join_kernel(a, b, c, out):
+    for j, ref in enumerate((a, b, c)):
+        out[j] = ref[...]
+
+
 def near_kernel(s, xa, _, out):
-    for j in range(4):
-        out[j] = (s[2 + j] + xa[j].astype(jnp.float32) if j < 2 else s[2 + j]).astype(jnp.bfloat16)
-
-
-def last_kernel(s, xr, x4, own, far):
+    for j in range(2):
+        out[j] = (s[2 + j] + xa[j].astype(jnp.float32)).astype(jnp.bfloat16)
+
+
+def last_kernel(s, xr, xb, own, far):
     for j, out in enumerate((own, far)):
-        out[...] = (s[j] + xr[j].astype(jnp.float32) + x4[j].astype(jnp.float32)).astype(out.dtype)
+        out[...] = (s[j] + xr[j].astype(jnp.float32) + xb[j].astype(jnp.float32)).astype(out.dtype)
 
 
 CHUNK, COLUMNS = 4 * ROWS, 16 * ROWS
@@ -238,7 +243,7 @@
 
 
 def update_kernel(bias_lane, scale, total_ref, add_a, add_b, vec_ref, bias_ref, acc_ref, bacc_ref, nv, nb, na, nba):
-    packed = total_ref[...] + (add_a[0] if len(add_a.shape) == 3 else add_a[...]).astype(jnp.float32)
+    packed = total_ref[...] + add_a[...].astype(jnp.float32)
     if add_b is not None:
         packed = packed + add_b[...].astype(jnp.float32)
     packed = packed * scale
@@ -296,6 +301,9 @@
             "x": (zl, x + s, c, y, z),
             "y": (zl, x, c, y + s, z),
             "z": (zl, x, c, y, z + s),
+            "x back": (zl, x - s, c, y, z),
+            "z back": (zl, x, c, y, z - s),
+            "z back, core": (zl, x, c + 1, y, z - s),
         }[axis]
         perm.append((i, place(*to)))
     return lax.ppermute(value, ("word", "ctx"), perm)
@@ -323,13 +331,16 @@
 
     both = jnp.stack([word_block, go(word_block, "core")])
     pair = jnp.stack([ctx_block, go(ctx_block, "zl")])
-    zr1 = go(both, "z")
+    zr1a, zr1b = go(word_block, "z"), go(word_block, "z back, core")
+    zr1 = jnp.stack([zr1a, zr1b])
     y1a = go(both, "y")
     four = jnp.concatenate([pair, go(pair, "core")])
-    zr2 = go(zr1[:1], "z")
+    zr2 = go(zr1a, "z")
     xr1 = go(four, "x")
     y1b = go(zr1, "y")
-    e1 = go(jnp.concatenate([zr1[1:], zr1[:1], zr2]), "core")
+    (joined,) = call(join_kernel, (), (zr1b, zr1a, zr2), [blocks_shape(3, low)], [], 3 * BLOCK * LO, 4)
+    zr2 = zr2[None]
+    e1 = go(joined, "core")
     y1c = go(jnp.concatenate([e1, zr2]), "y")
     xr2 = go(xr1[:2], "x")
     c0 = jnp.concatenate([four, xr1, xr2])
@@ -369,23 +380,21 @@
     hc = go(h_other, "core")
     ya2 = go(ya, "y")
     s = h_own + hc.astype(f32)
-    xa = go(s[6:].astype(low), "x")
+    xa, xb = go(s[6:].astype(low), "x"), go(s[4:6].astype(low), "x back")
     f2 = go(rn[4:], "core")
     z_own, z_next, z_far, z_back = call(
         sum_kernel, (), (g0, rn, f2, ya2),
         [jax.ShapeDtypeStruct((BLOCK, LO), f32)] * 2 + [low_shape(BLOCK, LO)] * 2, [], 4 * BLOCK * LO * 4, 8,
     )
-    za, f3 = go(z_far, "z"), go(z_back, "core")
-    (near_x,) = call(near_kernel, (), (s, xa, z_back), [blocks_shape(4, low)], [], 4 * BLOCK * LO * 2, 8)
+    za, rzb = go(z_far, "z"), go(z_back, "z back")
+    (near_x,) = call(near_kernel, (), (s, xa, z_back), [blocks_shape(2, low)], [], 2 * BLOCK * LO * 2, 8)
     xr = go(near_x, "x")
-    x4 = go(xr[2:], "core")
-    rz = go(jnp.stack([(z_next + za.astype(f32)).astype(low), f3]), "z")
+    rza = go((z_next + za.astype(f32)).astype(low), "z")
     t_own, t_far = call(
-        last_kernel, (), (s, xr, x4), [jax.ShapeDtypeStruct((BLOCK, LO), f32), low_shape(BLOCK, LO)],
+        last_kernel, (), (s, xr, xb), [jax.ShapeDtypeStruct((BLOCK, LO), f32), low_shape(BLOCK, LO)],
         [], 4 * BLOCK * LO, 8,
     )
     rl = go(t_far, "zl")
-    f4 = go(rz[1], "core")
 
     word_scale = 2.0 / (counts.shape[1] * lax.axis_size("ctx"))
     ctx_scale = 2.0 / (counts.shape[0] * lax.axis_size("word"))
@@ -393,7 +402,7 @@
         t_own, rl, None, ctx_vecs, ctx_bias, ctx_accum, ctx_bias_accum, D - LO + 1, ctx_scale
     )
     new_word_vecs, new_word_bias, new_word_accum, new_word_bias_accum = update(
-        z_own, rz, f4, word_vecs, word_bias, word_accum, word_bias_accum, D - LO, word_scale
+        z_own, rza, rzb, word_vecs, word_bias, word_accum, word_bias_accum, D - LO, word_scale
     )
     return (
         new_word_vecs,

time: 91.1 us -> 87.8 us (0.964)
  the two profiles are of different devices: /device:TPU:1 before, /device:TPU:32 now
where the time goes in v5:
time: 87.8 us; the launch traced here: 87.7 us
  waiting for transfers between devices  37.3 us (42%)
  starting transfers between devices  27.7 us (32%)
  Pallas kernels  21.1 us (24%)
  between operations  1.02 us (1%)
    ppermute x28, waiting for transfers between devices, move(): return lax.ppermute(value, ('word', 'ctx'), perm)  37.3 us
    ppermute x28, starting transfers between devices, move(): return lax.ppermute(value, ('word', 'ctx'), perm)  27.7 us
    pallas_call x9, Pallas kernels, call(): pl.pallas_call(kernel, in_specs=[SMEM_SPEC] * len(scalars) + [VMEM_SPEC]...  10.1 us
    pallas_call x2, Pallas kernels, weights(): pl.pallas_call(functools.partial(weight_kernel, chunks), in_specs=[pl.Blo...  7.48 us
    pallas_call x2, Pallas kernels, update(): pl.pallas_call(kernel, out_shape=[jax.ShapeDtypeStruct((ROWS, D), f32), j...  1.76 us
  transfers between devices with their start and end apart: 28, of which 11 were waited for; matrix products, arithmetic and copies ran while one was open for 1% of the time, Pallas kernels for 21%

profile of v5, /device:TPU:32, one launch (start us, length us, event | category | flops | bytes accessed | tf_op | source)
XLA Modules:
  0.0 87.7 jit_solution(6130956634091612479)
XLA Ops:
  0.6 1.7 %pack.1 = (bf16[120,256]{1,0:T(8,128)(2,1)S(1)}, bf16[120,256]{1,0:T(8,128)(2,1)S(1)}, s32[16]{0:T(128)S(1)}, s32[16]{0:T(128)S(1)}, s32[16]{0:T(128)S(1)}) custom-call(f32[96,300]{1,0:T(8,128)} %vec_ref.1, f32[1,96]{1,0:T(1,128)} %bitcast.25, f32[96,300]{1,0:T(8,128)} %rest_0_.1, f32[1,96]{1,0:T(1,128)} %bitcast.27), custom_call_target="tpu_custom_call" | custom-call | flops 100000 | bytes 400000 | tf_op jit(solution)/shard_map/pack/pallas_call | solution.py:81
  2.4 3.3 %collective-permute-start.1 = (bf16[120,256]{1,0:T(8,128)(2,1)S(1)}, bf16[120,256]{1,0:T(8,128)(2,1)S(1)}, u32[]{:S(2)}, u32[]{:S(2)}) collective-permute-start(bf16[120,256]{1,0:T(8,128)(2,1)S(1)} %get-tuple-element.51), channel_id=1, source_target_pairs={{0,1},{1,2},{2,3},{3,0},{4,5},{5,6},{6,7},{7,4},{8,9},{9,10},{10,1... | collective-permute-start | bytes 184328 | tf_op jit(solution)/shard_map/ppermute | solution.py:309
  5.7 2.7 %collective-permute-start = (bf16[120,256]{1,0:T(8,128)(2,1)S(1)}, bf16[120,256]{1,0:T(8,128)(2,1)S(1)}, u32[]{:S(2)}, u32[]{:S(2)}) collective-permute-start(bf16[120,256]{1,0:T(8,128)(2,1)S(1)} %get-tuple-element.51), channel_id=1, source_target_pairs={{0,19},{1,16},{2,17},{3,18},{4,23},{5,20},{6,21},{7,22},{8,27},{9,... | collective-permute-start | bytes 184328 | tf_op jit(solution)/shard_map/ppermute | solution.py:309
  8.5 1.0 %collective-permute-start.4 = (bf16[120,256]{1,0:T(8,128)(2,1)S(1)}, bf16[120,256]{1,0:T(8,128)(2,1)S(1)}, u32[]{:S(2)}, u32[]{:S(2)}) collective-permute-start(bf16[120,256]{1,0:T(8,128)(2,1)S(1)} %get-tuple-element.51), channel_id=1, source_target_pairs={{0,16},{1,17},{2,18},{3,19},{4,20},{5,21},{6,22},{7,23},{8,24},{9,... | collective-permute-start | bytes 184328 | tf_op jit(solution)/shard_map/ppermute | solution.py:309
  9.4 1.0 %collective-permute-start.8 = (bf16[120,256]{1,0:T(8,128)(2,1)S(1)}, bf16[120,256]{1,0:T(8,128)(2,1)S(1)}, u32[]{:S(2)}, u32[]{:S(2)}) collective-permute-start(bf16[120,256]{1,0:T(8,128)(2,1)S(1)} %get-tuple-element.56), channel_id=1, source_target_pairs={{0,128},{1,129},{2,130},{3,131},{4,132},{5,133},{6,134},{7,135},{8... | collective-permute-start | bytes 184328 | tf_op jit(solution)/shard_map/ppermute | solution.py:309
  10.4 3.7 %shard_map.153 = (f32[384,1536]{1,0:T(8,128)S(1)}, f32[384,1536]{1,0:T(8,128)S(1)}, f32[384,1536]{1,0:T(8,128)S(1)}, f32[384,1536]{1,0:T(8,128)S(1)}) custom-call(s32[16]{0:T(128)S(1)} %get-tuple-element.52.index_ref, s32[1536,1536]{1,0:T(8,128)} %counts.3), custom_call_target="tpu_custom_call" | custom-call | flops 23592960 | bytes 14155776 | tf_op jit(solution)/shard_map/pallas_call | solution.py:122
  14.2 3.7 %shard_map.156 = (f32[384,1536]{1,0:T(8,128)S(1)}, f32[384,1536]{1,0:T(8,128)S(1)}, f32[384,1536]{1,0:T(8,128)S(1)}, f32[384,1536]{1,0:T(8,128)S(1)}) custom-call(s32[16]{0:T(128)S(1)} %get-tuple-element.52.index_ref, s32[1536,1536]{1,0:T(8,128)} %counts.3), custom_call_target="tpu_custom_call" | custom-call | flops 23592960 | bytes 14155776 | tf_op jit(solution)/shard_map/pallas_call | solution.py:122
  18.0 1.7 %collective-permute-start.7 = (bf16[2,120,256]{2,1,0:T(8,128)(2,1)S(1)}, bf16[2,120,256]{2,1,0:T(8,128)(2,1)S(1)}, u32[]{:S(2)}, u32[]{:S(2)}) collective-permute-start(bf16[2,120,256]{2,1,0:T(8,128)(2,1)S(1)} %pad_maximum_fusion.8), channel_id=1, source_target_pairs={{0,4},{1,5},{2,6},{3,7},{4,8},{5,9},{6,10},{7,11},{8,12},{9,13},{1... | collective-permute-start | bytes 368648 | tf_op jit(solution)/shard_map/ppermute | solution.py:309
  19.7 1.7 %collective-permute-start.5 = (bf16[2,120,256]{2,1,0:T(8,128)(2,1)S(1)}, bf16[2,120,256]{2,1,0:T(8,128)(2,1)S(1)}, u32[]{:S(2)}, u32[]{:S(2)}) collective-permute-start(bf16[2,120,256]{2,1,0:T(8,128)(2,1)S(1)} %pad_maximum_fusion.7), channel_id=1, source_target_pairs={{0,4},{1,5},{2,6},{3,7},{4,8},{5,9},{6,10},{7,11},{8,12},{9,13},{1... | collective-permute-start | bytes 368648 | tf_op jit(solution)/shard_map/ppermute | solution.py:309
  21.3 0.1 collective-permute-start.9
  21.4 1.5 %collective-permute-start.2 = (bf16[120,256]{1,0:T(8,128)(2,1)S(1)}, bf16[120,256]{1,0:T(8,128)(2,1)S(1)}, u32[]{:S(2)}, u32[]{:S(2)}) collective-permute-start(bf16[120,256]{1,0:T(8,128)(2,1)S(1)} %collective-permute-done.1.b), channel_id=1, source_target_pairs={{0,1},{1,2},{2,3},{3,0},{4,5},{5,6},{6,7},{7,4},{8,9},{9,10},{10,1... | collective-permute-start | bytes 184328 | tf_op jit(solution)/shard_map/ppermute | solution.py:309
  23.0 5.5 %collective-permute-done.2.c = bf16[120,256]{1,0:T(8,128)(2,1)S(1)} collective-permute-done((bf16[120,256]{1,0:T(8,128)(2,1)S(1)}, bf16[120,256]{1,0:T(8,128)(2,1)S(1)}, u32[]{:S(2)}, u32[]{:S(2)}) %collective-permute-start.2) | collective-permute-done | bytes 61472 | tf_op jit(solution)/shard_map/ppermute | solution.py:309
  28.5 0.1 collective-permute-start.3
  28.7 1.6 %collective-permute-start.10 = (bf16[4,120,256]{2,1,0:T(8,128)(2,1)S(1)}, bf16[4,120,256]{2,1,0:T(8,128)(2,1)S(1)}, u32[]{:S(2)}, u32[]{:S(2)}) collective-permute-start(bf16[4,120,256]{2,1,0:T(8,128)(2,1)S(1)} %pad_maximum_fusion.5), channel_id=1, source_target_pairs={{0,32},{1,33},{2,34},{3,35},{4,36},{5,37},{6,38},{7,39},{8,40},{9,... | collective-permute-start | bytes 737288 | tf_op jit(solution)/shard_map/ppermute | solution.py:309
  30.4 1.4 %collective-permute-start.6 = (bf16[4,120,256]{2,1,0:T(8,128)(2,1)S(1)}, bf16[4,120,256]{2,1,0:T(8,128)(2,1)S(1)}, u32[]{:S(2)}, u32[]{:S(2)}) collective-permute-start(bf16[4,120,256]{2,1,0:T(8,128)(2,1)S(1)} %get-tuple-element.106), channel_id=1, source_target_pairs={{0,4},{1,5},{2,6},{3,7},{4,8},{5,9},{6,10},{7,11},{8,12},{9,13},{1... | collective-permute-start | bytes 737288 | tf_op jit(solution)/shard_map/ppermute | solution.py:309
  31.7 4.4 %collective-permute-done.10 = bf16[4,120,256]{2,1,0:T(8,128)(2,1)S(1)} collective-permute-done((bf16[4,120,256]{2,1,0:T(8,128)(2,1)S(1)}, bf16[4,120,256]{2,1,0:T(8,128)(2,1)S(1)}, u32[]{:S(2)}, u32[]{:S(2)}) %collective-permute-start.10) | collective-permute-done | bytes 245792 | tf_op jit(solution)/shard_map/ppermute | solution.py:309
  36.2 0.4 collective-permute-start.11
  36.6 5.8 %collective-permute-done.11 = bf16[2,120,256]{2,1,0:T(8,128)(2,1)S(1)} collective-permute-done((bf16[2,120,256]{2,1,0:T(8,128)(2,1)S(1)}, bf16[2,120,256]{2,1,0:T(8,128)(2,1)S(1)}, u32[]{:S(2)}, u32[]{:S(2)}) %collective-permute-start.11) | collective-permute-done | bytes 122912 | tf_op jit(solution)/shard_map/ppermute | solution.py:309
  42.4 0.1 collective-permute-start.12
  42.6 0.6 collective-permute-start.13
  43.2 1.5 %collective-permute-start.17 = (bf16[4,120,256]{2,1,0:T(8,128)(2,1)S(1)}, bf16[4,120,256]{2,1,0:T(8,128)(2,1)S(1)}, u32[]{:S(2)}, u32[]{:S(2)}) collective-permute-start(bf16[4,120,256]{2,1,0:T(8,128)(2,1)S(1)} %pad_maximum_fusion.4.w), channel_id=1, source_target_pairs={{0,4},{1,5},{2,6},{3,7},{4,8},{5,9},{6,10},{7,11},{8,12},{9,13},{1... | collective-permute-start | bytes 737288 | tf_op jit(solution)/shard_map/ppermute | solution.py:309
  44.7 2.3 %shard_map.154 = (bf16[4,120,256]{2,1,0:T(8,128)(2,1)S(1)}, bf16[384,1536]{1,0:T(8,128)(2,1)S(1)}, bf16[384,384]{1,0:T(8,128)(2,1)S(1)}, bf16[1536,384]{1,0:T(8,128)(2,1)S(1)}, bf16[384,1536]{1,0:T(8,128)(2,1)S(1)}) custom-call(s32[16]{0:T(128)S(1)} %get-tuple-element.55.index_ref, bf16[4,120,256]{2,1,0:T(8,128)(2,1)S(1)} %pad_maximum_fusion.4.w, ...), custom_call_target="tpu_custom_call" | custom-call | flops 905969664 | bytes 4194304 | tf_op jit(solution)/shard_map/pallas_call | solution.py:230
  47.0 0.2 collective-permute-start.14
  47.2 1.5 %shard_map.155 = (f32[4,120,256]{2,1,0:T(8,128)S(1)}, bf16[384,1536]{1,0:T(8,128)(2,1)S(1)}, bf16[384,384]{1,0:T(8,128)(2,1)S(1)}) custom-call(bf16[4,120,256]{2,1,0:T(8,128)(2,1)S(1)} %get-tuple-element.107.w, f32[384,1536]{1,0:T(8,128)S(1)} %get-tuple-element.53.weight, f32[384,1536]{1,0:T(8,128)S(1)} %get-tuple-element.54.log_count, ...), custom_call_target="tpu_custom_call" | custom-call | flops 905969664 | bytes 4194304 | tf_op jit(solution)/shard_map/pallas_call | solution.py:230
  48.7 1.5 %shard_map.157 = (bf16[4,120,256]{2,1,0:T(8,128)(2,1)S(1)}, bf16[384,1536]{1,0:T(8,128)(2,1)S(1)}, bf16[384,384]{1,0:T(8,128)(2,1)S(1)}) custom-call(bf16[4,120,256]{2,1,0:T(8,128)(2,1)S(1)} %collective-permute-done.13.w, f32[384,1536]{1,0:T(8,128)S(1)} %get-tuple-element.62.weight, f32[384,1536]{1,0:T(8,128)S(1)} %get-tuple-element.63.log_count, ...), custom_call_target="tpu_custom_call" | custom-call | flops 905969664 | bytes 4194304 | tf_op jit(solution)/shard_map/pallas_call | solution.py:230
  50.2 0.6 collective-permute-done.17.w
  50.8 1.5 %shard_map.158 = (bf16[4,120,256]{2,1,0:T(8,128)(2,1)S(1)}, bf16[384,1536]{1,0:T(8,128)(2,1)S(1)}, bf16[384,384]{1,0:T(8,128)(2,1)S(1)}) custom-call(bf16[4,120,256]{2,1,0:T(8,128)(2,1)S(1)} %collective-permute-done.17.w, f32[384,1536]{1,0:T(8,128)S(1)} %get-tuple-element.66.weight, f32[384,1536]{1,0:T(8,128)S(1)} %get-tuple-element.67.log_count, ...), custom_call_target="tpu_custom_call" | custom-call | flops 905969664 | bytes 4194304 | tf_op jit(solution)/shard_map/pallas_call | solution.py:230
  52.3 3.2 %shard_map.161 = (f32[8,120,256]{2,1,0:T(8,128)S(1)}, bf16[8,120,256]{2,1,0:T(8,128)(2,1)S(1)}) custom-call(s32[16]{0:T(128)S(1)} %get-tuple-element.77.index_ref, bf16[384,1536]{1,0:T(8,128)(2,1)S(1)} %get-tuple-element.78.s0, bf16[384,1536]{1,0:T(8,128)(2,1)S(1)} %get-tuple-element.79.s1, bf16[384,1536]{1,0:T(8,128)(2,1)S(1)} %get-tuple-element.80.s2, ...), custom_call_target="tpu_custom_call" | custom-call | flops 1811939328 | bytes 4194304 | tf_op jit(solution)/shard_map/pallas_call | solution.py:230
  55.5 0.1 collective-permute-start.23
  55.6 0.5 collective-permute-start.18
  56.1 1.2 %collective-permute-start.15 = (bf16[8,120,256]{2,1,0:T(8,128)(2,1)S(1)}, bf16[8,120,256]{2,1,0:T(8,128)(2,1)S(1)}, u32[]{:S(2)}, u32[]{:S(2)}) collective-permute-start(bf16[8,120,256]{2,1,0:T(8,128)(2,1)S(1)} %pad_maximum_fusion), channel_id=1, source_target_pairs={{0,4},{1,5},{2,6},{3,7},{4,8},{5,9},{6,10},{7,11},{8,12},{9,13},{1... | collective-permute-start | bytes 1474568 | tf_op jit(solution)/shard_map/ppermute | solution.py:309
  57.3 5.8 %collective-permute-done.18 = bf16[4,120,256]{2,1,0:T(8,128)(2,1)S(1)} collective-permute-done((bf16[4,120,256]{2,1,0:T(8,128)(2,1)S(1)}, bf16[4,120,256]{2,1,0:T(8,128)(2,1)S(1)}, u32[]{:S(2)}, u32[]{:S(2)}) %collective-permute-start.18) | collective-permute-done | bytes 245792 | tf_op jit(solution)/shard_map/ppermute | solution.py:309
  63.1 0.2 fusion
  63.3 5.1 %collective-permute-done.15.rn = bf16[8,120,256]{2,1,0:T(8,128)(2,1)S(1)} collective-permute-done((bf16[8,120,256]{2,1,0:T(8,128)(2,1)S(1)}, bf16[8,120,256]{2,1,0:T(8,128)(2,1)S(1)}, u32[]{:S(2)}, u32[]{:S(2)}) %collective-permute-start.15) | collective-permute-done | bytes 491552 | tf_op jit(solution)/shard_map/ppermute | solution.py:309
  68.4 0.1 collective-permute-start.16
  68.6 2.3 %collective-permute-done.19.ya = bf16[4,120,256]{2,1,0:T(8,128)(2,1)S(1)} collective-permute-done((bf16[4,120,256]{2,1,0:T(8,128)(2,1)S(1)}, bf16[4,120,256]{2,1,0:T(8,128)(2,1)S(1)}, u32[]{:S(2)}, u32[]{:S(2)}) %collective-permute-start.19) | collective-permute-done | bytes 245792 | tf_op jit(solution)/shard_map/ppermute | solution.py:309
  71.0 0.1 shard_map.159
  71.1 0.3 collective-permute-start.20
  71.5 1.0 %collective-permute-start.26 = (bf16[2,120,256]{2,1,0:T(8,128)(2,1)S(1)}, bf16[2,120,256]{2,1,0:T(8,128)(2,1)S(1)}, u32[]{:S(2)}, u32[]{:S(2)}) collective-permute-start(bf16[2,120,256]{2,1,0:T(8,128)(2,1)S(1)} %get-tuple-element.96), channel_id=1, source_target_pairs={{0,96},{1,97},{2,98},{3,99},{4,100},{5,101},{6,102},{7,103},{8,104... | collective-permute-start | bytes 368648 | tf_op jit(solution)/shard_map/ppermute | solution.py:309
  72.4 3.8 %collective-permute-start.22 = (bf16[120,256]{1,0:T(8,128)(2,1)S(1)}, bf16[120,256]{1,0:T(8,128)(2,1)S(1)}, u32[]{:S(2)}, u32[]{:S(2)}) collective-permute-start(bf16[120,256]{1,0:T(8,128)(2,1)S(1)} %get-tuple-element.72._), channel_id=1, source_target_pairs={{0,3},{1,0},{2,1},{3,2},{4,7},{5,4},{6,5},{7,6},{8,11},{9,8},{10,9... | collective-permute-start | bytes 184328 | tf_op jit(solution)/shard_map/ppermute | solution.py:309
  76.3 1.2 %collective-permute-start.25 = (bf16[2,120,256]{2,1,0:T(8,128)(2,1)S(1)}, bf16[2,120,256]{2,1,0:T(8,128)(2,1)S(1)}, u32[]{:S(2)}, u32[]{:S(2)}) collective-permute-start(bf16[2,120,256]{2,1,0:T(8,128)(2,1)S(1)} %shard_map.162), channel_id=1, source_target_pairs={{0,32},{1,33},{2,34},{3,35},{4,36},{5,37},{6,38},{7,39},{8,40},{9,... | collective-permute-start | bytes 368648 | tf_op jit(solution)/shard_map/ppermute | solution.py:309
  77.5 0.9 collective-permute-done.20
  78.5 4.0 %collective-permute-done.25.xr = bf16[2,120,256]{2,1,0:T(8,128)(2,1)S(1)} collective-permute-done((bf16[2,120,256]{2,1,0:T(8,128)(2,1)S(1)}, bf16[2,120,256]{2,1,0:T(8,128)(2,1)S(1)}, u32[]{:S(2)}, u32[]{:S(2)}) %collective-permute-start.25) | collective-permute-done | bytes 122912 | tf_op jit(solution)/shard_map/ppermute | solution.py:309
  82.5 0.6 collective-permute-start.27
  83.1 1.9 %collective-permute-done.21.add_a = bf16[120,256]{1,0:T(8,128)(2,1)S(1)} collective-permute-done((bf16[120,256]{1,0:T(8,128)(2,1)S(1)}, bf16[120,256]{1,0:T(8,128)(2,1)S(1)}, u32[]{:S(2)}, u32[]{:S(2)}) %collective-permute-start.21) | collective-permute-done | bytes 61472 | tf_op jit(solution)/shard_map/ppermute | solution.py:309
  84.9 0.9 %shard_map.160 = (f32[96,300]{1,0:T(8,128)}, f32[1,96]{1,0:T(1,128)}, f32[96,300]{1,0:T(8,128)}, f32[1,96]{1,0:T(1,128)}) custom-call(f32[120,256]{1,0:T(8,128)S(1)} %get-tuple-element.69.total_ref, bf16[120,256]{1,0:T(8,128)(2,1)S(1)} %collective-permute-done.21.add_a, bf16[120,256]{1,0:T(8,128)(2,1)S(1)} %collective-permute-done.22.add_b, ...), custom_call_target="tpu_custom_call" | custom-call | flops 400000 | bytes 800000 | tf_op jit(solution)/shard_map/pallas_call | solution.py:270
  85.8 1.0 %collective-permute-done.27.a = bf16[120,256]{1,0:T(8,128)(2,1)S(1)} collective-permute-done((bf16[120,256]{1,0:T(8,128)(2,1)S(1)}, bf16[120,256]{1,0:T(8,128)(2,1)S(1)}, u32[]{:S(2)}, u32[]{:S(2)}) %collective-permute-start.27) | collective-permute-done | bytes 61472 | tf_op jit(solution)/shard_map/ppermute | solution.py:309
  86.8 0.9 shard_map.164
  (61 shorter events, 0.8 us)
Async XLA Ops:
  2.4 15.6 %collective-permute-start.1 = (bf16[120,256]{1,0:T(8,128)(2,1)S(1)}, bf16[120,256]{1,0:T(8,128)(2,1)S(1)}, u32[]{:S(2)}, u32[]{:S(2)}) collective-permute-start(bf16[120,256]{1,0:T(8,128)(2,1)S(1)} %get-tuple-element.51), channel_id=1, source_target_pairs={{0,1},{1,2},{2,3},{3,0},{4,5},{5,6},{6,7},{7,4},{8,9},{9,10},{10,1... | collective-permute-start | bytes 184328 | tf_op jit(solution)/shard_map/ppermute | solution.py:309
  5.7 12.2 %collective-permute-start = (bf16[120,256]{1,0:T(8,128)(2,1)S(1)}, bf16[120,256]{1,0:T(8,128)(2,1)S(1)}, u32[]{:S(2)}, u32[]{:S(2)}) collective-permute-start(bf16[120,256]{1,0:T(8,128)(2,1)S(1)} %get-tuple-element.51), channel_id=1, source_target_pairs={{0,19},{1,16},{2,17},{3,18},{4,23},{5,20},{6,21},{7,22},{8,27},{9,... | collective-permute-start | bytes 184328 | tf_op jit(solution)/shard_map/ppermute | solution.py:309
  8.5 11.2 %collective-permute-start.4 = (bf16[120,256]{1,0:T(8,128)(2,1)S(1)}, bf16[120,256]{1,0:T(8,128)(2,1)S(1)}, u32[]{:S(2)}, u32[]{:S(2)}) collective-permute-start(bf16[120,256]{1,0:T(8,128)(2,1)S(1)} %get-tuple-element.51), channel_id=1, source_target_pairs={{0,16},{1,17},{2,18},{3,19},{4,20},{5,21},{6,22},{7,23},{8,24},{9,... | collective-permute-start | bytes 184328 | tf_op jit(solution)/shard_map/ppermute | solution.py:309
  9.4 11.9 %collective-permute-start.8 = (bf16[120,256]{1,0:T(8,128)(2,1)S(1)}, bf16[120,256]{1,0:T(8,128)(2,1)S(1)}, u32[]{:S(2)}, u32[]{:S(2)}) collective-permute-start(bf16[120,256]{1,0:T(8,128)(2,1)S(1)} %get-tuple-element.56), channel_id=1, source_target_pairs={{0,128},{1,129},{2,130},{3,131},{4,132},{5,133},{6,134},{7,135},{8... | collective-permute-start | bytes 184328 | tf_op jit(solution)/shard_map/ppermute | solution.py:309
  18.0 12.3 %collective-permute-start.7 = (bf16[2,120,256]{2,1,0:T(8,128)(2,1)S(1)}, bf16[2,120,256]{2,1,0:T(8,128)(2,1)S(1)}, u32[]{:S(2)}, u32[]{:S(2)}) collective-permute-start(bf16[2,120,256]{2,1,0:T(8,128)(2,1)S(1)} %pad_maximum_fusion.8), channel_id=1, source_target_pairs={{0,4},{1,5},{2,6},{3,7},{4,8},{5,9},{6,10},{7,11},{8,12},{9,13},{1... | collective-permute-start | bytes 368648 | tf_op jit(solution)/shard_map/ppermute | solution.py:309
  19.7 10.6 %collective-permute-start.5 = (bf16[2,120,256]{2,1,0:T(8,128)(2,1)S(1)}, bf16[2,120,256]{2,1,0:T(8,128)(2,1)S(1)}, u32[]{:S(2)}, u32[]{:S(2)}) collective-permute-start(bf16[2,120,256]{2,1,0:T(8,128)(2,1)S(1)} %pad_maximum_fusion.7), channel_id=1, source_target_pairs={{0,4},{1,5},{2,6},{3,7},{4,8},{5,9},{6,10},{7,11},{8,12},{9,13},{1... | collective-permute-start | bytes 368648 | tf_op jit(solution)/shard_map/ppermute | solution.py:309
  21.3 7.3 %collective-permute-start.9 = (bf16[2,120,256]{2,1,0:T(8,128)(2,1)S(1)}, bf16[2,120,256]{2,1,0:T(8,128)(2,1)S(1)}, u32[]{:S(2)}, u32[]{:S(2)}) collective-permute-start(bf16[2,120,256]{2,1,0:T(8,128)(2,1)S(1)} %pad_maximum_fusion.9), channel_id=1, source_target_pairs={{0,16},{1,17},{2,18},{3,19},{4,20},{5,21},{6,22},{7,23},{8,24},{9,... | collective-permute-start | bytes 368648 | tf_op jit(solution)/shard_map/ppermute | solution.py:309
  21.4 7.1 %collective-permute-start.2 = (bf16[120,256]{1,0:T(8,128)(2,1)S(1)}, bf16[120,256]{1,0:T(8,128)(2,1)S(1)}, u32[]{:S(2)}, u32[]{:S(2)}) collective-permute-start(bf16[120,256]{1,0:T(8,128)(2,1)S(1)} %collective-permute-done.1.b), channel_id=1, source_target_pairs={{0,1},{1,2},{2,3},{3,0},{4,5},{5,6},{6,7},{7,4},{8,9},{9,10},{10,1... | collective-permute-start | bytes 184328 | tf_op jit(solution)/shard_map/ppermute | solution.py:309
  28.5 1.8 %collective-permute-start.3 = (bf16[3,120,256]{2,1,0:T(8,128)(2,1)S(1)}, bf16[3,120,256]{2,1,0:T(8,128)(2,1)S(1)}, u32[]{:S(2)}, u32[]{:S(2)}) collective-permute-start(bf16[3,120,256]{2,1,0:T(8,128)(2,1)S(1)} %shard_map.152), channel_id=1, source_target_pairs={{0,16},{1,17},{2,18},{3,19},{4,20},{5,21},{6,22},{7,23},{8,24},{9,... | collective-permute-start | bytes 552968 | tf_op jit(solution)/shard_map/ppermute | solution.py:309
  28.7 7.5 %collective-permute-start.10 = (bf16[4,120,256]{2,1,0:T(8,128)(2,1)S(1)}, bf16[4,120,256]{2,1,0:T(8,128)(2,1)S(1)}, u32[]{:S(2)}, u32[]{:S(2)}) collective-permute-start(bf16[4,120,256]{2,1,0:T(8,128)(2,1)S(1)} %pad_maximum_fusion.5), channel_id=1, source_target_pairs={{0,32},{1,33},{2,34},{3,35},{4,36},{5,37},{6,38},{7,39},{8,40},{9,... | collective-permute-start | bytes 737288 | tf_op jit(solution)/shard_map/ppermute | solution.py:309
  30.4 12.1 %collective-permute-start.6 = (bf16[4,120,256]{2,1,0:T(8,128)(2,1)S(1)}, bf16[4,120,256]{2,1,0:T(8,128)(2,1)S(1)}, u32[]{:S(2)}, u32[]{:S(2)}) collective-permute-start(bf16[4,120,256]{2,1,0:T(8,128)(2,1)S(1)} %get-tuple-element.106), channel_id=1, source_target_pairs={{0,4},{1,5},{2,6},{3,7},{4,8},{5,9},{6,10},{7,11},{8,12},{9,13},{1... | collective-permute-start | bytes 737288 | tf_op jit(solution)/shard_map/ppermute | solution.py:309
  36.2 6.2 %collective-permute-start.11 = (bf16[2,120,256]{2,1,0:T(8,128)(2,1)S(1)}, bf16[2,120,256]{2,1,0:T(8,128)(2,1)S(1)}, u32[]{:S(2)}, u32[]{:S(2)}) collective-permute-start(bf16[2,120,256]{2,1,0:T(8,128)(2,1)S(1)} %slice.61), channel_id=1, source_target_pairs={{0,32},{1,33},{2,34},{3,35},{4,36},{5,37},{6,38},{7,39},{8,40},{9,... | collective-permute-start | bytes 368648 | tf_op jit(solution)/shard_map/ppermute | solution.py:309
  42.4 2.3 %collective-permute-start.12 = (bf16[6,120,256]{2,1,0:T(8,128)(2,1)S(1)}, bf16[6,120,256]{2,1,0:T(8,128)(2,1)S(1)}, u32[]{:S(2)}, u32[]{:S(2)}) collective-permute-start(bf16[6,120,256]{2,1,0:T(8,128)(2,1)S(1)} %pad_maximum_fusion.1), channel_id=1, source_target_pairs={{0,16},{1,17},{2,18},{3,19},{4,20},{5,21},{6,22},{7,23},{8,24},{9,... | collective-permute-start | bytes 1105928 | tf_op jit(solution)/shard_map/ppermute | solution.py:309
  42.6 6.1 %collective-permute-start.13 = (bf16[4,120,256]{2,1,0:T(8,128)(2,1)S(1)}, bf16[4,120,256]{2,1,0:T(8,128)(2,1)S(1)}, u32[]{:S(2)}, u32[]{:S(2)}) collective-permute-start(bf16[4,120,256]{2,1,0:T(8,128)(2,1)S(1)} %pad_maximum_fusion.6), channel_id=1, source_target_pairs={{0,16},{1,17},{2,18},{3,19},{4,20},{5,21},{6,22},{7,23},{8,24},{9,... | collective-permute-start | bytes 737288 | tf_op jit(solution)/shard_map/ppermute | solution.py:309
  43.2 7.7 %collective-permute-start.17 = (bf16[4,120,256]{2,1,0:T(8,128)(2,1)S(1)}, bf16[4,120,256]{2,1,0:T(8,128)(2,1)S(1)}, u32[]{:S(2)}, u32[]{:S(2)}) collective-permute-start(bf16[4,120,256]{2,1,0:T(8,128)(2,1)S(1)} %pad_maximum_fusion.4.w), channel_id=1, source_target_pairs={{0,4},{1,5},{2,6},{3,7},{4,8},{5,9},{6,10},{7,11},{8,12},{9,13},{1... | collective-permute-start | bytes 737288 | tf_op jit(solution)/shard_map/ppermute | solution.py:309
  47.0 9.1 %collective-permute-start.14 = (bf16[4,120,256]{2,1,0:T(8,128)(2,1)S(1)}, bf16[4,120,256]{2,1,0:T(8,128)(2,1)S(1)}, u32[]{:S(2)}, u32[]{:S(2)}) collective-permute-start(bf16[4,120,256]{2,1,0:T(8,128)(2,1)S(1)} %get-tuple-element.65), channel_id=1, source_target_pairs={{0,16},{1,17},{2,18},{3,19},{4,20},{5,21},{6,22},{7,23},{8,24},{9,... | collective-permute-start | bytes 737288 | tf_op jit(solution)/shard_map/ppermute | solution.py:309
  55.5 7.6 %collective-permute-start.23 = (bf16[8,120,256]{2,1,0:T(8,128)(2,1)S(1)}, bf16[8,120,256]{2,1,0:T(8,128)(2,1)S(1)}, u32[]{:S(2)}, u32[]{:S(2)}) collective-permute-start(bf16[8,120,256]{2,1,0:T(8,128)(2,1)S(1)} %get-tuple-element.87), channel_id=1, source_target_pairs={{0,16},{1,17},{2,18},{3,19},{4,20},{5,21},{6,22},{7,23},{8,24},{9,... | collective-permute-start | bytes 1474568 | tf_op jit(solution)/shard_map/ppermute | solution.py:309
  55.6 7.5 %collective-permute-start.18 = (bf16[4,120,256]{2,1,0:T(8,128)(2,1)S(1)}, bf16[4,120,256]{2,1,0:T(8,128)(2,1)S(1)}, u32[]{:S(2)}, u32[]{:S(2)}) collective-permute-start(bf16[4,120,256]{2,1,0:T(8,128)(2,1)S(1)} %get-tuple-element.68), channel_id=1, source_target_pairs={{0,4},{1,5},{2,6},{3,7},{4,8},{5,9},{6,10},{7,11},{8,12},{9,13},{1... | collective-permute-start | bytes 737288 | tf_op jit(solution)/shard_map/ppermute | solution.py:309
  56.1 12.2 %collective-permute-start.15 = (bf16[8,120,256]{2,1,0:T(8,128)(2,1)S(1)}, bf16[8,120,256]{2,1,0:T(8,128)(2,1)S(1)}, u32[]{:S(2)}, u32[]{:S(2)}) collective-permute-start(bf16[8,120,256]{2,1,0:T(8,128)(2,1)S(1)} %pad_maximum_fusion), channel_id=1, source_target_pairs={{0,4},{1,5},{2,6},{3,7},{4,8},{5,9},{6,10},{7,11},{8,12},{9,13},{1... | collective-permute-start | bytes 1474568 | tf_op jit(solution)/shard_map/ppermute | solution.py:309
  63.1 7.9 %collective-permute-start.19 = (bf16[4,120,256]{2,1,0:T(8,128)(2,1)S(1)}, bf16[4,120,256]{2,1,0:T(8,128)(2,1)S(1)}, u32[]{:S(2)}, u32[]{:S(2)}) collective-permute-start(bf16[4,120,256]{2,1,0:T(8,128)(2,1)S(1)} %collective-permute-done.18), channel_id=1, source_target_pairs={{0,4},{1,5},{2,6},{3,7},{4,8},{5,9},{6,10},{7,11},{8,12},{9,13},{1... | collective-permute-start | bytes 737288 | tf_op jit(solution)/shard_map/ppermute | solution.py:309
  68.4 2.6 %collective-permute-start.16 = (bf16[4,120,256]{2,1,0:T(8,128)(2,1)S(1)}, bf16[4,120,256]{2,1,0:T(8,128)(2,1)S(1)}, u32[]{:S(2)}, u32[]{:S(2)}) collective-permute-start(bf16[4,120,256]{2,1,0:T(8,128)(2,1)S(1)} %slice.66), channel_id=1, source_target_pairs={{0,16},{1,17},{2,18},{3,19},{4,20},{5,21},{6,22},{7,23},{8,24},{9,... | collective-permute-start | bytes 737288 | tf_op jit(solution)/shard_map/ppermute | solution.py:309
  68.5 16.4 %copy-start = (f32[96,300]{1,0:T(8,128)S(1)}, f32[96,300]{1,0:T(8,128)}, u32[]{:S(2)}) copy-start(f32[96,300]{1,0:T(8,128)} %vec_ref.1) | copy-start | bytes 345604
  68.5 16.4 %copy-start.2 = (f32[96,300]{1,0:T(8,128)S(1)}, f32[96,300]{1,0:T(8,128)}, u32[]{:S(2)}) copy-start(f32[96,300]{1,0:T(8,128)} %acc_ref.1) | copy-start | bytes 345604
  68.5 16.4 %copy-start.4 = (f32[96]{0:T(128)S(1)}, f32[96]{0:T(128)}, u32[]{:S(2)}) copy-start(f32[96]{0:T(128)} %param.11) | copy-start | bytes 1156
  68.5 16.4 %copy-start.6 = (f32[96]{0:T(128)S(1)}, f32[96]{0:T(128)}, u32[]{:S(2)}) copy-start(f32[96]{0:T(128)} %param.13) | copy-start | bytes 1156
  68.6 7.7 %collective-permute-start.24 = (bf16[2,120,256]{2,1,0:T(8,128)(2,1)S(1)}, bf16[2,120,256]{2,1,0:T(8,128)(2,1)S(1)}, u32[]{:S(2)}, u32[]{:S(2)}) collective-permute-start(bf16[2,120,256]{2,1,0:T(8,128)(2,1)S(1)} %get-tuple-element.97), channel_id=1, source_target_pairs={{0,32},{1,33},{2,34},{3,35},{4,36},{5,37},{6,38},{7,39},{8,40},{9,... | collective-permute-start | bytes 368648 | tf_op jit(solution)/shard_map/ppermute | solution.py:309
  71.0 15.8 %copy-start.1 = (f32[96,300]{1,0:T(8,128)S(1)}, f32[96,300]{1,0:T(8,128)}, u32[]{:S(2)}) copy-start(f32[96,300]{1,0:T(8,128)} %rest_0_.1) | copy-start | bytes 345604
  71.0 15.8 %copy-start.3 = (f32[96,300]{1,0:T(8,128)S(1)}, f32[96,300]{1,0:T(8,128)}, u32[]{:S(2)}) copy-start(f32[96,300]{1,0:T(8,128)} %rest_2_.1) | copy-start | bytes 345604
  71.0 15.8 %copy-start.5 = (f32[96]{0:T(128)S(1)}, f32[96]{0:T(128)}, u32[]{:S(2)}) copy-start(f32[96]{0:T(128)} %param.15) | copy-start | bytes 1156
  71.0 15.8 %copy-start.7 = (f32[96]{0:T(128)S(1)}, f32[96]{0:T(128)}, u32[]{:S(2)}) copy-start(f32[96]{0:T(128)} %param.17) | copy-start | bytes 1156
  71.1 7.2 %collective-permute-start.20 = (bf16[120,256]{1,0:T(8,128)(2,1)S(1)}, bf16[120,256]{1,0:T(8,128)(2,1)S(1)}, u32[]{:S(2)}, u32[]{:S(2)}) collective-permute-start(bf16[120,256]{1,0:T(8,128)(2,1)S(1)} %get-tuple-element.71), channel_id=1, source_target_pairs={{0,1},{1,2},{2,3},{3,0},{4,5},{5,6},{6,7},{7,4},{8,9},{9,10},{10,1... | collective-permute-start | bytes 184328 | tf_op jit(solution)/shard_map/ppermute | solution.py:309
  71.5 7.0 %collective-permute-start.26 = (bf16[2,120,256]{2,1,0:T(8,128)(2,1)S(1)}, bf16[2,120,256]{2,1,0:T(8,128)(2,1)S(1)}, u32[]{:S(2)}, u32[]{:S(2)}) collective-permute-start(bf16[2,120,256]{2,1,0:T(8,128)(2,1)S(1)} %get-tuple-element.96), channel_id=1, source_target_pairs={{0,96},{1,97},{2,98},{3,99},{4,100},{5,101},{6,102},{7,103},{8,104... | collective-permute-start | bytes 368648 | tf_op jit(solution)/shard_map/ppermute | solution.py:309
  72.4 10.6 %collective-permute-start.22 = (bf16[120,256]{1,0:T(8,128)(2,1)S(1)}, bf16[120,256]{1,0:T(8,128)(2,1)S(1)}, u32[]{:S(2)}, u32[]{:S(2)}) collective-permute-start(bf16[120,256]{1,0:T(8,128)(2,1)S(1)} %get-tuple-element.72._), channel_id=1, source_target_pairs={{0,3},{1,0},{2,1},{3,2},{4,7},{5,4},{6,5},{7,6},{8,11},{9,8},{10,9... | collective-permute-start | bytes 184328 | tf_op jit(solution)/shard_map/ppermute | solution.py:309
  76.3 6.2 %collective-permute-start.25 = (bf16[2,120,256]{2,1,0:T(8,128)(2,1)S(1)}, bf16[2,120,256]{2,1,0:T(8,128)(2,1)S(1)}, u32[]{:S(2)}, u32[]{:S(2)}) collective-permute-start(bf16[2,120,256]{2,1,0:T(8,128)(2,1)S(1)} %shard_map.162), channel_id=1, source_target_pairs={{0,32},{1,33},{2,34},{3,35},{4,36},{5,37},{6,38},{7,39},{8,40},{9,... | collective-permute-start | bytes 368648 | tf_op jit(solution)/shard_map/ppermute | solution.py:309
  78.4 6.5 %collective-permute-start.21 = (bf16[120,256]{1,0:T(8,128)(2,1)S(1)}, bf16[120,256]{1,0:T(8,128)(2,1)S(1)}, u32[]{:S(2)}, u32[]{:S(2)}) collective-permute-start(bf16[120,256]{1,0:T(8,128)(2,1)S(1)} %add_convert_fusion), channel_id=1, source_target_pairs={{0,1},{1,2},{2,3},{3,0},{4,5},{5,6},{6,7},{7,4},{8,9},{9,10},{10,1... | collective-permute-start | bytes 184328 | tf_op jit(solution)/shard_map/ppermute | solution.py:309
  82.5 4.3 %collective-permute-start.27 = (bf16[120,256]{1,0:T(8,128)(2,1)S(1)}, bf16[120,256]{1,0:T(8,128)(2,1)S(1)}, u32[]{:S(2)}, u32[]{:S(2)}) collective-permute-start(bf16[120,256]{1,0:T(8,128)(2,1)S(1)} %get-tuple-element.89), channel_id=1, source_target_pairs={{0,128},{1,129},{2,130},{3,131},{4,132},{5,133},{6,134},{7,135},{8... | collective-permute-start | bytes 184328 | tf_op jit(solution)/shard_map/ppermute | solution.py:309

commit v6 on v5

--- a/solution.py
+++ b/solution.py
@@ -89,6 +89,9 @@
     )(*(pltpu.with_memory_space_constraint(v, pltpu.HBM) for v in (word_vecs, word_bias.reshape(1, ROWS), ctx_vecs, ctx_bias.reshape(1, ROWS))))
 
 
+AHEAD = 3
+
+
 def weight_kernel(chunks, index_ref, counts, *refs):
     outs, (held, sems) = refs[:-2], refs[-2:]
 
@@ -97,11 +100,13 @@
         return pltpu.make_async_copy(counts.at[pl.ds(start, ROWS)], held.at[n], sems.at[n])
 
     copies = [fetch(n) for n in range(4 * len(chunks))]
-    for copy in copies:
+    for copy in copies[:AHEAD]:
         copy.start()
     for n, copy in enumerate(copies):
         weight_ref, log_ref = outs[n // 4 * 2], outs[n // 4 * 2 + 1]
         copy.wait()
+        if n + AHEAD < len(copies):
+            copies[n + AHEAD].start()
 
         def step(i, _):
             rows = pl.ds(pl.multiple_of(i * 8, 8), 8)
@@ -242,10 +247,12 @@
 WORDS_SCRATCH = [pltpu.VMEM((CHUNK, 384), jnp.bfloat16)]
 
 
-def update_kernel(bias_lane, scale, total_ref, add_a, add_b, vec_ref, bias_ref, acc_ref, bacc_ref, nv, nb, na, nba):
-    packed = total_ref[...] + add_a[...].astype(jnp.float32)
-    if add_b is not None:
-        packed = packed + add_b[...].astype(jnp.float32)
+def update_one(bias_lane, scale, sums, params, outs):
+    vec_ref, bias_ref, acc_ref, bacc_ref = params
+    nv, nb, na, nba = outs
+    packed = sums[0][...]
+    for ref in sums[1:]:
+        packed = packed + ref[...].astype(jnp.float32)
     packed = packed * scale
     tail = unpack_tail(packed)
     for columns, grad in ((slice(0, LO), packed[:ROWS]), (slice(LO, D), tail[:, : D - LO])):
@@ -258,27 +265,23 @@
     nb[...] = bias_ref[...] - step_rate * grad / jnp.sqrt(accum)
 
 
-def update(total, add_a, add_b, vecs, bias, accum, bias_accum, bias_lane, scale):
-    row = lambda a: a.reshape(1, ROWS)
-    if add_b is None:
-        kernel = lambda t, a, *rest: update_kernel(bias_lane, scale, t, a, None, *rest)
-        sums = (total, add_a)
-    else:
-        kernel = functools.partial(update_kernel, bias_lane, scale)
-        sums = (total, add_a, add_b)
-    f32 = jnp.float32
-    nv, nb, na, nba = pl.pallas_call(
+def update(word_sums, word_params, word_scale, ctx_sums, ctx_params, ctx_scale):
+    def kernel(*refs):
+        words, refs = refs[:3], refs[3:]
+        contexts, refs = refs[:2], refs[2:]
+        update_one(D - LO, word_scale, words, refs[:4], refs[8:12])
+        update_one(D - LO + 1, ctx_scale, contexts, refs[4:8], refs[12:16])
+
+    row = lambda a: a.reshape(1, ROWS) if a.ndim == 1 else a
+    shapes = [jax.ShapeDtypeStruct((ROWS, D), jnp.float32), jax.ShapeDtypeStruct((1, ROWS), jnp.float32)]
+    outs = pl.pallas_call(
         kernel,
-        out_shape=[
-            jax.ShapeDtypeStruct((ROWS, D), f32),
-            jax.ShapeDtypeStruct((1, ROWS), f32),
-            jax.ShapeDtypeStruct((ROWS, D), f32),
-            jax.ShapeDtypeStruct((1, ROWS), f32),
-        ],
-        compiler_params=pltpu.CompilerParams(vmem_limit_bytes=6 * MIB),
-        cost_estimate=pl.CostEstimate(flops=400000, bytes_accessed=800000, transcendentals=30000),
-    )(*sums, vecs, row(bias), accum, row(bias_accum))
-    return nv, nb.reshape(ROWS), na, nba.reshape(ROWS)
+        out_shape=shapes * 4,
+        compiler_params=pltpu.CompilerParams(vmem_limit_bytes=8 * MIB),
+        cost_estimate=pl.CostEstimate(flops=800000, bytes_accessed=1600000, transcendentals=60000),
+        name="update",
+    )(*word_sums, *ctx_sums, *(row(a) for a in (*word_params, *ctx_params)))
+    return tuple(a.reshape(ROWS) if a.shape[0] == 1 else a for a in outs)
 
 
 def spread(index):
@@ -398,21 +401,9 @@
 
     word_scale = 2.0 / (counts.shape[1] * lax.axis_size("ctx"))
     ctx_scale = 2.0 / (counts.shape[0] * lax.axis_size("word"))
-    new_ctx_vecs, new_ctx_bias, new_ctx_accum, new_ctx_bias_accum = update(
-        t_own, rl, None, ctx_vecs, ctx_bias, ctx_accum, ctx_bias_accum, D - LO + 1, ctx_scale
-    )
-    new_word_vecs, new_word_bias, new_word_accum, new_word_bias_accum = update(
-        z_own, rza, rzb, word_vecs, word_bias, word_accum, word_bias_accum, D - LO, word_scale
-    )
-    return (
-        new_word_vecs,
-        new_word_bias,
-        new_word_accum,
-        new_word_bias_accum,
-        new_ctx_vecs,
-        new_ctx_bias,
-        new_ctx_accum,
-        new_ctx_bias_accum,
+    return update(
+        (z_own, rza, rzb), (word_vecs, word_bias, word_accum, word_bias_accum), word_scale,
+        (t_own, rl), (ctx_vecs, ctx_bias, ctx_accum, ctx_bias_accum), ctx_scale,
     )
 
 

time: 87.8 us -> 89.7 us (1.022)
  waiting for transfers between devices: 37.3 us -> 38.2 us
    pallas_call x2, Pallas kernels: 7.48 us -> 8.99 us  [weights(): pl.pallas_call(functools.partial(weight_kernel, chunks), in_specs=[pl.Blo...]
    ppermute x28, waiting for transfers between devices: 37.3 us -> 38.2 us  [move(): return lax.ppermute(value, ('word', 'ctx'), perm)]
where the time goes in v6:
time: 89.7 us; the launch traced here: 89.4 us
  waiting for transfers between devices  38.2 us (43%)
  starting transfers between devices  27.7 us (31%)
  Pallas kernels  21.9 us (24%)
  between operations  1.05 us (1%)
    ppermute x28, waiting for transfers between devices, move(): return lax.ppermute(value, ('word', 'ctx'), perm)  38.2 us
    ppermute x28, starting transfers between devices, move(): return lax.ppermute(value, ('word', 'ctx'), perm)  27.7 us
    pallas_call x9, Pallas kernels, call(): pl.pallas_call(kernel, in_specs=[SMEM_SPEC] * len(scalars) + [VMEM_SPEC]...  10.1 us
    pallas_call x2, Pallas kernels, weights(): pl.pallas_call(functools.partial(weight_kernel, chunks), in_specs=[pl.Blo...  8.99 us
  transfers between devices with their start and end apart: 28, of which 11 were waited for; matrix products, arithmetic and copies ran while one was open for 1% of the time, Pallas kernels for 21%

profile of v6, /device:TPU:32, one launch (start us, length us, event | category | flops | bytes accessed | tf_op | source)
XLA Modules:
  0.0 89.4 jit_solution(5916936105719149184)
XLA Ops:
  0.6 1.7 %pack.1 = (bf16[120,256]{1,0:T(8,128)(2,1)S(1)}, bf16[120,256]{1,0:T(8,128)(2,1)S(1)}, s32[16]{0:T(128)S(1)}, s32[16]{0:T(128)S(1)}, s32[16]{0:T(128)S(1)}) custom-call(f32[96,300]{1,0:T(8,128)} %refs_5_.1, f32[1,96]{1,0:T(1,128)} %bitcast.25, f32[96,300]{1,0:T(8,128)} %refs_9_.1, f32[1,96]{1,0:T(1,128)} %bitcast.27), custom_call_target="tpu_custom_call" | custom-call | flops 100000 | bytes 400000 | tf_op jit(solution)/shard_map/pack/pallas_call | solution.py:81
  2.4 3.3 %collective-permute-start.1 = (bf16[120,256]{1,0:T(8,128)(2,1)S(1)}, bf16[120,256]{1,0:T(8,128)(2,1)S(1)}, u32[]{:S(2)}, u32[]{:S(2)}) collective-permute-start(bf16[120,256]{1,0:T(8,128)(2,1)S(1)} %get-tuple-element.51), channel_id=1, source_target_pairs={{0,1},{1,2},{2,3},{3,0},{4,5},{5,6},{6,7},{7,4},{8,9},{9,10},{10,1... | collective-permute-start | bytes 184328 | tf_op jit(solution)/shard_map/ppermute | solution.py:312
  5.7 2.7 %collective-permute-start = (bf16[120,256]{1,0:T(8,128)(2,1)S(1)}, bf16[120,256]{1,0:T(8,128)(2,1)S(1)}, u32[]{:S(2)}, u32[]{:S(2)}) collective-permute-start(bf16[120,256]{1,0:T(8,128)(2,1)S(1)} %get-tuple-element.51), channel_id=1, source_target_pairs={{0,19},{1,16},{2,17},{3,18},{4,23},{5,20},{6,21},{7,22},{8,27},{9,... | collective-permute-start | bytes 184328 | tf_op jit(solution)/shard_map/ppermute | solution.py:312
  8.5 1.0 %collective-permute-start.4 = (bf16[120,256]{1,0:T(8,128)(2,1)S(1)}, bf16[120,256]{1,0:T(8,128)(2,1)S(1)}, u32[]{:S(2)}, u32[]{:S(2)}) collective-permute-start(bf16[120,256]{1,0:T(8,128)(2,1)S(1)} %get-tuple-element.51), channel_id=1, source_target_pairs={{0,16},{1,17},{2,18},{3,19},{4,20},{5,21},{6,22},{7,23},{8,24},{9,... | collective-permute-start | bytes 184328 | tf_op jit(solution)/shard_map/ppermute | solution.py:312
  9.4 1.0 %collective-permute-start.8 = (bf16[120,256]{1,0:T(8,128)(2,1)S(1)}, bf16[120,256]{1,0:T(8,128)(2,1)S(1)}, u32[]{:S(2)}, u32[]{:S(2)}) collective-permute-start(bf16[120,256]{1,0:T(8,128)(2,1)S(1)} %get-tuple-element.56), channel_id=1, source_target_pairs={{0,128},{1,129},{2,130},{3,131},{4,132},{5,133},{6,134},{7,135},{8... | collective-permute-start | bytes 184328 | tf_op jit(solution)/shard_map/ppermute | solution.py:312
  10.4 4.5 %shard_map.153 = (f32[384,1536]{1,0:T(8,128)S(1)}, f32[384,1536]{1,0:T(8,128)S(1)}, f32[384,1536]{1,0:T(8,128)S(1)}, f32[384,1536]{1,0:T(8,128)S(1)}) custom-call(s32[16]{0:T(128)S(1)} %get-tuple-element.52.index_ref, s32[1536,1536]{1,0:T(8,128)} %counts.3), custom_call_target="tpu_custom_call" | custom-call | flops 23592960 | bytes 14155776 | tf_op jit(solution)/shard_map/pallas_call | solution.py:127
  15.0 4.5 %shard_map.156 = (f32[384,1536]{1,0:T(8,128)S(1)}, f32[384,1536]{1,0:T(8,128)S(1)}, f32[384,1536]{1,0:T(8,128)S(1)}, f32[384,1536]{1,0:T(8,128)S(1)}) custom-call(s32[16]{0:T(128)S(1)} %get-tuple-element.52.index_ref, s32[1536,1536]{1,0:T(8,128)} %counts.3), custom_call_target="tpu_custom_call" | custom-call | flops 23592960 | bytes 14155776 | tf_op jit(solution)/shard_map/pallas_call | solution.py:127
  19.5 1.7 %collective-permute-start.7 = (bf16[2,120,256]{2,1,0:T(8,128)(2,1)S(1)}, bf16[2,120,256]{2,1,0:T(8,128)(2,1)S(1)}, u32[]{:S(2)}, u32[]{:S(2)}) collective-permute-start(bf16[2,120,256]{2,1,0:T(8,128)(2,1)S(1)} %pad_maximum_fusion.8), channel_id=1, source_target_pairs={{0,4},{1,5},{2,6},{3,7},{4,8},{5,9},{6,10},{7,11},{8,12},{9,13},{1... | collective-permute-start | bytes 368648 | tf_op jit(solution)/shard_map/ppermute | solution.py:312
  21.2 1.7 %collective-permute-start.5 = (bf16[2,120,256]{2,1,0:T(8,128)(2,1)S(1)}, bf16[2,120,256]{2,1,0:T(8,128)(2,1)S(1)}, u32[]{:S(2)}, u32[]{:S(2)}) collective-permute-start(bf16[2,120,256]{2,1,0:T(8,128)(2,1)S(1)} %pad_maximum_fusion.7), channel_id=1, source_target_pairs={{0,4},{1,5},{2,6},{3,7},{4,8},{5,9},{6,10},{7,11},{8,12},{9,13},{1... | collective-permute-start | bytes 368648 | tf_op jit(solution)/shard_map/ppermute | solution.py:312
  22.8 0.1 collective-permute-start.9
  22.9 1.5 %collective-permute-start.2 = (bf16[120,256]{1,0:T(8,128)(2,1)S(1)}, bf16[120,256]{1,0:T(8,128)(2,1)S(1)}, u32[]{:S(2)}, u32[]{:S(2)}) collective-permute-start(bf16[120,256]{1,0:T(8,128)(2,1)S(1)} %collective-permute-done.1.b), channel_id=1, source_target_pairs={{0,1},{1,2},{2,3},{3,0},{4,5},{5,6},{6,7},{7,4},{8,9},{9,10},{10,1... | collective-permute-start | bytes 184328 | tf_op jit(solution)/shard_map/ppermute | solution.py:312
  24.5 5.5 %collective-permute-done.2.c = bf16[120,256]{1,0:T(8,128)(2,1)S(1)} collective-permute-done((bf16[120,256]{1,0:T(8,128)(2,1)S(1)}, bf16[120,256]{1,0:T(8,128)(2,1)S(1)}, u32[]{:S(2)}, u32[]{:S(2)}) %collective-permute-start.2) | collective-permute-done | bytes 61472 | tf_op jit(solution)/shard_map/ppermute | solution.py:312
  30.0 0.1 collective-permute-start.3
  30.2 1.6 %collective-permute-start.10 = (bf16[4,120,256]{2,1,0:T(8,128)(2,1)S(1)}, bf16[4,120,256]{2,1,0:T(8,128)(2,1)S(1)}, u32[]{:S(2)}, u32[]{:S(2)}) collective-permute-start(bf16[4,120,256]{2,1,0:T(8,128)(2,1)S(1)} %pad_maximum_fusion.5), channel_id=1, source_target_pairs={{0,32},{1,33},{2,34},{3,35},{4,36},{5,37},{6,38},{7,39},{8,40},{9,... | collective-permute-start | bytes 737288 | tf_op jit(solution)/shard_map/ppermute | solution.py:312
  31.9 1.4 %collective-permute-start.6 = (bf16[4,120,256]{2,1,0:T(8,128)(2,1)S(1)}, bf16[4,120,256]{2,1,0:T(8,128)(2,1)S(1)}, u32[]{:S(2)}, u32[]{:S(2)}) collective-permute-start(bf16[4,120,256]{2,1,0:T(8,128)(2,1)S(1)} %get-tuple-element.106), channel_id=1, source_target_pairs={{0,4},{1,5},{2,6},{3,7},{4,8},{5,9},{6,10},{7,11},{8,12},{9,13},{1... | collective-permute-start | bytes 737288 | tf_op jit(solution)/shard_map/ppermute | solution.py:312
  33.2 4.4 %collective-permute-done.10 = bf16[4,120,256]{2,1,0:T(8,128)(2,1)S(1)} collective-permute-done((bf16[4,120,256]{2,1,0:T(8,128)(2,1)S(1)}, bf16[4,120,256]{2,1,0:T(8,128)(2,1)S(1)}, u32[]{:S(2)}, u32[]{:S(2)}) %collective-permute-start.10) | collective-permute-done | bytes 245792 | tf_op jit(solution)/shard_map/ppermute | solution.py:312
  37.7 0.4 collective-permute-start.11
  38.1 5.8 %collective-permute-done.11 = bf16[2,120,256]{2,1,0:T(8,128)(2,1)S(1)} collective-permute-done((bf16[2,120,256]{2,1,0:T(8,128)(2,1)S(1)}, bf16[2,120,256]{2,1,0:T(8,128)(2,1)S(1)}, u32[]{:S(2)}, u32[]{:S(2)}) %collective-permute-start.11) | collective-permute-done | bytes 122912 | tf_op jit(solution)/shard_map/ppermute | solution.py:312
  43.9 0.1 collective-permute-start.12
  44.1 0.6 collective-permute-start.13
  44.7 1.5 %collective-permute-start.17 = (bf16[4,120,256]{2,1,0:T(8,128)(2,1)S(1)}, bf16[4,120,256]{2,1,0:T(8,128)(2,1)S(1)}, u32[]{:S(2)}, u32[]{:S(2)}) collective-permute-start(bf16[4,120,256]{2,1,0:T(8,128)(2,1)S(1)} %pad_maximum_fusion.4.w), channel_id=1, source_target_pairs={{0,4},{1,5},{2,6},{3,7},{4,8},{5,9},{6,10},{7,11},{8,12},{9,13},{1... | collective-permute-start | bytes 737288 | tf_op jit(solution)/shard_map/ppermute | solution.py:312
  46.2 2.3 %shard_map.154 = (bf16[4,120,256]{2,1,0:T(8,128)(2,1)S(1)}, bf16[384,1536]{1,0:T(8,128)(2,1)S(1)}, bf16[384,384]{1,0:T(8,128)(2,1)S(1)}, bf16[1536,384]{1,0:T(8,128)(2,1)S(1)}, bf16[384,1536]{1,0:T(8,128)(2,1)S(1)}) custom-call(s32[16]{0:T(128)S(1)} %get-tuple-element.55.index_ref, bf16[4,120,256]{2,1,0:T(8,128)(2,1)S(1)} %pad_maximum_fusion.4.w, ...), custom_call_target="tpu_custom_call" | custom-call | flops 905969664 | bytes 4194304 | tf_op jit(solution)/shard_map/pallas_call | solution.py:235
  48.5 0.2 collective-permute-start.14
  48.7 1.5 %shard_map.155 = (f32[4,120,256]{2,1,0:T(8,128)S(1)}, bf16[384,1536]{1,0:T(8,128)(2,1)S(1)}, bf16[384,384]{1,0:T(8,128)(2,1)S(1)}) custom-call(bf16[4,120,256]{2,1,0:T(8,128)(2,1)S(1)} %get-tuple-element.107.w, f32[384,1536]{1,0:T(8,128)S(1)} %get-tuple-element.53.weight, f32[384,1536]{1,0:T(8,128)S(1)} %get-tuple-element.54.log_count, ...), custom_call_target="tpu_custom_call" | custom-call | flops 905969664 | bytes 4194304 | tf_op jit(solution)/shard_map/pallas_call | solution.py:235
  50.2 1.5 %shard_map.157 = (bf16[4,120,256]{2,1,0:T(8,128)(2,1)S(1)}, bf16[384,1536]{1,0:T(8,128)(2,1)S(1)}, bf16[384,384]{1,0:T(8,128)(2,1)S(1)}) custom-call(bf16[4,120,256]{2,1,0:T(8,128)(2,1)S(1)} %collective-permute-done.13.w, f32[384,1536]{1,0:T(8,128)S(1)} %get-tuple-element.62.weight, f32[384,1536]{1,0:T(8,128)S(1)} %get-tuple-element.63.log_count, ...), custom_call_target="tpu_custom_call" | custom-call | flops 905969664 | bytes 4194304 | tf_op jit(solution)/shard_map/pallas_call | solution.py:235
  51.7 0.6 collective-permute-done.17.w
  52.3 1.5 %shard_map.158 = (bf16[4,120,256]{2,1,0:T(8,128)(2,1)S(1)}, bf16[384,1536]{1,0:T(8,128)(2,1)S(1)}, bf16[384,384]{1,0:T(8,128)(2,1)S(1)}) custom-call(bf16[4,120,256]{2,1,0:T(8,128)(2,1)S(1)} %collective-permute-done.17.w, f32[384,1536]{1,0:T(8,128)S(1)} %get-tuple-element.66.weight, f32[384,1536]{1,0:T(8,128)S(1)} %get-tuple-element.67.log_count, ...), custom_call_target="tpu_custom_call" | custom-call | flops 905969664 | bytes 4194304 | tf_op jit(solution)/shard_map/pallas_call | solution.py:235
  53.8 3.2 %shard_map.160 = (f32[8,120,256]{2,1,0:T(8,128)S(1)}, bf16[8,120,256]{2,1,0:T(8,128)(2,1)S(1)}) custom-call(s32[16]{0:T(128)S(1)} %get-tuple-element.73.index_ref, bf16[384,1536]{1,0:T(8,128)(2,1)S(1)} %get-tuple-element.74.s0, bf16[384,1536]{1,0:T(8,128)(2,1)S(1)} %get-tuple-element.75.s1, bf16[384,1536]{1,0:T(8,128)(2,1)S(1)} %get-tuple-element.76.s2, ...), custom_call_target="tpu_custom_call" | custom-call | flops 1811939328 | bytes 4194304 | tf_op jit(solution)/shard_map/pallas_call | solution.py:235
  57.0 0.1 collective-permute-start.23
  57.1 0.4 collective-permute-start.18
  57.6 1.2 %collective-permute-start.15 = (bf16[8,120,256]{2,1,0:T(8,128)(2,1)S(1)}, bf16[8,120,256]{2,1,0:T(8,128)(2,1)S(1)}, u32[]{:S(2)}, u32[]{:S(2)}) collective-permute-start(bf16[8,120,256]{2,1,0:T(8,128)(2,1)S(1)} %pad_maximum_fusion), channel_id=1, source_target_pairs={{0,4},{1,5},{2,6},{3,7},{4,8},{5,9},{6,10},{7,11},{8,12},{9,13},{1... | collective-permute-start | bytes 1474568 | tf_op jit(solution)/shard_map/ppermute | solution.py:312
  58.8 5.8 %collective-permute-done.18 = bf16[4,120,256]{2,1,0:T(8,128)(2,1)S(1)} collective-permute-done((bf16[4,120,256]{2,1,0:T(8,128)(2,1)S(1)}, bf16[4,120,256]{2,1,0:T(8,128)(2,1)S(1)}, u32[]{:S(2)}, u32[]{:S(2)}) %collective-permute-start.18) | collective-permute-done | bytes 245792 | tf_op jit(solution)/shard_map/ppermute | solution.py:312
  64.6 0.2 fusion
  64.8 5.1 %collective-permute-done.15.rn = bf16[8,120,256]{2,1,0:T(8,128)(2,1)S(1)} collective-permute-done((bf16[8,120,256]{2,1,0:T(8,128)(2,1)S(1)}, bf16[8,120,256]{2,1,0:T(8,128)(2,1)S(1)}, u32[]{:S(2)}, u32[]{:S(2)}) %collective-permute-start.15) | collective-permute-done | bytes 491552 | tf_op jit(solution)/shard_map/ppermute | solution.py:312
  69.9 0.1 collective-permute-start.16
  70.1 0.1 collective-permute-start.24
  70.2 2.3 %collective-permute-done.19.ya = bf16[4,120,256]{2,1,0:T(8,128)(2,1)S(1)} collective-permute-done((bf16[4,120,256]{2,1,0:T(8,128)(2,1)S(1)}, bf16[4,120,256]{2,1,0:T(8,128)(2,1)S(1)}, u32[]{:S(2)}, u32[]{:S(2)}) %collective-permute-start.19) | collective-permute-done | bytes 245792 | tf_op jit(solution)/shard_map/ppermute | solution.py:312
  72.5 0.1 shard_map.159
  72.6 0.3 collective-permute-start.20
  73.0 1.0 %collective-permute-start.26 = (bf16[2,120,256]{2,1,0:T(8,128)(2,1)S(1)}, bf16[2,120,256]{2,1,0:T(8,128)(2,1)S(1)}, u32[]{:S(2)}, u32[]{:S(2)}) collective-permute-start(bf16[2,120,256]{2,1,0:T(8,128)(2,1)S(1)} %get-tuple-element.96), channel_id=1, source_target_pairs={{0,96},{1,97},{2,98},{3,99},{4,100},{5,101},{6,102},{7,103},{8,104... | collective-permute-start | bytes 368648 | tf_op jit(solution)/shard_map/ppermute | solution.py:312
  73.9 3.8 %collective-permute-start.22 = (bf16[120,256]{1,0:T(8,128)(2,1)S(1)}, bf16[120,256]{1,0:T(8,128)(2,1)S(1)}, u32[]{:S(2)}, u32[]{:S(2)}) collective-permute-start(bf16[120,256]{1,0:T(8,128)(2,1)S(1)} %get-tuple-element.72._), channel_id=1, source_target_pairs={{0,3},{1,0},{2,1},{3,2},{4,7},{5,4},{6,5},{7,6},{8,11},{9,8},{10,9... | collective-permute-start | bytes 184328 | tf_op jit(solution)/shard_map/ppermute | solution.py:312
  77.8 1.2 %collective-permute-start.25 = (bf16[2,120,256]{2,1,0:T(8,128)(2,1)S(1)}, bf16[2,120,256]{2,1,0:T(8,128)(2,1)S(1)}, u32[]{:S(2)}, u32[]{:S(2)}) collective-permute-start(bf16[2,120,256]{2,1,0:T(8,128)(2,1)S(1)} %shard_map.161), channel_id=1, source_target_pairs={{0,32},{1,33},{2,34},{3,35},{4,36},{5,37},{6,38},{7,39},{8,40},{9,... | collective-permute-start | bytes 368648 | tf_op jit(solution)/shard_map/ppermute | solution.py:312
  79.0 0.9 collective-permute-done.20
  80.0 4.0 %collective-permute-done.25.xr = bf16[2,120,256]{2,1,0:T(8,128)(2,1)S(1)} collective-permute-done((bf16[2,120,256]{2,1,0:T(8,128)(2,1)S(1)}, bf16[2,120,256]{2,1,0:T(8,128)(2,1)S(1)}, u32[]{:S(2)}, u32[]{:S(2)}) %collective-permute-start.25) | collective-permute-done | bytes 122912 | tf_op jit(solution)/shard_map/ppermute | solution.py:312
  84.0 0.6 collective-permute-start.27
  84.6 1.8 %collective-permute-done.21.refs_1_ = bf16[120,256]{1,0:T(8,128)(2,1)S(1)} collective-permute-done((bf16[120,256]{1,0:T(8,128)(2,1)S(1)}, bf16[120,256]{1,0:T(8,128)(2,1)S(1)}, u32[]{:S(2)}, u32[]{:S(2)}) %collective-permute-start.21) | collective-permute-done | bytes 61472 | tf_op jit(solution)/shard_map/ppermute | solution.py:312
  86.4 1.9 %collective-permute-done.27.refs_4_ = bf16[120,256]{1,0:T(8,128)(2,1)S(1)} collective-permute-done((bf16[120,256]{1,0:T(8,128)(2,1)S(1)}, bf16[120,256]{1,0:T(8,128)(2,1)S(1)}, u32[]{:S(2)}, u32[]{:S(2)}) %collective-permute-start.27) | collective-permute-done | bytes 61472 | tf_op jit(solution)/shard_map/ppermute | solution.py:312
  88.4 1.0 %update.1 = (f32[96,300]{1,0:T(8,128)}, f32[1,96]{1,0:T(1,128)}, f32[96,300]{1,0:T(8,128)}, f32[1,96]{1,0:T(1,128)}, f32[96,300]{1,0:T(8,128)}, /*index=5*/f32[1...) custom-call(f32[120,256]{1,0:T(8,128)S(1)} %get-tuple-element.69.refs_0_, ...), custom_call_target="tpu_custom_call" | custom-call | flops 800000 | bytes 1600000 | tf_op jit(solution)/shard_map/update/pallas_call | solution.py:277
  (60 shorter events, 0.7 us)
Async XLA Ops:
  2.4 17.1 %collective-permute-start.1 = (bf16[120,256]{1,0:T(8,128)(2,1)S(1)}, bf16[120,256]{1,0:T(8,128)(2,1)S(1)}, u32[]{:S(2)}, u32[]{:S(2)}) collective-permute-start(bf16[120,256]{1,0:T(8,128)(2,1)S(1)} %get-tuple-element.51), channel_id=1, source_target_pairs={{0,1},{1,2},{2,3},{3,0},{4,5},{5,6},{6,7},{7,4},{8,9},{9,10},{10,1... | collective-permute-start | bytes 184328 | tf_op jit(solution)/shard_map/ppermute | solution.py:312
  5.7 13.7 %collective-permute-start = (bf16[120,256]{1,0:T(8,128)(2,1)S(1)}, bf16[120,256]{1,0:T(8,128)(2,1)S(1)}, u32[]{:S(2)}, u32[]{:S(2)}) collective-permute-start(bf16[120,256]{1,0:T(8,128)(2,1)S(1)} %get-tuple-element.51), channel_id=1, source_target_pairs={{0,19},{1,16},{2,17},{3,18},{4,23},{5,20},{6,21},{7,22},{8,27},{9,... | collective-permute-start | bytes 184328 | tf_op jit(solution)/shard_map/ppermute | solution.py:312
  8.5 12.7 %collective-permute-start.4 = (bf16[120,256]{1,0:T(8,128)(2,1)S(1)}, bf16[120,256]{1,0:T(8,128)(2,1)S(1)}, u32[]{:S(2)}, u32[]{:S(2)}) collective-permute-start(bf16[120,256]{1,0:T(8,128)(2,1)S(1)} %get-tuple-element.51), channel_id=1, source_target_pairs={{0,16},{1,17},{2,18},{3,19},{4,20},{5,21},{6,22},{7,23},{8,24},{9,... | collective-permute-start | bytes 184328 | tf_op jit(solution)/shard_map/ppermute | solution.py:312
  9.4 13.4 %collective-permute-start.8 = (bf16[120,256]{1,0:T(8,128)(2,1)S(1)}, bf16[120,256]{1,0:T(8,128)(2,1)S(1)}, u32[]{:S(2)}, u32[]{:S(2)}) collective-permute-start(bf16[120,256]{1,0:T(8,128)(2,1)S(1)} %get-tuple-element.56), channel_id=1, source_target_pairs={{0,128},{1,129},{2,130},{3,131},{4,132},{5,133},{6,134},{7,135},{8... | collective-permute-start | bytes 184328 | tf_op jit(solution)/shard_map/ppermute | solution.py:312
  19.5 12.3 %collective-permute-start.7 = (bf16[2,120,256]{2,1,0:T(8,128)(2,1)S(1)}, bf16[2,120,256]{2,1,0:T(8,128)(2,1)S(1)}, u32[]{:S(2)}, u32[]{:S(2)}) collective-permute-start(bf16[2,120,256]{2,1,0:T(8,128)(2,1)S(1)} %pad_maximum_fusion.8), channel_id=1, source_target_pairs={{0,4},{1,5},{2,6},{3,7},{4,8},{5,9},{6,10},{7,11},{8,12},{9,13},{1... | collective-permute-start | bytes 368648 | tf_op jit(solution)/shard_map/ppermute | solution.py:312
  21.2 10.6 %collective-permute-start.5 = (bf16[2,120,256]{2,1,0:T(8,128)(2,1)S(1)}, bf16[2,120,256]{2,1,0:T(8,128)(2,1)S(1)}, u32[]{:S(2)}, u32[]{:S(2)}) collective-permute-start(bf16[2,120,256]{2,1,0:T(8,128)(2,1)S(1)} %pad_maximum_fusion.7), channel_id=1, source_target_pairs={{0,4},{1,5},{2,6},{3,7},{4,8},{5,9},{6,10},{7,11},{8,12},{9,13},{1... | collective-permute-start | bytes 368648 | tf_op jit(solution)/shard_map/ppermute | solution.py:312
  22.8 7.3 %collective-permute-start.9 = (bf16[2,120,256]{2,1,0:T(8,128)(2,1)S(1)}, bf16[2,120,256]{2,1,0:T(8,128)(2,1)S(1)}, u32[]{:S(2)}, u32[]{:S(2)}) collective-permute-start(bf16[2,120,256]{2,1,0:T(8,128)(2,1)S(1)} %pad_maximum_fusion.9), channel_id=1, source_target_pairs={{0,16},{1,17},{2,18},{3,19},{4,20},{5,21},{6,22},{7,23},{8,24},{9,... | collective-permute-start | bytes 368648 | tf_op jit(solution)/shard_map/ppermute | solution.py:312
  22.9 7.1 %collective-permute-start.2 = (bf16[120,256]{1,0:T(8,128)(2,1)S(1)}, bf16[120,256]{1,0:T(8,128)(2,1)S(1)}, u32[]{:S(2)}, u32[]{:S(2)}) collective-permute-start(bf16[120,256]{1,0:T(8,128)(2,1)S(1)} %collective-permute-done.1.b), channel_id=1, source_target_pairs={{0,1},{1,2},{2,3},{3,0},{4,5},{5,6},{6,7},{7,4},{8,9},{9,10},{10,1... | collective-permute-start | bytes 184328 | tf_op jit(solution)/shard_map/ppermute | solution.py:312
  30.0 1.8 %collective-permute-start.3 = (bf16[3,120,256]{2,1,0:T(8,128)(2,1)S(1)}, bf16[3,120,256]{2,1,0:T(8,128)(2,1)S(1)}, u32[]{:S(2)}, u32[]{:S(2)}) collective-permute-start(bf16[3,120,256]{2,1,0:T(8,128)(2,1)S(1)} %shard_map.152), channel_id=1, source_target_pairs={{0,16},{1,17},{2,18},{3,19},{4,20},{5,21},{6,22},{7,23},{8,24},{9,... | collective-permute-start | bytes 552968 | tf_op jit(solution)/shard_map/ppermute | solution.py:312
  30.2 7.5 %collective-permute-start.10 = (bf16[4,120,256]{2,1,0:T(8,128)(2,1)S(1)}, bf16[4,120,256]{2,1,0:T(8,128)(2,1)S(1)}, u32[]{:S(2)}, u32[]{:S(2)}) collective-permute-start(bf16[4,120,256]{2,1,0:T(8,128)(2,1)S(1)} %pad_maximum_fusion.5), channel_id=1, source_target_pairs={{0,32},{1,33},{2,34},{3,35},{4,36},{5,37},{6,38},{7,39},{8,40},{9,... | collective-permute-start | bytes 737288 | tf_op jit(solution)/shard_map/ppermute | solution.py:312
  31.9 12.1 %collective-permute-start.6 = (bf16[4,120,256]{2,1,0:T(8,128)(2,1)S(1)}, bf16[4,120,256]{2,1,0:T(8,128)(2,1)S(1)}, u32[]{:S(2)}, u32[]{:S(2)}) collective-permute-start(bf16[4,120,256]{2,1,0:T(8,128)(2,1)S(1)} %get-tuple-element.106), channel_id=1, source_target_pairs={{0,4},{1,5},{2,6},{3,7},{4,8},{5,9},{6,10},{7,11},{8,12},{9,13},{1... | collective-permute-start | bytes 737288 | tf_op jit(solution)/shard_map/ppermute | solution.py:312
  37.7 6.2 %collective-permute-start.11 = (bf16[2,120,256]{2,1,0:T(8,128)(2,1)S(1)}, bf16[2,120,256]{2,1,0:T(8,128)(2,1)S(1)}, u32[]{:S(2)}, u32[]{:S(2)}) collective-permute-start(bf16[2,120,256]{2,1,0:T(8,128)(2,1)S(1)} %slice.61), channel_id=1, source_target_pairs={{0,32},{1,33},{2,34},{3,35},{4,36},{5,37},{6,38},{7,39},{8,40},{9,... | collective-permute-start | bytes 368648 | tf_op jit(solution)/shard_map/ppermute | solution.py:312
  43.9 2.3 %collective-permute-start.12 = (bf16[6,120,256]{2,1,0:T(8,128)(2,1)S(1)}, bf16[6,120,256]{2,1,0:T(8,128)(2,1)S(1)}, u32[]{:S(2)}, u32[]{:S(2)}) collective-permute-start(bf16[6,120,256]{2,1,0:T(8,128)(2,1)S(1)} %pad_maximum_fusion.1), channel_id=1, source_target_pairs={{0,16},{1,17},{2,18},{3,19},{4,20},{5,21},{6,22},{7,23},{8,24},{9,... | collective-permute-start | bytes 1105928 | tf_op jit(solution)/shard_map/ppermute | solution.py:312
  44.1 6.1 %collective-permute-start.13 = (bf16[4,120,256]{2,1,0:T(8,128)(2,1)S(1)}, bf16[4,120,256]{2,1,0:T(8,128)(2,1)S(1)}, u32[]{:S(2)}, u32[]{:S(2)}) collective-permute-start(bf16[4,120,256]{2,1,0:T(8,128)(2,1)S(1)} %pad_maximum_fusion.6), channel_id=1, source_target_pairs={{0,16},{1,17},{2,18},{3,19},{4,20},{5,21},{6,22},{7,23},{8,24},{9,... | collective-permute-start | bytes 737288 | tf_op jit(solution)/shard_map/ppermute | solution.py:312
  44.7 7.7 %collective-permute-start.17 = (bf16[4,120,256]{2,1,0:T(8,128)(2,1)S(1)}, bf16[4,120,256]{2,1,0:T(8,128)(2,1)S(1)}, u32[]{:S(2)}, u32[]{:S(2)}) collective-permute-start(bf16[4,120,256]{2,1,0:T(8,128)(2,1)S(1)} %pad_maximum_fusion.4.w), channel_id=1, source_target_pairs={{0,4},{1,5},{2,6},{3,7},{4,8},{5,9},{6,10},{7,11},{8,12},{9,13},{1... | collective-permute-start | bytes 737288 | tf_op jit(solution)/shard_map/ppermute | solution.py:312
  48.5 9.1 %collective-permute-start.14 = (bf16[4,120,256]{2,1,0:T(8,128)(2,1)S(1)}, bf16[4,120,256]{2,1,0:T(8,128)(2,1)S(1)}, u32[]{:S(2)}, u32[]{:S(2)}) collective-permute-start(bf16[4,120,256]{2,1,0:T(8,128)(2,1)S(1)} %get-tuple-element.65), channel_id=1, source_target_pairs={{0,16},{1,17},{2,18},{3,19},{4,20},{5,21},{6,22},{7,23},{8,24},{9,... | collective-permute-start | bytes 737288 | tf_op jit(solution)/shard_map/ppermute | solution.py:312
  57.0 7.6 %collective-permute-start.23 = (bf16[8,120,256]{2,1,0:T(8,128)(2,1)S(1)}, bf16[8,120,256]{2,1,0:T(8,128)(2,1)S(1)}, u32[]{:S(2)}, u32[]{:S(2)}) collective-permute-start(bf16[8,120,256]{2,1,0:T(8,128)(2,1)S(1)} %get-tuple-element.83), channel_id=1, source_target_pairs={{0,16},{1,17},{2,18},{3,19},{4,20},{5,21},{6,22},{7,23},{8,24},{9,... | collective-permute-start | bytes 1474568 | tf_op jit(solution)/shard_map/ppermute | solution.py:312
  57.1 7.5 %collective-permute-start.18 = (bf16[4,120,256]{2,1,0:T(8,128)(2,1)S(1)}, bf16[4,120,256]{2,1,0:T(8,128)(2,1)S(1)}, u32[]{:S(2)}, u32[]{:S(2)}) collective-permute-start(bf16[4,120,256]{2,1,0:T(8,128)(2,1)S(1)} %get-tuple-element.68), channel_id=1, source_target_pairs={{0,4},{1,5},{2,6},{3,7},{4,8},{5,9},{6,10},{7,11},{8,12},{9,13},{1... | collective-permute-start | bytes 737288 | tf_op jit(solution)/shard_map/ppermute | solution.py:312
  57.6 12.2 %collective-permute-start.15 = (bf16[8,120,256]{2,1,0:T(8,128)(2,1)S(1)}, bf16[8,120,256]{2,1,0:T(8,128)(2,1)S(1)}, u32[]{:S(2)}, u32[]{:S(2)}) collective-permute-start(bf16[8,120,256]{2,1,0:T(8,128)(2,1)S(1)} %pad_maximum_fusion), channel_id=1, source_target_pairs={{0,4},{1,5},{2,6},{3,7},{4,8},{5,9},{6,10},{7,11},{8,12},{9,13},{1... | collective-permute-start | bytes 1474568 | tf_op jit(solution)/shard_map/ppermute | solution.py:312
  64.6 7.9 %collective-permute-start.19 = (bf16[4,120,256]{2,1,0:T(8,128)(2,1)S(1)}, bf16[4,120,256]{2,1,0:T(8,128)(2,1)S(1)}, u32[]{:S(2)}, u32[]{:S(2)}) collective-permute-start(bf16[4,120,256]{2,1,0:T(8,128)(2,1)S(1)} %collective-permute-done.18), channel_id=1, source_target_pairs={{0,4},{1,5},{2,6},{3,7},{4,8},{5,9},{6,10},{7,11},{8,12},{9,13},{1... | collective-permute-start | bytes 737288 | tf_op jit(solution)/shard_map/ppermute | solution.py:312
  69.9 2.6 %collective-permute-start.16 = (bf16[4,120,256]{2,1,0:T(8,128)(2,1)S(1)}, bf16[4,120,256]{2,1,0:T(8,128)(2,1)S(1)}, u32[]{:S(2)}, u32[]{:S(2)}) collective-permute-start(bf16[4,120,256]{2,1,0:T(8,128)(2,1)S(1)} %slice.66), channel_id=1, source_target_pairs={{0,16},{1,17},{2,18},{3,19},{4,20},{5,21},{6,22},{7,23},{8,24},{9,... | collective-permute-start | bytes 737288 | tf_op jit(solution)/shard_map/ppermute | solution.py:312
  70.0 18.3 %copy-start = (f32[96,300]{1,0:T(8,128)S(1)}, f32[96,300]{1,0:T(8,128)}, u32[]{:S(2)}) copy-start(f32[96,300]{1,0:T(8,128)} %refs_5_.1) | copy-start | bytes 345604
  70.0 18.3 %copy-start.1 = (f32[96,300]{1,0:T(8,128)S(1)}, f32[96,300]{1,0:T(8,128)}, u32[]{:S(2)}) copy-start(f32[96,300]{1,0:T(8,128)} %refs_9_.1) | copy-start | bytes 345604
  70.0 18.3 %copy-start.2 = (f32[96,300]{1,0:T(8,128)S(1)}, f32[96,300]{1,0:T(8,128)}, u32[]{:S(2)}) copy-start(f32[96,300]{1,0:T(8,128)} %refs_7_.1) | copy-start | bytes 345604
  70.0 18.3 %copy-start.3 = (f32[96,300]{1,0:T(8,128)S(1)}, f32[96,300]{1,0:T(8,128)}, u32[]{:S(2)}) copy-start(f32[96,300]{1,0:T(8,128)} %refs_11_.1) | copy-start | bytes 345604
  70.0 18.3 %copy-start.4 = (f32[96]{0:T(128)S(1)}, f32[96]{0:T(128)}, u32[]{:S(2)}) copy-start(f32[96]{0:T(128)} %param.11) | copy-start | bytes 1156
  70.0 18.3 %copy-start.5 = (f32[96]{0:T(128)S(1)}, f32[96]{0:T(128)}, u32[]{:S(2)}) copy-start(f32[96]{0:T(128)} %param.15) | copy-start | bytes 1156
  70.1 18.3 %copy-start.6 = (f32[96]{0:T(128)S(1)}, f32[96]{0:T(128)}, u32[]{:S(2)}) copy-start(f32[96]{0:T(128)} %param.13) | copy-start | bytes 1156
  70.1 18.3 %copy-start.7 = (f32[96]{0:T(128)S(1)}, f32[96]{0:T(128)}, u32[]{:S(2)}) copy-start(f32[96]{0:T(128)} %param.17) | copy-start | bytes 1156
  70.1 7.7 %collective-permute-start.24 = (bf16[2,120,256]{2,1,0:T(8,128)(2,1)S(1)}, bf16[2,120,256]{2,1,0:T(8,128)(2,1)S(1)}, u32[]{:S(2)}, u32[]{:S(2)}) collective-permute-start(bf16[2,120,256]{2,1,0:T(8,128)(2,1)S(1)} %get-tuple-element.97), channel_id=1, source_target_pairs={{0,32},{1,33},{2,34},{3,35},{4,36},{5,37},{6,38},{7,39},{8,40},{9,... | collective-permute-start | bytes 368648 | tf_op jit(solution)/shard_map/ppermute | solution.py:312
  72.6 7.2 %collective-permute-start.20 = (bf16[120,256]{1,0:T(8,128)(2,1)S(1)}, bf16[120,256]{1,0:T(8,128)(2,1)S(1)}, u32[]{:S(2)}, u32[]{:S(2)}) collective-permute-start(bf16[120,256]{1,0:T(8,128)(2,1)S(1)} %get-tuple-element.71), channel_id=1, source_target_pairs={{0,1},{1,2},{2,3},{3,0},{4,5},{5,6},{6,7},{7,4},{8,9},{9,10},{10,1... | collective-permute-start | bytes 184328 | tf_op jit(solution)/shard_map/ppermute | solution.py:312
  73.0 7.0 %collective-permute-start.26 = (bf16[2,120,256]{2,1,0:T(8,128)(2,1)S(1)}, bf16[2,120,256]{2,1,0:T(8,128)(2,1)S(1)}, u32[]{:S(2)}, u32[]{:S(2)}) collective-permute-start(bf16[2,120,256]{2,1,0:T(8,128)(2,1)S(1)} %get-tuple-element.96), channel_id=1, source_target_pairs={{0,96},{1,97},{2,98},{3,99},{4,100},{5,101},{6,102},{7,103},{8,104... | collective-permute-start | bytes 368648 | tf_op jit(solution)/shard_map/ppermute | solution.py:312
  73.9 10.6 %collective-permute-start.22 = (bf16[120,256]{1,0:T(8,128)(2,1)S(1)}, bf16[120,256]{1,0:T(8,128)(2,1)S(1)}, u32[]{:S(2)}, u32[]{:S(2)}) collective-permute-start(bf16[120,256]{1,0:T(8,128)(2,1)S(1)} %get-tuple-element.72._), channel_id=1, source_target_pairs={{0,3},{1,0},{2,1},{3,2},{4,7},{5,4},{6,5},{7,6},{8,11},{9,8},{10,9... | collective-permute-start | bytes 184328 | tf_op jit(solution)/shard_map/ppermute | solution.py:312
  77.8 6.2 %collective-permute-start.25 = (bf16[2,120,256]{2,1,0:T(8,128)(2,1)S(1)}, bf16[2,120,256]{2,1,0:T(8,128)(2,1)S(1)}, u32[]{:S(2)}, u32[]{:S(2)}) collective-permute-start(bf16[2,120,256]{2,1,0:T(8,128)(2,1)S(1)} %shard_map.161), channel_id=1, source_target_pairs={{0,32},{1,33},{2,34},{3,35},{4,36},{5,37},{6,38},{7,39},{8,40},{9,... | collective-permute-start | bytes 368648 | tf_op jit(solution)/shard_map/ppermute | solution.py:312
  79.9 6.5 %collective-permute-start.21 = (bf16[120,256]{1,0:T(8,128)(2,1)S(1)}, bf16[120,256]{1,0:T(8,128)(2,1)S(1)}, u32[]{:S(2)}, u32[]{:S(2)}) collective-permute-start(bf16[120,256]{1,0:T(8,128)(2,1)S(1)} %add_convert_fusion), channel_id=1, source_target_pairs={{0,1},{1,2},{2,3},{3,0},{4,5},{5,6},{6,7},{7,4},{8,9},{9,10},{10,1... | collective-permute-start | bytes 184328 | tf_op jit(solution)/shard_map/ppermute | solution.py:312
  84.0 4.3 %collective-permute-start.27 = (bf16[120,256]{1,0:T(8,128)(2,1)S(1)}, bf16[120,256]{1,0:T(8,128)(2,1)S(1)}, u32[]{:S(2)}, u32[]{:S(2)}) collective-permute-start(bf16[120,256]{1,0:T(8,128)(2,1)S(1)} %get-tuple-element.85), channel_id=1, source_target_pairs={{0,128},{1,129},{2,130},{3,131},{4,132},{5,133},{6,134},{7,135},{8... | collective-permute-start | bytes 184328 | tf_op jit(solution)/shard_map/ppermute | solution.py:312
